TPU v7x, 32 devices: a whole 2x2x4 slice. The times are simulated.
32 devices in a mesh: tier: 4 (over z), aux: 8 (over y, x, core).
Axes of the slice: x: 2, y: 2, z: 4, core: 2. Of those that a mesh axis runs over, the one named last changes fastest.
Arguments:
- section_state: float32 [256, 18432], P(('tier', 'aux')), may hold values from -6 to 6
- coupling: float32 [96, 96], replicated, may hold values from -0.625 to 0.625
- site_energy: float32 [96], replicated, may hold values from -1 to 1
- bath_rate: float32 [96], replicated, may hold values from 0.3 to 3
- bath_strength: float32 [96], replicated, may hold values from 0.1 to 1
- bath_of_site: int32 [96], replicated, may hold values from 0 to 95, each once
- quanta: int32 [256, 4], P(('tier', 'aux')), may hold values from -1 to 95, as said below
- send_list: int32 [32, 48], P(('tier', 'aux')), may hold values from -1 to 31, as said below
- dest_slot: int32 [32, 48], P(('tier', 'aux')), may hold values from 0 to 7
Outputs:
- derivative: float32 [256, 18432], P(('tier', 'aux'))
Inputs may be any that keep to these rules, and one draw needn't show every extreme that they name: Row a lists the sites of auxiliary a's quanta, 1 to 4 of them with repeats allowed, in ascending order, then -1 in the empty places. `send_list`: entry [d, l] is slot * 4 + place for an auxiliary slot of device d, or -1. The first place of every distinct site of every auxiliary stands in exactly one lane of its device, and no other place stands anywhere. On every device the 3 lanes of group 0 towards one aux index are all used.
All inputs are finite; a program needn't handle non-finite values.
Results may differ from a plain program's by a relative error of at most 0.00005.
Values sent between devices are 32-bit elements; how exact they have to be, the bound alone decides.
No kernel may reach another device: no remote copies, remote signals or barrier semaphores. Data moves between devices by JAX's collectives and lax.ppermute only.
A program may use at most 64 MiB of HBM per device.

v0:
```python
import jax
import jax.numpy as jnp
from jax import lax
from jax.sharding import PartitionSpec as P

thermal = 0.5
highest = lax.Precision.HIGHEST


def passed_along(value, axis, steps):
    count = lax.axis_size(axis)
    first, last = (max(0, -steps), min(count, count - steps))
    return lax.ppermute(value, axis, [(source, source + steps) for source in range(first, last)])


def take_slices(states, holders, columns):
    site_count = states.shape[1]
    flat_holders = holders.reshape(-1)
    flat_columns = columns.reshape(-1)
    positions = jnp.arange(site_count, dtype=jnp.int32)
    row_part = states[flat_holders, flat_columns, :]
    column_real = states[flat_holders[:, None], positions[None, :], flat_columns[:, None]]
    column_imag = states[
        flat_holders[:, None], positions[None, :], flat_columns[:, None] + site_count
    ]
    joined = jnp.concatenate([row_part, column_real, column_imag], axis=-1)
    return joined.reshape(holders.shape + (4 * site_count,))


def descend(payload_pair):
    return passed_along(payload_pair, "tier", -1)


def ascend(reply_block):
    return passed_along(reply_block, "tier", 1)


def answer(states, labels):
    slot_ids = labels[..., 0]
    wanted = labels[..., 1]
    picked = take_slices(states, slot_ids, jnp.maximum(wanted, 0))
    return jnp.where((wanted >= 0)[..., None], picked, 0.0)


def trade_edges(states, payload, labels):
    inbound = lax.all_to_all(payload, "aux", split_axis=1, concat_axis=1, tiled=True)
    inbound_tags = lax.all_to_all(labels, "aux", split_axis=1, concat_axis=1, tiled=True)
    lower_in, lower_tags = descend((inbound[1], inbound_tags[1]))
    lower_reply = ascend(answer(states, lower_tags))
    replies = jnp.stack([answer(states, inbound_tags[0]), lower_reply])
    arrived = jnp.stack([inbound[0], lower_in])
    arrived_tags = jnp.stack([inbound_tags[0], lower_tags])
    returned = lax.all_to_all(replies, "aux", split_axis=1, concat_axis=1, tiled=True)
    return (returned, arrived, arrived_tags)


def on_device(
    section_state,
    coupling,
    site_energy,
    bath_rate,
    bath_strength,
    bath_of_site,
    quanta,
    send_list,
    dest_slot,
):
    site_count = coupling.shape[0]
    doubled_width = 2 * site_count
    aux_count = section_state.shape[0]
    flat_shape = section_state.shape
    section_state = section_state.reshape(aux_count, site_count, doubled_width)
    depth_count = quanta.shape[1]
    lane_count = send_list.shape[1]
    peer_count = lax.axis_size("aux")
    capacity = lane_count // (2 * peer_count)
    band_index = lax.axis_index("tier")
    positions = jnp.arange(site_count, dtype=jnp.int32)
    hamilton = (coupling + coupling.T) * 0.5 + jnp.diag(site_energy)
    zero_block = jnp.zeros_like(hamilton)
    paired = jnp.concatenate(
        [jnp.concatenate([hamilton, zero_block], 1), jnp.concatenate([zero_block, hamilton], 1)], 0
    )
    chooser = (bath_of_site[:, None] == positions[None, :]).astype(jnp.float32)
    site_params = jnp.dot(chooser, jnp.stack([bath_rate, bath_strength], axis=1), precision=highest)
    site_rate = site_params[:, 0]
    site_strength = site_params[:, 1]
    real_coef = 2.0 * thermal * site_strength
    imag_coef = site_strength * site_rate
    matches = (quanta[:, :, None] == positions[None, None, :]).astype(jnp.float32)
    multiple = jnp.sum(matches, axis=1)
    damping = jnp.dot(multiple, site_rate, precision=highest)
    entries = send_list[0]
    clipped = jnp.maximum(entries, 0)
    sources = clipped // depth_count
    lane_sites = quanta[sources, clipped % depth_count]
    lane_ids = jnp.arange(lane_count, dtype=jnp.int32)
    lane_group = lane_ids // (peer_count * capacity)
    usable = (entries >= 0) & (lane_sites >= 0) & (band_index - lane_group >= 0)
    lane_columns = jnp.maximum(lane_sites, 0)
    outgoing = jnp.where(usable[:, None], take_slices(section_state, sources, lane_columns), 0.0)
    labels = jnp.stack([dest_slot[0], jnp.where(usable, lane_sites, -1)], axis=-1)
    outgoing = outgoing.reshape(2, peer_count, capacity, 4 * site_count)
    labels = labels.reshape(2, peer_count, capacity, 2)
    returned, arrived, arrived_tags = trade_edges(section_state, outgoing, labels)
    left_product = jnp.einsum("ij,ajc->aic", hamilton, section_state, precision=highest)
    right_product = jnp.dot(
        section_state.reshape(-1, doubled_width), paired, precision=highest
    ).reshape(section_state.shape)
    commutator = left_product - right_product
    coherent = jnp.concatenate(
        [commutator[..., site_count:], -commutator[..., :site_count]], axis=-1
    )
    local_part = coherent - damping[:, None, None] * section_state
    arrived = arrived.reshape(-1, 4 * site_count)
    arrived_tags = arrived_tags.reshape(-1, 2)
    up_sites = arrived_tags[:, 1]
    up_usable = up_sites >= 0
    up_slot = jnp.where(up_usable, arrived_tags[:, 0], 0)
    up_site = jnp.maximum(up_sites, 0)
    up_data = jnp.concatenate(
        [
            arrived[:, site_count : 2 * site_count],
            -arrived[:, :site_count],
            -arrived[:, 3 * site_count :],
            arrived[:, 2 * site_count : 3 * site_count],
        ],
        axis=-1,
    )
    up_data = jnp.where(up_usable[:, None], up_data, 0.0)
    returned = returned.reshape(lane_count, 4 * site_count)
    lane_onehot = (lane_columns[:, None] == positions[None, :]).astype(jnp.float32)
    weights = jnp.sum(lane_onehot * multiple[sources], axis=1)
    lane_coefs = jnp.dot(lane_onehot, jnp.stack([real_coef, imag_coef], axis=1), precision=highest)
    shared = (-weights * lane_coefs[:, 1])[:, None]
    row_turn = (-weights * lane_coefs[:, 0])[:, None]
    column_turn = (weights * lane_coefs[:, 0])[:, None]
    row_real = returned[:, :site_count]
    row_imag = returned[:, site_count : 2 * site_count]
    column_real = returned[:, 2 * site_count : 3 * site_count]
    column_imag = returned[:, 3 * site_count :]
    down_data = jnp.concatenate(
        [
            shared * row_real - row_turn * row_imag,
            shared * row_imag + row_turn * row_real,
            shared * column_real - column_turn * column_imag,
            shared * column_imag + column_turn * column_real,
        ],
        axis=-1,
    )
    down_data = jnp.where(usable[:, None], down_data, 0.0)
    all_data = jnp.concatenate([up_data, down_data], axis=0)
    all_slot = jnp.concatenate([up_slot, sources], axis=0).astype(jnp.int32)
    all_site = jnp.concatenate([up_site, lane_columns], axis=0).astype(jnp.int32)
    result = local_part.at[all_slot, all_site, :].add(all_data[:, :doubled_width])
    result = result.at[all_slot[:, None], positions[None, :], all_site[:, None]].add(
        all_data[:, doubled_width : doubled_width + site_count]
    )
    result = result.at[all_slot[:, None], positions[None, :], all_site[:, None] + site_count].add(
        all_data[:, doubled_width + site_count :]
    )
    return result.reshape(flat_shape)


def solution(mesh):
    return jax.shard_map(
        on_device,
        mesh=mesh,
        in_specs=(
            P(("tier", "aux"), None),
            P(),
            P(),
            P(),
            P(),
            P(),
            P(("tier", "aux"), None),
            P(("tier", "aux"), None),
            P(("tier", "aux"), None),
        ),
        out_specs=P(("tier", "aux"), None),
        check_vma=False,
    )
```

profile of v0, /device:TPU:0, one launch (start us, length us, event | category | flops | bytes accessed | tf_op | source)
XLA Modules:
  0.0 348.1 jit_solution(16747967051430989833)
XLA Ops:
  0.0 0.7 fusion.78
  0.7 0.7 compare_bitcast_fusion.1
  1.4 1.7 gather_fusion
  3.4 0.5 broadcast.1225
  3.9 1.3 reduce.17
  5.3 0.6 copy.110
  5.9 5.2 %all-to-all-start = ((s32[2,8,3,2]{2,0,3,1:T(2,128)}), s32[2,8,3,2]{2,0,3,1:T(2,128)S(1)}, u32[]{:S(2)}, u32[]{:S(2)}) async-start(s32[2,8,3,2]{2,0,3,1:T(2,128)} %copy.110), calls=%async_computation | async-start | bytes 32768 | tf_op jit(solution)/shard_map/all_to_all | solution.py:47
  11.1 0.3 reshape_reshape.3
  11.5 0.3 reshape.714
  11.9 0.3 copy-done
  12.5 1.3 convolution_bitcast_fusion.1
  13.8 0.3 copy.109
  14.1 0.8 fusion
  14.9 0.2 fusion.88
  15.1 0.5 copy-done.7
  15.6 0.2 fusion.24
  15.8 0.2 convolution_bitcast_fusion.2
  16.1 43.9 %gather_fusion.3 = f32[4608]{0:T(1024)S(1)} fusion(f32[8,96,192]{2,1,0:T(8,128)S(1)} %reshape.714, s32[4608]{0:T(1024)S(1)} %reshape.750), kind=kCustom, calls=%fused_computation.3 | custom fusion | bytes 92160 | tf_op jit(solution)/shard_map/gather | solution.py:23
  60.2 43.9 %gather_fusion.2 = f32[4608]{0:T(1024)S(1)} fusion(f32[8,96,192]{2,1,0:T(8,128)S(1)} %reshape.714, s32[4608]{0:T(1024)S(1)} %reshape.744), kind=kCustom, calls=%fused_computation.2 | custom fusion | bytes 92160 | tf_op jit(solution)/shard_map/gather | solution.py:22
  104.2 1.0 gather_fusion.1
  105.4 0.6 gather_fusion.4
  106.0 0.2 select_reduce_fusion
  106.2 0.2 fusion.25
  106.4 0.4 maximum_subtract_fusion
  106.7 0.1 maximum_select_fusion
  106.9 0.7 copy.114
  107.6 4.2 %all-to-all-start.1 = ((f32[2,8,3,384]{3,0,2,1:T(2,128)}), f32[2,8,3,384]{3,0,2,1:T(2,128)S(1)}, u32[]{:S(2)}, u32[]{:S(2)}) async-start(f32[2,8,3,384]{3,0,2,1:T(2,128)} %copy.114), calls=%async_computation.1 | async-start | bytes 147456 | tf_op jit(solution)/shard_map/all_to_all | solution.py:46
  112.3 1.3 collective-permute-start
  114.2 22.2 %gather_fusion.7 = f32[2304]{0:T(1024)S(1)} fusion(f32[8,96,192]{2,1,0:T(8,128)S(1)} %reshape.714, s32[2304]{0:T(1024)S(1)} %reshape.776), kind=kCustom, calls=%fused_computation.7 | custom fusion | bytes 46080 | tf_op jit(solution)/shard_map/gather | solution.py:23
  136.6 22.2 %gather_fusion.6 = f32[2304]{0:T(1024)S(1)} fusion(f32[8,96,192]{2,1,0:T(8,128)S(1)} %reshape.714, s32[2304]{0:T(1024)S(1)} %reshape.770), kind=kCustom, calls=%fused_computation.6 | custom fusion | bytes 46080 | tf_op jit(solution)/shard_map/gather | solution.py:22
  159.0 0.8 gather_fusion.5
  161.2 22.2 %gather_fusion.10 = f32[2304]{0:T(1024)S(1)} fusion(f32[8,96,192]{2,1,0:T(8,128)S(1)} %reshape.714, s32[2304]{0:T(1024)S(1)} %reshape.794), kind=kCustom, calls=%fused_computation.10 | custom fusion | bytes 46080 | tf_op jit(solution)/shard_map/gather | solution.py:23
  183.6 22.2 %gather_fusion.9 = f32[2304]{0:T(1024)S(1)} fusion(f32[8,96,192]{2,1,0:T(8,128)S(1)} %reshape.714, s32[2304]{0:T(1024)S(1)} %reshape.788), kind=kCustom, calls=%fused_computation.9 | custom fusion | bytes 46080 | tf_op jit(solution)/shard_map/gather | solution.py:22
  206.1 0.8 gather_fusion.8
  207.1 4.5 %collective-permute-start.2 = (f32[8,3,384]{2,1,0:T(4,128)S(1)}, f32[8,3,384]{2,1,0:T(4,128)S(1)}, u32[]{:S(2)}, u32[]{:S(2)}) collective-permute-start(f32[8,3,384]{2,1,0:T(4,128)S(1)} %broadcast_select_fusion.2), channel_id=1, source_target_pairs={{0,8},{8,16},{16,24},{1,9},{9,17},{17,25},{2,10},{10,18},{18,26},{... | collective-permute-start | bytes 110600 | tf_op jit(solution)/shard_map/ppermute | solution.py:13
  212.1 0.1 fusion.16
  212.7 1.3 collective-permute-start.1
  214.1 0.7 copy.132
  214.7 4.2 %all-to-all-start.2 = ((f32[2,8,3,384]{3,0,2,1:T(2,128)}), f32[2,8,3,384]{3,0,2,1:T(2,128)S(1)}, u32[]{:S(2)}, u32[]{:S(2)}) async-start(f32[2,8,3,384]{3,0,2,1:T(2,128)} %copy.132), calls=%async_computation.2 | async-start | bytes 147456 | tf_op jit(solution)/shard_map/all_to_all | solution.py:53
  219.1 0.1 maximum_select_fusion.1
  219.3 4.7 %all-to-all-done.2 = f32[2,8,3,384]{3,0,2,1:T(2,128)S(1)} async-done(((f32[2,8,3,384]{3,0,2,1:T(2,128)}), f32[2,8,3,384]{3,0,2,1:T(2,128)S(1)}, u32[]{:S(2)}, u32[]{:S(2)}) %all-to-all-start.2) | async-done | bytes 73760 | tf_op jit(solution)/shard_map/all_to_all | solution.py:53
  224.1 0.1 multiply_subtract_fusion.1
  224.2 0.1 maximum_select_fusion.2
  224.4 5.6 %scatter_fusion = f32[8,96,192]{2,1,0:T(8,128)S(1)} fusion(f32[8,96,192]{2,1,0:T(8,128)S(1)} %maximum_subtract_fusion, s32[96]{0:T(128)S(1)} %fusion.79, f32[96,192]{1,0:T(8,128)S(1)} %fusion.17), kind=kCustom, calls=%fused_computation.11 | custom fusion | flops 18432 | bytes 221952 | tf_op jit(solution)/shard_map/scatter-add | solution.py:155
  230.0 0.4 reshape.723
  230.6 58.3 %scatter_fusion.1 = f32[147456]{0:T(1024)S(1)} fusion(f32[147456]{0:T(1024)S(1)} %reshape.723, s32[9216]{0:T(1024)S(1)} %reshape.806, f32[9216]{0:T(1024)S(1)} %reshape.808), kind=kCustom, calls=%fused_computation.12 | custom fusion | flops 9216 | bytes 147456
  289.0 58.2 %scatter_fusion.2 = f32[147456]{0:T(1024)S(1)} fusion(f32[147456]{0:T(1024)S(1)} %scatter_fusion.1, s32[9216]{0:T(1024)S(1)} %reshape.812, f32[9216]{0:T(1024)S(1)} %reshape.814), kind=kCustom, calls=%fused_computation.13 | custom fusion | flops 9216 | bytes 147456
  347.1 0.9 reshape.721
  (128 shorter events, 6.3 us)
Async XLA Ops:
  0.0 11.1 %copy-start.1 = (f32[8,18432]{1,0:T(8,128)S(1)}, f32[8,18432]{1,0:T(8,128)}, u32[]{:S(2)}) copy-start(f32[8,18432]{1,0:T(8,128)} %param.9) | copy-start | bytes 1769476
  5.9 101.7 %all-to-all-start = ((s32[2,8,3,2]{2,0,3,1:T(2,128)}), s32[2,8,3,2]{2,0,3,1:T(2,128)S(1)}, u32[]{:S(2)}, u32[]{:S(2)}) async-start(s32[2,8,3,2]{2,0,3,1:T(2,128)} %copy.110), calls=%async_computation | async-start | bytes 32768 | tf_op jit(solution)/shard_map/all_to_all | solution.py:47
  11.5 0.7 copy-start
  11.5 0.8 copy-start.3
  11.5 0.8 copy-start.2
  11.5 0.9 copy-start.4
  14.9 0.7 copy-start.7
  14.9 0.7 copy-start.8
  14.9 0.7 copy-start.9
  107.6 105.1 %all-to-all-start.1 = ((f32[2,8,3,384]{3,0,2,1:T(2,128)}), f32[2,8,3,384]{3,0,2,1:T(2,128)S(1)}, u32[]{:S(2)}, u32[]{:S(2)}) async-start(f32[2,8,3,384]{3,0,2,1:T(2,128)} %copy.114), calls=%async_computation.1 | async-start | bytes 147456 | tf_op jit(solution)/shard_map/all_to_all | solution.py:46
  112.3 47.8 %collective-permute-start = (s32[8,3,2]{0,2,1:T(2,128)S(1)}, s32[8,3,2]{0,2,1:T(2,128)S(1)}, u32[]{:S(2)}, u32[]{:S(2)}) collective-permute-start(s32[8,3,2]{0,2,1:T(2,128)S(1)} %bitcast.149), channel_id=1, source_target_pairs={{8,0},{16,8},{24,16},{9,1},{17,9},{25,17},{10,2},{18,10},{26,18},{... | collective-permute-start | bytes 584 | tf_op jit(solution)/shard_map/ppermute | solution.py:13
  183.6 28.5 %copy-start.6 = (s32[3]{0:T(128)S(1)}, s32[3]{0:T(128)}, u32[]{:S(2)}) copy-start(s32[3]{0:T(128)} %constant.115) | copy-start | bytes 40
  205.8 6.4 %copy-start.5 = (s32[3]{0:T(128)S(1)}, s32[3]{0:T(128)}, u32[]{:S(2)}) copy-start(s32[3]{0:T(128)} %constant.112) | copy-start | bytes 40
  207.1 6.9 %collective-permute-start.2 = (f32[8,3,384]{2,1,0:T(4,128)S(1)}, f32[8,3,384]{2,1,0:T(4,128)S(1)}, u32[]{:S(2)}, u32[]{:S(2)}) collective-permute-start(f32[8,3,384]{2,1,0:T(4,128)S(1)} %broadcast_select_fusion.2), channel_id=1, source_target_pairs={{0,8},{8,16},{16,24},{1,9},{9,17},{17,25},{2,10},{10,18},{18,26},{... | collective-permute-start | bytes 110600 | tf_op jit(solution)/shard_map/ppermute | solution.py:13
  212.7 6.2 %collective-permute-start.1 = (f32[8,3,384]{2,0,1:T(8,128)S(1)}, f32[8,3,384]{2,0,1:T(8,128)S(1)}, u32[]{:S(2)}, u32[]{:S(2)}) collective-permute-start(f32[8,3,384]{2,0,1:T(8,128)S(1)} %bitcast.144), channel_id=1, source_target_pairs={{8,0},{16,8},{24,16},{9,1},{17,9},{25,17},{10,2},{18,10},{26,18},{... | collective-permute-start | bytes 110600 | tf_op jit(solution)/shard_map/ppermute | solution.py:13
  214.7 9.3 %all-to-all-start.2 = ((f32[2,8,3,384]{3,0,2,1:T(2,128)}), f32[2,8,3,384]{3,0,2,1:T(2,128)S(1)}, u32[]{:S(2)}, u32[]{:S(2)}) async-start(f32[2,8,3,384]{3,0,2,1:T(2,128)} %copy.132), calls=%async_computation.2 | async-start | bytes 147456 | tf_op jit(solution)/shard_map/all_to_all | solution.py:53
where the time goes:
time: 349 us; the launch traced here: 348 us
  local copies, waits for them, and re-layouts  192 us (55%)
  other arithmetic  128 us (37%)
  starting transfers between devices  20.7 us (6%)
  waiting for transfers between devices  4.76 us (1%)
    unnamed x7, other arithmetic  118 us
    gather x5, local copies, waits for them, and re-layouts, take_slices(): states[flat_holders[:, None], positions[None, :], flat_columns[:, None] +...  88.4 us
    gather x5, local copies, waits for them, and re-layouts, take_slices(): states[flat_holders[:, None], positions[None, :], flat_columns[:, None]]  88.4 us
    ppermute x3, starting transfers between devices, passed_along(): lax.ppermute(value, axis, [(source, source + steps) for source in range(f...  7.12 us
  transfers between devices with their start and end apart: 6, of which 1 were waited for; matrix products, arithmetic and copies ran while one was open for 55% of the time, Pallas kernels for 0%

commit v1 on v0

v1 whole, which is shorter than its diff:
```python
import functools

import jax
import jax.numpy as jnp
from jax import lax
from jax.experimental import pallas as pl
from jax.experimental.pallas import tpu as pltpu
from jax.sharding import PartitionSpec as P

thermal = 0.5
LANES = 128
SUB = 8
FIELDS = 4
VMEM = pltpu.VMEM
SMEM = pltpu.SMEM


def spec(space):
    return pl.BlockSpec(memory_space=space)


def lane_index(shape):
    return lax.broadcasted_iota(jnp.int32, shape, 1)


def pack_kernel(
    sizes, band_ref, send_ref, quanta_ref, slot_ref, state_ref, store_ref, payload_ref
):
    sites, aux, depth, peers, capacity, tiers = sizes
    tiles = 4 * sites // LANES
    pair_blocks = sites // (2 * SUB)
    rows = aux * sites
    lane = lane_index((SUB, LANES))
    store_ref[:, pl.ds(rows, LANES - sites), :] = jnp.zeros((4, LANES - sites, LANES), jnp.float32)
    for a in range(aux):
        for block in range(pair_blocks):
            parts = [
                state_ref[pl.ds(a + aux * (tiles * SUB * block + u), SUB, stride=aux * tiles), :]
                for u in range(tiles)
            ]
            first, middle, last = parts
            even_imag = jnp.where(lane < 32, pltpu.roll(first, 32, 1), pltpu.roll(middle, 32, 1))
            odd_real = jnp.where(lane < 64, pltpu.roll(middle, 64, 1), pltpu.roll(last, 64, 1))
            odd_imag = pltpu.roll(last, 96, 1)
            base = a * sites + 2 * SUB * block
            store_ref[0, pl.ds(base, SUB, stride=2), :] = first
            store_ref[1, pl.ds(base, SUB, stride=2), :] = even_imag
            store_ref[0, pl.ds(base + 1, SUB, stride=2), :] = odd_real
            store_ref[1, pl.ds(base + 1, SUB, stride=2), :] = odd_imag
    for a in range(aux):
        for c in range(2):
            block = store_ref[c, pl.ds(a * sites, LANES), :]
            store_ref[2 + c, pl.ds(a * sites, sites), :] = block.T[:sites, :]
    band = band_ref[0]
    row_lane = lane_index((1, LANES))
    for g in (1, 0):
        target = jnp.maximum(band - g, 0)
        for q in range(peers):
            at_row = target * peers + q
            tags = []
            for j in range(capacity):
                l = (g * peers + q) * capacity + j
                entry = send_ref[0, l]
                clipped = jnp.maximum(entry, 0)
                source = clipped // depth
                site = quanta_ref[source, clipped % depth]
                usable = (entry >= 0) & (site >= 0) & (band - g >= 0)
                row = source * sites + jnp.maximum(site, 0)
                tags.append(slot_ref[0, l].astype(jnp.float32))
                tags.append(jnp.where(usable, site, -1).astype(jnp.float32))
                for f in range(FIELDS):
                    if f == 0 and j == 0:
                        head = store_ref[0, pl.ds(row, 1), :]
                        continue
                    at = (j * FIELDS + f) * LANES
                    payload_ref[at_row, :, pl.ds(at, LANES)] = store_ref[f, pl.ds(row, 1), :]
            for t, tag in enumerate(tags):
                head = jnp.where(row_lane == sites + t, tag, head)
            payload_ref[at_row, :, pl.ds(0, LANES)] = head


def read_tags(arrived_ref, tag_ref, sem):
    copy = pltpu.make_async_copy(arrived_ref.at[:, :, pl.ds(0, LANES)], tag_ref, sem)
    copy.start()
    copy.wait()


def answer_kernel(sizes, band_ref, arrived_ref, store_ref, reply_ref, tag_ref, sem):
    sites, aux, depth, peers, capacity, tiers = sizes
    band = band_ref[0]
    read_tags(arrived_ref, tag_ref, sem)
    for g in (1, 0):
        origin = jnp.minimum(band + g, tiers - 1)
        for p in range(peers):
            at_row = origin * peers + p
            for j in range(capacity):
                slot = tag_ref[at_row, 0, sites + 2 * j].astype(jnp.int32)
                site = tag_ref[at_row, 0, sites + 2 * j + 1].astype(jnp.int32)
                row = slot * sites + jnp.maximum(site, 0)
                for f in range(FIELDS):
                    at = (j * FIELDS + f) * LANES
                    reply_ref[at_row, :, pl.ds(at, LANES)] = store_ref[f, pl.ds(row, 1), :]


def split(value):
    high = value.astype(jnp.bfloat16)
    low = (value - high.astype(jnp.float32)).astype(jnp.bfloat16)
    return high, low


def local_kernel(
    sizes, quanta_ref, bath_ref, rate_ref, store_ref, coupling_ref, energy_ref, acc_ref, matrix_ref
):
    sites, aux, depth, peers, capacity, tiers = sizes
    row_ids = lax.broadcasted_iota(jnp.int32, (sites, sites), 0)
    col_ids = lax.broadcasted_iota(jnp.int32, (sites, sites), 1)
    coupling = coupling_ref[...]
    hamilton = (coupling + coupling.T) * 0.5 + jnp.where(row_ids == col_ids, energy_ref[...], 0.0)
    matrix_ref[...] = jnp.zeros_like(matrix_ref)
    matrix_ref[pl.ds(0, sites), pl.ds(LANES, sites)] = hamilton
    matrix_ref[pl.ds(LANES, sites), pl.ds(0, sites)] = -hamilton
    high, low = split(matrix_ref[...])
    dot = functools.partial(jnp.dot, preferred_element_type=jnp.float32)
    for a in range(aux):
        damp = jnp.float32(0.0)
        for place in range(depth):
            site = quanta_ref[a, place]
            rate = rate_ref[0, bath_ref[0, jnp.maximum(site, 0)]]
            damp = damp + jnp.where(site >= 0, rate, 0.0)
        here = pl.ds(a * sites, sites)
        for half in range(2):
            real, imag = store_ref[2 * half, here, :], store_ref[2 * half + 1, here, :]
            both = jnp.concatenate([real, imag], axis=1)
            both_high, both_low = split(both)
            product = dot(both_high, high) + (dot(both_low, high) + dot(both_high, low))
            if half == 0:
                product = product - damp * both
            else:
                product = -product
            acc_ref[2 * half, here, :] = product[:, :LANES]
            acc_ref[2 * half + 1, here, :] = product[:, LANES:]
    tail = pl.ds(aux * sites, LANES - sites)
    acc_ref[:, tail, :] = jnp.zeros((4, LANES - sites, LANES), jnp.float32)


def raise_kernel(sizes, band_ref, arrived_ref, acc_ref, sum_ref, work_ref, tag_ref, sem):
    sites, aux, depth, peers, capacity, tiers = sizes
    rows = aux * sites
    band = band_ref[0]
    read_tags(arrived_ref, tag_ref, sem)
    work_ref[...] = acc_ref[...]
    for g in range(2):
        origin = jnp.minimum(band + g, tiers - 1)
        inside = band + g < tiers
        for p in range(peers):
            at_row = origin * peers + p
            for j in range(capacity):
                slot = tag_ref[at_row, 0, sites + 2 * j].astype(jnp.int32)
                site = tag_ref[at_row, 0, sites + 2 * j + 1].astype(jnp.int32)
                usable = (site >= 0) & inside
                row = pl.ds(jnp.where(usable, slot * sites + jnp.maximum(site, 0), rows), 1)
                at = j * FIELDS * LANES
                parts = [
                    arrived_ref[at_row, :, pl.ds(at + f * LANES, LANES)]
                    for f in range(FIELDS)
                ]
                work_ref[0, row, :] = work_ref[0, row, :] + parts[1]
                work_ref[1, row, :] = work_ref[1, row, :] - parts[0]
                work_ref[2, row, :] = work_ref[2, row, :] - parts[3]
                work_ref[3, row, :] = work_ref[3, row, :] + parts[2]
    for a in range(aux):
        here = pl.ds(a * sites, sites)
        for c in range(2):
            turned = work_ref[2 + c, pl.ds(a * sites, LANES), :].T[:sites, :]
            sum_ref[c, here, :] = work_ref[c, here, :] + turned
    tail = pl.ds(rows, LANES - sites)
    sum_ref[:, tail, :] = jnp.zeros((2, LANES - sites, LANES), jnp.float32)


def lower_kernel(
    sizes,
    band_ref,
    send_ref,
    quanta_ref,
    bath_ref,
    rate_ref,
    strength_ref,
    returned_ref,
    sum_ref,
    out_ref,
    work_ref,
):
    sites, aux, depth, peers, capacity, tiers = sizes
    rows = aux * sites
    tiles = 4 * sites // LANES
    pair_blocks = sites // (2 * SUB)
    band = band_ref[0]
    work_ref[pl.ds(0, 2)] = sum_ref[...]
    work_ref[pl.ds(2, 2)] = jnp.zeros((2,) + work_ref.shape[1:], jnp.float32)
    for g in range(2):
        target = jnp.maximum(band - g, 0)
        for q in range(peers):
            at_row = target * peers + q
            for j in range(capacity):
                l = (g * peers + q) * capacity + j
                entry = send_ref[0, l]
                clipped = jnp.maximum(entry, 0)
                source = clipped // depth
                site = quanta_ref[source, clipped % depth]
                usable = (entry >= 0) & (site >= 0) & (band - g >= 0)
                safe = jnp.maximum(site, 0)
                weight = jnp.float32(0.0)
                for place in range(depth):
                    weight = weight + jnp.where(quanta_ref[source, place] == safe, 1.0, 0.0)
                bath = bath_ref[0, safe]
                strength = strength_ref[0, bath]
                turn = weight * (2.0 * thermal * strength)
                shared = -weight * (strength * rate_ref[0, bath])
                row = pl.ds(jnp.where(usable, source * sites + safe, rows), 1)
                at = j * FIELDS * LANES
                row_real, row_imag, col_real, col_imag = (
                    returned_ref[at_row, :, pl.ds(at + f * LANES, LANES)]
                    for f in range(FIELDS)
                )
                work_ref[0, row, :] = work_ref[0, row, :] + (shared * row_real + turn * row_imag)
                work_ref[1, row, :] = work_ref[1, row, :] + (shared * row_imag - turn * row_real)
                work_ref[2, row, :] = work_ref[2, row, :] + (shared * col_real - turn * col_imag)
                work_ref[3, row, :] = work_ref[3, row, :] + (shared * col_imag + turn * col_real)
    for a in range(aux):
        here = pl.ds(a * sites, sites)
        for c in range(2):
            turned = work_ref[2 + c, pl.ds(a * sites, LANES), :].T[:sites, :]
            work_ref[c, here, :] = work_ref[c, here, :] + turned
    lane = lane_index((SUB, LANES))
    for a in range(aux):
        for block in range(pair_blocks):
            base = a * sites + 2 * SUB * block
            even_real, even_imag, odd_real, odd_imag = (
                work_ref[c, pl.ds(base + o, SUB, stride=2), :] for o in (0, 1) for c in (0, 1)
            )
            turned_imag = pltpu.roll(even_imag, 96, 1)
            turned_real = pltpu.roll(odd_real, 64, 1)
            parts = (
                jnp.where(lane < 96, even_real, turned_imag),
                jnp.where(lane < 64, turned_imag, turned_real),
                jnp.where(lane < 32, turned_real, pltpu.roll(odd_imag, 32, 1)),
            )
            for u in range(tiles):
                start = a + aux * (tiles * SUB * block + u)
                out_ref[pl.ds(start, SUB, stride=aux * tiles), :] = parts[u]


def on_device(
    section_state,
    coupling,
    site_energy,
    bath_rate,
    bath_strength,
    bath_of_site,
    quanta,
    send_list,
    dest_slot,
):
    sites = coupling.shape[0]
    aux, flat = section_state.shape
    depth = quanta.shape[1]
    lane_count = send_list.shape[1]
    peers = lax.axis_size("aux")
    tiers = lax.axis_size("tier")
    capacity = lane_count // (2 * peers)
    sizes = (sites, aux, depth, peers, capacity, tiers)
    rows = aux * sites
    padded = rows + LANES - sites
    width = capacity * FIELDS * LANES
    chunks = flat // LANES
    f32 = jnp.float32
    band = lax.axis_index("tier").reshape(1)
    tiled = section_state.reshape(aux, chunks, LANES).transpose(1, 0, 2).reshape(-1, LANES)
    bath_row = bath_of_site.reshape(1, -1)
    rate_row = bath_rate.reshape(1, -1)
    strength_row = bath_strength.reshape(1, -1)

    def call(kernel, in_spaces, outs, scratch, name):
        many = isinstance(outs, list)
        return pl.pallas_call(
            functools.partial(kernel, sizes),
            out_shape=outs,
            in_specs=[spec(space) for space in in_spaces],
            out_specs=[spec(VMEM)] * len(outs) if many else spec(VMEM),
            scratch_shapes=scratch,
            name=name,
            compiler_params=pltpu.CompilerParams(vmem_limit_bytes=24 * 1024 * 1024),
        )

    store_shape = jax.ShapeDtypeStruct((4, padded, LANES), f32)
    wire_shape = jax.ShapeDtypeStruct((tiers * peers, 1, width), f32)
    tag_scratch = [SMEM((tiers * peers, 1, LANES), f32), pltpu.SemaphoreType.DMA(())]
    trade = functools.partial(
        lax.all_to_all, axis_name=("tier", "aux"), split_axis=0, concat_axis=0, tiled=True
    )
    store, payload = call(
        pack_kernel, [SMEM] * 4 + [VMEM], [store_shape, wire_shape], [], "pack"
    )(band, send_list, quanta, dest_slot, tiled)
    arrived = trade(payload)
    acc = call(
        local_kernel,
        [SMEM] * 3 + [VMEM] * 3,
        store_shape,
        [VMEM((2 * LANES, 2 * LANES), f32)],
        "local",
    )(quanta, bath_row, rate_row, store, coupling, site_energy.reshape(1, -1))
    reply = call(answer_kernel, [SMEM, VMEM, VMEM], wire_shape, tag_scratch, "answer")(
        band, arrived, store
    )
    returned = trade(reply)
    total = call(
        raise_kernel,
        [SMEM, VMEM, VMEM],
        jax.ShapeDtypeStruct((2, padded, LANES), f32),
        [VMEM(store_shape.shape, f32)] + tag_scratch,
        "raise",
    )(band, arrived, acc)
    out = call(
        lower_kernel,
        [SMEM] * 6 + [VMEM] * 2,
        jax.ShapeDtypeStruct((aux * chunks, LANES), f32),
        [VMEM(store_shape.shape, f32)],
        "lower",
    )(band, send_list, quanta, bath_row, rate_row, strength_row, returned, total)
    return out.reshape(chunks, aux, LANES).transpose(1, 0, 2).reshape(aux, flat)


def solution(mesh):
    return jax.shard_map(
        on_device,
        mesh=mesh,
        in_specs=(
            P(("tier", "aux"), None),
            P(),
            P(),
            P(),
            P(),
            P(),
            P(("tier", "aux"), None),
            P(("tier", "aux"), None),
            P(("tier", "aux"), None),
        ),
        out_specs=P(("tier", "aux"), None),
        check_vma=False,
    )
```

time: 349 us -> 37 us (0.11)
  local copies, waits for them, and re-layouts: 192 us -> 3.16 us
  other arithmetic: 128 us -> 0 us
  starting transfers between devices: 20.7 us -> 2.63 us
  blocking collectives: 0 us -> 16.1 us
  Pallas kernels: 0 us -> 9.27 us
    gather x16 -> x0, local copies, waits for them, and re-layouts: 182 us -> none  [the longest x5 88.4 us: take_slices(): states[flat_holders[:, None], positions[None, :], flat_columns[:, None] +...]
    unnamed x7 -> x0, other arithmetic: 118 us -> none
    all_to_all x0 -> x1, blocking collectives: none -> 16.1 us  [on_device(): arrived = trade(payload)]
    all_to_all x3 -> x1, starting transfers between devices: 13.6 us -> 2.63 us  [on_device(): returned = trade(reply)]
    pallas_call x0 -> x5, Pallas kernels: none -> 9.27 us  [the longest x1 2.78 us: on_device(): call(lower_kernel, [SMEM] * 6 + [VMEM] * 2, jax.ShapeDtypeStruct((aux * c...]
    ppermute x3 -> x0, starting transfers between devices: 7.12 us -> none  [passed_along(): lax.ppermute(value, axis, [(source, source + steps) for source in range(f...]
    scatter-add x1 -> x0, other arithmetic: 5.61 us -> none  [on_device(): local_part.at[all_slot, all_site, :].add(all_data[:, :doubled_width])]
  transfers between devices with their start and end apart: 6 -> 1, of which waited for: 1 -> 1; matrix products, arithmetic and copies ran while one was open for 55% -> 0% of each run, Pallas kernels for 0% -> 9%
where the time goes in v1:
time: 37 us; the launch traced here: 36.7 us
  blocking collectives  16.1 us (44%)
  Pallas kernels  9.27 us (25%)
  waiting for transfers between devices  5.46 us (15%)
  local copies, waits for them, and re-layouts  3.16 us (9%)
  starting transfers between devices  2.63 us (7%)
    all_to_all x1, blocking collectives, on_device(): arrived = trade(payload)  16.1 us
    all_to_all x1, waiting for transfers between devices, on_device(): returned = trade(reply)  5.46 us
    unnamed x19, local copies, waits for them, and re-layouts  3.16 us
    pallas_call x1, Pallas kernels, on_device(): call(lower_kernel, [SMEM] * 6 + [VMEM] * 2, jax.ShapeDtypeStruct((aux * c...  2.78 us
    all_to_all x1, starting transfers between devices, on_device(): returned = trade(reply)  2.63 us
    pallas_call x1, Pallas kernels, on_device(): call(local_kernel, [SMEM] * 3 + [VMEM] * 3, store_shape, [VMEM((2 * LANES...  1.84 us
    pallas_call x1, Pallas kernels, on_device(): call(answer_kernel, [SMEM, VMEM, VMEM], wire_shape, tag_scratch, 'answer')  1.74 us
    pallas_call x1, Pallas kernels, on_device(): call(raise_kernel, [SMEM, VMEM, VMEM], jax.ShapeDtypeStruct((2, padded, L...  1.57 us
  transfers between devices with their start and end apart: 1, of which 1 were waited for; matrix products, arithmetic and copies ran while one was open for 0% of the time, Pallas kernels for 9%

profile of v1, /device:TPU:0, one launch (start us, length us, event | category | flops | bytes accessed | tf_op | source)
XLA Modules:
  0.0 36.7 jit_solution(7332595394565572569)
XLA Ops:
  0.0 0.8 %copy.12.quanta_ref = s32[8,4]{1,0:T(8,128)S(1)} copy(s32[8,4]{0,1:T(4,128)} %param.15) | data formatting | bytes 256 | tf_op args[6]
  0.8 0.0 copy-start
  0.8 1.1 %copy-done = f32[8,18432]{1,0:T(8,128)S(1)} copy-done((f32[8,18432]{1,0:T(8,128)S(1)}, f32[8,18432]{1,0:T(8,128)}, u32[]{:S(2)}) %copy-start) | copy-done | bytes 589848
  1.8 0.0 copy-start.2
  1.8 0.7 %copy-done.2 = s32[1,48]{1,0:T(1,128)S(1)} copy-done((s32[1,48]{1,0:T(1,128)S(1)}, s32[1,48]{1,0:T(1,128)}, u32[]{:S(2)}) %copy-start.2) | copy-done | bytes 216
  2.5 0.0 copy-start.7
  2.5 0.7 %copy-done.7 = s32[1,48]{1,0:T(1,128)S(1)} copy-done((s32[1,48]{1,0:T(1,128)S(1)}, s32[1,48]{1,0:T(1,128)}, u32[]{:S(2)}) %copy-start.7) | copy-done | bytes 216
  3.1 0.0 copy-start.1
  3.1 0.0 copy-start.4
  3.1 0.0 copy-start.5
  3.1 0.0 copy-start.8
  3.1 1.3 %pack.1 = (f32[4,800,128]{2,1,0:T(8,128)S(1)}, f32[32,1,1536]{2,1,0:T(1,128)S(1)}) custom-call(s32[1]{0:T(128)} %bitcast.band_ref, s32[1,48]{1,0:T(1,128)S(1)} %copy-done.2, s32[8,4]{1,0:T(8,128)S(1)} %copy.12.quanta_ref, s32[1,48]{1,0:T(1,128)S(1)} %copy-done.7, f32[1152,128]{1,0:T(8,128)S(1)} %bitcast.15), custom_call_target="tpu_custom_call" | custom-call | tf_op jit(solution)/shard_map/pack/pallas_call | solution.py:301
  4.5 16.1 %all_to_all.10.arrived_ref = f32[32,1,1536]{2,1,0:T(1,128)S(1)} all-to-all(f32[32,1,1536]{2,1,0:T(1,128)S(1)} %get-tuple-element.7), channel_id=1, replica_groups=mesh['tier'=4,'aux'=8] {'tier','aux'}, dimensions={0} | all-to-all | bytes 393216 | tf_op jit(solution)/shard_map/all_to_all | solution.py:304
  20.6 1.7 %answer.1 = f32[32,1,1536]{2,1,0:T(1,128)} custom-call(s32[1]{0:T(128)} %bitcast.band_ref, f32[32,1,1536]{2,1,0:T(1,128)S(1)} %all_to_all.10.arrived_ref, f32[4,800,128]{2,1,0:T(8,128)S(1)} %get-tuple-element.8.store_ref), custom_call_target="tpu_custom_call" | custom-call | tf_op jit(solution)/shard_map/answer/pallas_call | solution.py:312
  22.3 2.6 %all-to-all-start.1 = ((f32[32,1,1536]{2,1,0:T(1,128)}), f32[32,1,1536]{2,1,0:T(1,128)S(1)}, u32[]{:S(2)}, u32[]{:S(2)}) async-start(f32[32,1,1536]{2,1,0:T(1,128)} %answer.1), calls=%async_computation.1 | async-start | bytes 393216 | tf_op jit(solution)/shard_map/all_to_all | solution.py:315
  25.0 0.0 copy-done.1
  25.0 0.0 copy-done.4
  25.0 0.0 copy-done.5
  25.0 0.0 copy-done.8
  25.0 1.8 %local.1.acc_ref = f32[4,800,128]{2,1,0:T(8,128)S(1)} custom-call(s32[8,4]{1,0:T(8,128)S(1)} %copy.12.quanta_ref, s32[1,96]{1,0:T(1,128)S(1)} %bitcast.16, f32[1,96]{1,0:T(1,128)S(1)} %bitcast.18, f32[4,800,128]{2,1,0:T(8,128)S(1)} %get-tuple-element.8.store_ref, f32[96,96]{1,0:T(8,128)S(1)} %copy-done.1, f32[1,96]{1,0:T(1,128)S(1)} %bitcast.21), custom_call_target="tpu_custom_call" | custom-call | tf_op jit(solution)/shard_map/local/pallas_call | solution.py:305
  26.8 0.0 copy-start.3
  26.9 0.0 copy-start.6
  26.9 1.6 %raise.1.sum_ref = f32[2,800,128]{2,1,0:T(8,128)S(1)} custom-call(s32[1]{0:T(128)} %bitcast.band_ref, f32[32,1,1536]{2,1,0:T(1,128)S(1)} %all_to_all.10.arrived_ref, f32[4,800,128]{2,1,0:T(8,128)S(1)} %local.1.acc_ref), custom_call_target="tpu_custom_call" | custom-call | tf_op jit(solution)/shard_map/raise/pallas_call | solution.py:316
  28.4 5.5 %all-to-all-done.1.returned_ref = f32[32,1,1536]{2,1,0:T(1,128)S(1)} async-done(((f32[32,1,1536]{2,1,0:T(1,128)}), f32[32,1,1536]{2,1,0:T(1,128)S(1)}, u32[]{:S(2)}, u32[]{:S(2)}) %all-to-all-start.1) | async-done | bytes 196640 | tf_op jit(solution)/shard_map/all_to_all | solution.py:315
  33.9 0.0 copy-done.3
  33.9 0.0 copy-done.6
  33.9 2.8 %lower.1 = f32[1152,128]{1,0:T(8,128)} custom-call(s32[1]{0:T(128)} %bitcast.band_ref, s32[1,48]{1,0:T(1,128)S(1)} %copy-done.3, s32[8,4]{1,0:T(8,128)S(1)} %copy.12.quanta_ref, s32[1,96]{1,0:T(1,128)S(1)} %bitcast.17, f32[1,96]{1,0:T(1,128)S(1)} %bitcast.19, f32[1,96]{1,0:T(1,128)S(1)} %bitcast.20, f32[32,1,1536]{2,1,0:T(1,128)S(1)} %all-to-all-done.1.returned_ref, ...), custom_call_target="tpu_custom_call" | custom-call | tf_op jit(solution)/shard_map/lower/pallas_call | solution.py:323
Async XLA Ops:
  0.8 1.1 %copy-start = (f32[8,18432]{1,0:T(8,128)S(1)}, f32[8,18432]{1,0:T(8,128)}, u32[]{:S(2)}) copy-start(f32[8,18432]{1,0:T(8,128)} %param.9) | copy-start | bytes 1769476
  1.8 0.7 %copy-start.2 = (s32[1,48]{1,0:T(1,128)S(1)}, s32[1,48]{1,0:T(1,128)}, u32[]{:S(2)}) copy-start(s32[1,48]{1,0:T(1,128)} %send_ref.3) | copy-start | bytes 580
  2.5 0.7 %copy-start.7 = (s32[1,48]{1,0:T(1,128)S(1)}, s32[1,48]{1,0:T(1,128)}, u32[]{:S(2)}) copy-start(s32[1,48]{1,0:T(1,128)} %slot_ref.1) | copy-start | bytes 580
  3.1 21.8 %copy-start.1 = (f32[96,96]{1,0:T(8,128)S(1)}, f32[96,96]{1,0:T(8,128)}, u32[]{:S(2)}) copy-start(f32[96,96]{1,0:T(8,128)} %coupling_ref.1) | copy-start | bytes 110596
  3.1 21.8 %copy-start.4 = (s32[96]{0:T(128)S(1)}, s32[96]{0:T(128)}, u32[]{:S(2)}) copy-start(s32[96]{0:T(128)} %param.14) | copy-start | bytes 1156
  3.1 21.8 %copy-start.5 = (f32[96]{0:T(128)S(1)}, f32[96]{0:T(128)}, u32[]{:S(2)}) copy-start(f32[96]{0:T(128)} %param.12) | copy-start | bytes 1156
  3.1 21.9 %copy-start.8 = (f32[96]{0:T(128)S(1)}, f32[96]{0:T(128)}, u32[]{:S(2)}) copy-start(f32[96]{0:T(128)} %param.11) | copy-start | bytes 1156
  22.3 11.6 %all-to-all-start.1 = ((f32[32,1,1536]{2,1,0:T(1,128)}), f32[32,1,1536]{2,1,0:T(1,128)S(1)}, u32[]{:S(2)}, u32[]{:S(2)}) async-start(f32[32,1,1536]{2,1,0:T(1,128)} %answer.1), calls=%async_computation.1 | async-start | bytes 393216 | tf_op jit(solution)/shard_map/all_to_all | solution.py:315
  26.8 7.1 %copy-start.3 = (s32[1,48]{1,0:T(1,128)S(1)}, s32[1,48]{1,0:T(1,128)}, u32[]{:S(2)}) copy-start(s32[1,48]{1,0:T(1,128)} %send_ref.3) | copy-start | bytes 580
  26.9 7.1 %copy-start.6 = (f32[96]{0:T(128)S(1)}, f32[96]{0:T(128)}, u32[]{:S(2)}) copy-start(f32[96]{0:T(128)} %param.13) | copy-start | bytes 1156

commit v2 on v1

v2 whole, which is shorter than its diff:
```python
import functools

import jax
import jax.numpy as jnp
from jax import lax
from jax.experimental import pallas as pl
from jax.experimental.pallas import tpu as pltpu
from jax.sharding import PartitionSpec as P

thermal = 0.5
LANES = 128
SUB = 8
FIELDS = 3
VMEM = pltpu.VMEM
SMEM = pltpu.SMEM


def spec(space):
    return pl.BlockSpec(memory_space=space)


def lane_index(shape):
    return lax.broadcasted_iota(jnp.int32, shape, 1)


def merge(parts, lane, sites):
    spare = LANES - sites
    turned = [pltpu.roll(parts[FIELDS], sites - f * spare, 1) for f in range(FIELDS)]
    return [jnp.where(lane < sites, parts[f], turned[f]) for f in range(FIELDS)]


def unmerge(parts, lane, sites):
    spare = LANES - sites
    last = pltpu.roll(parts[FIELDS - 1], FIELDS * spare, 1)
    for f in reversed(range(FIELDS - 1)):
        last = jnp.where(lane < (f + 1) * spare, pltpu.roll(parts[f], (f + 1) * spare, 1), last)
    return list(parts) + [last]


def pack_kernel(
    sizes,
    band_ref,
    send_hbm,
    quanta_hbm,
    slot_hbm,
    state_hbm,
    store_ref,
    payload_ref,
    state_ref,
    send_ref,
    quanta_ref,
    slot_ref,
    sems,
    table_sems,
):
    sites, aux, depth, peers, capacity, tiers = sizes
    tiles = 4 * sites // LANES
    pair_blocks = sites // (2 * SUB)
    chunk = aux * tiles * SUB
    rows = aux * sites
    copies = [
        pltpu.make_async_copy(
            state_hbm.at[pl.ds(b * chunk, chunk), :],
            state_ref.at[pl.ds(b * chunk, chunk), :],
            sems.at[b],
        )
        for b in range(pair_blocks)
    ]
    tables = [
        pltpu.make_async_copy(source, target, table_sems.at[t])
        for t, (source, target) in enumerate(
            ((send_hbm, send_ref), (quanta_hbm, quanta_ref), (slot_hbm, slot_ref))
        )
    ]
    for copy in copies + tables:
        copy.start()
    lane = lane_index((SUB, LANES))
    store_ref[:, pl.ds(rows, LANES - sites), :] = jnp.zeros((4, LANES - sites, LANES), jnp.float32)
    for block in range(pair_blocks):
        copies[block].wait()
        for a in range(aux):
            first, middle, last = (
                state_ref[pl.ds(a + aux * (tiles * SUB * block + u), SUB, stride=aux * tiles), :]
                for u in range(tiles)
            )
            even_imag = jnp.where(lane < 32, pltpu.roll(first, 32, 1), pltpu.roll(middle, 32, 1))
            odd_real = jnp.where(lane < 64, pltpu.roll(middle, 64, 1), pltpu.roll(last, 64, 1))
            odd_imag = pltpu.roll(last, 96, 1)
            base = a * sites + 2 * SUB * block
            store_ref[0, pl.ds(base, SUB, stride=2), :] = first
            store_ref[1, pl.ds(base, SUB, stride=2), :] = even_imag
            store_ref[0, pl.ds(base + 1, SUB, stride=2), :] = odd_real
            store_ref[1, pl.ds(base + 1, SUB, stride=2), :] = odd_imag
    for a in range(aux):
        for c in range(2):
            block = store_ref[c, pl.ds(a * sites, LANES), :]
            store_ref[2 + c, pl.ds(a * sites, sites), :] = block.T[:sites, :]
    for table in tables:
        table.wait()
    band = band_ref[0]
    row_lane = lane_index((1, LANES))
    for g in (1, 0):
        target = jnp.maximum(band - g, 0)
        inside = band - g >= 0
        for q in range(peers):
            at_row = target * peers + q
            tags = jnp.zeros((1, LANES), jnp.int32)
            for j in range(capacity):
                l = (g * peers + q) * capacity + j
                entry = send_ref[0, l]
                clipped = jnp.maximum(entry, 0)
                source = clipped // depth
                site = quanta_ref[clipped % depth, source]
                usable = (entry >= 0) & (site >= 0) & inside
                site = jnp.maximum(site, 0)
                row = pl.ds(source * sites + site, 1)
                tags = jnp.where(
                    row_lane == 2 * j, jnp.where(usable, slot_ref[0, l] * sites, rows), tags
                )
                tags = jnp.where(row_lane == 2 * j + 1, jnp.where(usable, site, 0), tags)
                fields = merge([store_ref[f, row, :] for f in range(4)], row_lane, sites)
                for f in range(FIELDS):
                    payload_ref[at_row, :, pl.ds((j * FIELDS + f) * LANES, LANES)] = fields[f]
            payload_ref[at_row, :, pl.ds(capacity * FIELDS * LANES, LANES)] = tags.astype(
                jnp.float32
            )


def read_tags(sizes, band, arrived_ref, tag_ref, sems):
    sites, aux, depth, peers, capacity, tiers = sizes
    copies = [
        pltpu.make_async_copy(
            arrived_ref.at[
                pl.ds(jnp.minimum(band + g, tiers - 1) * peers, peers),
                :,
                pl.ds(capacity * FIELDS * LANES, LANES),
            ],
            tag_ref.at[pl.ds(g * peers, peers)],
            sems.at[g],
        )
        for g in range(2)
    ]
    for copy in copies:
        copy.start()
    return copies


def tag_row(tag_ref, g, p, j, peers):
    at = g * peers + p
    return tag_ref[at, 0, 2 * j].astype(jnp.int32) + tag_ref[at, 0, 2 * j + 1].astype(jnp.int32)


def answer_kernel(sizes, band_ref, arrived_ref, store_ref, reply_ref, tag_ref, sems):
    sites, aux, depth, peers, capacity, tiers = sizes
    band = band_ref[0]
    for copy in read_tags(sizes, band, arrived_ref, tag_ref, sems):
        copy.wait()
    for g in (1, 0):
        origin = jnp.minimum(band + g, tiers - 1)
        for p in range(peers):
            at_row = origin * peers + p
            for j in range(capacity):
                row = pl.ds(tag_row(tag_ref, g, p, j, peers), 1)
                for f in range(FIELDS):
                    reply_ref[at_row, :, pl.ds((j * FIELDS + f) * LANES, LANES)] = store_ref[
                        f, row, :
                    ]


def split(value):
    high = value.astype(jnp.bfloat16)
    low = (value - high.astype(jnp.float32)).astype(jnp.bfloat16)
    return high, low


def local_kernel(
    sizes,
    quanta_ref,
    bath_ref,
    rate_ref,
    store_ref,
    coupling_ref,
    energy_ref,
    acc_ref,
    merged_ref,
    matrix_ref,
):
    sites, aux, depth, peers, capacity, tiers = sizes
    row_ids = lax.broadcasted_iota(jnp.int32, (sites, sites), 0)
    col_ids = lax.broadcasted_iota(jnp.int32, (sites, sites), 1)
    coupling = coupling_ref[...]
    hamilton = (coupling + coupling.T) * 0.5 + jnp.where(row_ids == col_ids, energy_ref[...], 0.0)
    matrix_ref[...] = jnp.zeros_like(matrix_ref)
    matrix_ref[pl.ds(0, sites), pl.ds(LANES, sites)] = hamilton
    matrix_ref[pl.ds(LANES, sites), pl.ds(0, sites)] = -hamilton
    high, low = split(matrix_ref[...])
    dot = functools.partial(jnp.dot, preferred_element_type=jnp.float32)
    for a in range(aux):
        damp = jnp.float32(0.0)
        for place in range(depth):
            site = quanta_ref[place, a]
            rate = rate_ref[0, bath_ref[0, jnp.maximum(site, 0)]]
            damp = damp + jnp.where(site >= 0, rate, 0.0)
        here = pl.ds(a * sites, sites)
        for half in range(2):
            real, imag = store_ref[2 * half, here, :], store_ref[2 * half + 1, here, :]
            both = jnp.concatenate([real, imag], axis=1)
            both_high, both_low = split(both)
            product = dot(both_high, high) + (dot(both_low, high) + dot(both_high, low))
            if half == 0:
                product = product - damp * both
            else:
                product = -product
            acc_ref[2 * half, here, :] = product[:, :LANES]
            acc_ref[2 * half + 1, here, :] = product[:, LANES:]
        fields = merge([store_ref[f, here, :] for f in range(4)], lane_index((sites, LANES)), sites)
        for f in range(FIELDS):
            merged_ref[f, here, :] = fields[f]
    tail = pl.ds(aux * sites, LANES - sites)
    acc_ref[:, tail, :] = jnp.zeros((4, LANES - sites, LANES), jnp.float32)
    merged_ref[:, tail, :] = jnp.zeros((FIELDS, LANES - sites, LANES), jnp.float32)


def raise_kernel(
    sizes,
    band_ref,
    send_ref,
    quanta_ref,
    bath_ref,
    rate_ref,
    strength_ref,
    arrived_ref,
    acc_ref,
    sum_ref,
    column_ref,
    place_ref,
    coef_ref,
    work_ref,
    column_work,
    place_work,
    tag_ref,
    sems,
):
    sites, aux, depth, peers, capacity, tiers = sizes
    rows = aux * sites
    band = band_ref[0]
    copies = read_tags(sizes, band, arrived_ref, tag_ref, sems)
    row_lane = lane_index((1, LANES))
    work_ref[...] = acc_ref[...]
    column_work[...] = jnp.zeros_like(column_work)
    place_work[...] = jnp.zeros_like(place_work)
    half = column_work.shape[0] // 2
    for g in range(2):
        inside = band - g >= 0
        for q in range(peers):
            for j in range(capacity):
                l = (g * peers + q) * capacity + j
                at = (g * capacity + j) * peers + q
                entry = send_ref[0, l]
                clipped = jnp.maximum(entry, 0)
                source = clipped // depth
                site = quanta_ref[clipped % depth, source]
                usable = (entry >= 0) & (site >= 0) & inside
                safe = jnp.maximum(site, 0)
                weight = jnp.float32(0.0)
                for place in range(depth):
                    weight = weight + jnp.where(quanta_ref[place, source] == safe, 1.0, 0.0)
                weight = jnp.where(usable, weight, 0.0)
                bath = bath_ref[0, safe]
                strength = strength_ref[0, bath]
                turn = weight * (2.0 * thermal * strength)
                shared = -weight * (strength * rate_ref[0, bath])
                coef_ref[0, pl.ds(at, 1), :] = jnp.full((1, LANES), shared)
                coef_ref[1, pl.ds(at, 1), :] = jnp.full((1, LANES), turn)
                row = pl.ds(jnp.where(usable, source * sites + safe, rows), 1)
                for spot in (at, half + at):
                    slab = spot // LANES
                    place_work[slab, row, :] = jnp.where(
                        row_lane == spot % LANES, 1.0, place_work[slab, row, :]
                    )
                hot = (row_lane == safe).astype(jnp.float32)
                block = jnp.where(usable, source, aux)
                column_work[at, pl.ds(block, 1), :] = hot
                column_work[half + at, pl.ds(block, 1), :] = hot
    for slab in range(place_work.shape[0]):
        place_ref[:, pl.ds(slab * LANES, LANES)] = place_work[slab, pl.ds(0, rows), :].astype(
            jnp.bfloat16
        )
    for a in range(aux):
        column_ref[:, pl.ds(a * LANES, LANES)] = column_work[:, a, :].astype(jnp.bfloat16)
    for copy in copies:
        copy.wait()
    for g in range(2):
        origin = jnp.minimum(band + g, tiers - 1)
        inside = band + g < tiers
        for p in range(peers):
            at_row = origin * peers + p
            for j in range(capacity):
                row = pl.ds(jnp.where(inside, tag_row(tag_ref, g, p, j, peers), rows), 1)
                parts = unmerge(
                    [
                        arrived_ref[at_row, :, pl.ds((j * FIELDS + f) * LANES, LANES)]
                        for f in range(FIELDS)
                    ],
                    row_lane,
                    sites,
                )
                work_ref[0, row, :] = work_ref[0, row, :] + parts[1]
                work_ref[1, row, :] = work_ref[1, row, :] - parts[0]
                work_ref[2, row, :] = work_ref[2, row, :] - parts[3]
                work_ref[3, row, :] = work_ref[3, row, :] + parts[2]
    for a in range(aux):
        here = pl.ds(a * sites, sites)
        for c in range(2):
            turned = work_ref[2 + c, pl.ds(a * sites, LANES), :].T[:sites, :]
            sum_ref[c, here, :] = work_ref[c, here, :] + turned


def lower_kernel(
    sizes,
    band_ref,
    returned_ref,
    sum_ref,
    column_ref,
    place_ref,
    coef_ref,
    out_hbm,
    work_ref,
    edge_ref,
    out_ref,
    sems,
):
    sites, aux, depth, peers, capacity, tiers = sizes
    tiles = 4 * sites // LANES
    pair_blocks = sites // (2 * SUB)
    chunk = aux * tiles * SUB
    slabs = capacity * FIELDS
    used = 2 * capacity * peers
    half = edge_ref.shape[1] // 2
    band = band_ref[0]
    lane = lane_index((peers, LANES))
    if used < half:
        for top in (used, half + used):
            edge_ref[:, pl.ds(top, half - used), :] = jnp.zeros(
                (4, half - used, LANES), jnp.float32
            )
    for g in range(2):
        target = jnp.maximum(band - g, 0)
        for j in range(capacity):
            start = target * (peers * slabs) + j * FIELDS
            parts = [
                returned_ref[pl.ds(start + f, peers, stride=slabs), :] for f in range(FIELDS)
            ]
            row_real, row_imag, col_real, col_imag = unmerge(parts, lane, sites)
            base = (g * capacity + j) * peers
            shared = coef_ref[0, pl.ds(base, peers), :]
            turn = coef_ref[1, pl.ds(base, peers), :]
            values = (
                shared * row_real + turn * row_imag,
                shared * row_imag - turn * row_real,
                shared * col_real - turn * col_imag,
                shared * col_imag + turn * col_real,
            )
            for f, value in enumerate(values):
                high = value.astype(jnp.bfloat16).astype(jnp.float32)
                edge_ref[f, pl.ds(base, peers), :] = high
                edge_ref[f, pl.ds(half + base, peers), :] = value - high
    dot = functools.partial(jnp.dot, preferred_element_type=jnp.float32)
    row_data = jnp.concatenate([edge_ref[0], edge_ref[1]], axis=1).astype(jnp.bfloat16)
    col_data = jnp.concatenate([edge_ref[2].T, edge_ref[3].T], axis=0).astype(jnp.bfloat16)
    for pair in range(aux // 2):
        columns = dot(col_data, column_ref[:, pl.ds(2 * pair * LANES, 2 * LANES)])
        for o in range(2):
            here = pl.ds((2 * pair + o) * sites, sites)
            placed = dot(place_ref[here, :], row_data)
            for c in range(2):
                work_ref[c, here, :] = (
                    sum_ref[c, here, :]
                    + placed[:, c * LANES : (c + 1) * LANES]
                    + columns[c * LANES : c * LANES + sites, o * LANES : (o + 1) * LANES]
                )
    lane = lane_index((SUB, LANES))
    copies = []
    for block in range(pair_blocks):
        for a in range(aux):
            base = a * sites + 2 * SUB * block
            even_real, even_imag, odd_real, odd_imag = (
                work_ref[c, pl.ds(base + o, SUB, stride=2), :] for o in (0, 1) for c in (0, 1)
            )
            turned_imag = pltpu.roll(even_imag, 96, 1)
            turned_real = pltpu.roll(odd_real, 64, 1)
            parts = (
                jnp.where(lane < 96, even_real, turned_imag),
                jnp.where(lane < 64, turned_imag, turned_real),
                jnp.where(lane < 32, turned_real, pltpu.roll(odd_imag, 32, 1)),
            )
            for u in range(tiles):
                start = a + aux * (tiles * SUB * block + u)
                out_ref[pl.ds(start, SUB, stride=aux * tiles), :] = parts[u]
        here = pl.ds(block * chunk, chunk)
        copies.append(pltpu.make_async_copy(out_ref.at[here, :], out_hbm.at[here, :], sems.at[block]))
        copies[-1].start()
    for copy in copies:
        copy.wait()


def on_device(
    section_state,
    coupling,
    site_energy,
    bath_rate,
    bath_strength,
    bath_of_site,
    quanta,
    send_list,
    dest_slot,
):
    sites = coupling.shape[0]
    aux, flat = section_state.shape
    depth = quanta.shape[1]
    lane_count = send_list.shape[1]
    peers = lax.axis_size("aux")
    tiers = lax.axis_size("tier")
    capacity = lane_count // (2 * peers)
    sizes = (sites, aux, depth, peers, capacity, tiers)
    rows = aux * sites
    padded = rows + LANES - sites
    slabs = capacity * FIELDS
    chunks = flat // LANES
    half = -(-lane_count // 64) * 64
    f32 = jnp.float32
    bf16 = jnp.bfloat16
    band = lax.axis_index("tier").reshape(1)
    tiled = section_state.reshape(aux, chunks, LANES).transpose(1, 0, 2).reshape(-1, LANES)
    turned_quanta = quanta.T
    bath_row = bath_of_site.reshape(1, -1)
    rate_row = bath_rate.reshape(1, -1)
    strength_row = bath_strength.reshape(1, -1)
    pair_blocks = sites // (2 * SUB)

    def call(kernel, name, in_spaces, outs, scratch, out_spaces=None):
        return pl.pallas_call(
            functools.partial(kernel, sizes),
            out_shape=[jax.ShapeDtypeStruct(*out) for out in outs],
            in_specs=[spec(space) for space in in_spaces],
            out_specs=[spec(space) for space in out_spaces or [VMEM] * len(outs)],
            scratch_shapes=scratch,
            name=name,
            compiler_params=pltpu.CompilerParams(vmem_limit_bytes=24 * 1024 * 1024),
        )

    dma = pltpu.SemaphoreType.DMA
    store_shape = (4, padded, LANES)
    reply_shape = (tiers * peers, 1, slabs * LANES)
    payload_shape = (tiers * peers, 1, (slabs + 1) * LANES)
    tag_scratch = [SMEM((2 * peers, 1, LANES), f32), dma((2,))]
    flat_shape = (aux * chunks, LANES)
    trade = functools.partial(
        lax.all_to_all, axis_name=("tier", "aux"), split_axis=0, concat_axis=0, tiled=True
    )
    store, payload = call(
        pack_kernel,
        "pack",
        [SMEM] + [pltpu.HBM] * 4,
        [(store_shape, f32), (payload_shape, f32)],
        [
            VMEM(flat_shape, f32),
            SMEM(send_list.shape, jnp.int32),
            SMEM(turned_quanta.shape, jnp.int32),
            SMEM(dest_slot.shape, jnp.int32),
            dma((pair_blocks,)),
            dma((3,)),
        ],
    )(band, send_list, turned_quanta, dest_slot, tiled)
    arrived = trade(payload)
    acc, merged = call(
        local_kernel,
        "local",
        [SMEM] * 3 + [VMEM] * 3,
        [(store_shape, f32), ((FIELDS, padded, LANES), f32)],
        [VMEM((2 * LANES, 2 * LANES), f32)],
    )(turned_quanta, bath_row, rate_row, store, coupling, site_energy.reshape(1, -1))
    (reply,) = call(
        answer_kernel, "answer", [SMEM, VMEM, VMEM], [(reply_shape, f32)], tag_scratch
    )(band, arrived, merged)
    returned = trade(reply)
    total, columns, places, coefs = call(
        raise_kernel,
        "raise",
        [SMEM] * 6 + [VMEM] * 2,
        [
            ((2, rows, LANES), f32),
            ((2 * half, aux * LANES), bf16),
            ((rows, 2 * half), bf16),
            ((2, lane_count, LANES), f32),
        ],
        [VMEM(store_shape, f32), VMEM((2 * half, 2 * SUB, LANES), f32), VMEM((2 * half // LANES, padded, LANES), f32)]
        + tag_scratch,
    )(band, send_list, turned_quanta, bath_row, rate_row, strength_row, arrived, acc)
    (out,) = call(
        lower_kernel,
        "lower",
        [SMEM] + [VMEM] * 5,
        [(flat_shape, f32)],
        [
            VMEM((2, rows, LANES), f32),
            VMEM((4, 2 * half, LANES), f32),
            VMEM(flat_shape, f32),
            dma((pair_blocks,)),
        ],
        [pltpu.HBM],
    )(band, returned.reshape(-1, LANES), total, columns, places, coefs)
    return out.reshape(chunks, aux, LANES).transpose(1, 0, 2).reshape(aux, flat)


def solution(mesh):
    return jax.shard_map(
        on_device,
        mesh=mesh,
        in_specs=(
            P(("tier", "aux"), None),
            P(),
            P(),
            P(),
            P(),
            P(),
            P(("tier", "aux"), None),
            P(("tier", "aux"), None),
            P(("tier", "aux"), None),
        ),
        out_specs=P(("tier", "aux"), None),
        check_vma=False,
    )
```

time: 37 us -> 38.7 us (1.046)
  blocking collectives: 16.1 us -> 0 us
  starting transfers between devices: 2.63 us -> 10.9 us
  local copies, waits for them, and re-layouts: 3.16 us -> 8.85 us
  waiting for transfers between devices: 5.46 us -> 7.64 us
  Pallas kernels: 9.27 us -> 10.8 us
    all_to_all x1 -> x0, blocking collectives: 16.1 us -> none  [on_device(): arrived = trade(payload)]
    all_to_all x0 -> x1, starting transfers between devices: none -> 7.33 us  [on_device(): arrived = trade(payload)]
    unnamed x19 -> x32, local copies, waits for them, and re-layouts: 3.16 us -> 8.85 us
    all_to_all x0 -> x1, waiting for transfers between devices: none -> 2.28 us  [on_device(): arrived = trade(payload)]
    pallas_call x5, Pallas kernels: 9.27 us -> 10.8 us  [the longest x1 3 us: on_device(): call(raise_kernel, 'raise', [SMEM] * 6 + [VMEM] * 2, [((2, rows, LANES),...]
    all_to_all x1, starting transfers between devices: 2.63 us -> 3.56 us  [on_device(): returned = trade(reply)]
  transfers between devices with their start and end apart: 1 -> 2, of which waited for: 1 -> 2; matrix products, arithmetic and copies ran while one was open for 0% -> 0% of each run, Pallas kernels for 9% -> 13%
where the time goes in v2:
time: 38.7 us; the launch traced here: 38.3 us
  starting transfers between devices  10.9 us (28%)
  Pallas kernels  10.8 us (28%)
  local copies, waits for them, and re-layouts  8.85 us (23%)
  waiting for transfers between devices  7.64 us (20%)
    unnamed x32, local copies, waits for them, and re-layouts  8.85 us
    all_to_all x1, starting transfers between devices, on_device(): arrived = trade(payload)  7.33 us
    all_to_all x1, waiting for transfers between devices, on_device(): returned = trade(reply)  5.36 us
    all_to_all x1, starting transfers between devices, on_device(): returned = trade(reply)  3.56 us
    pallas_call x1, Pallas kernels, on_device(): call(raise_kernel, 'raise', [SMEM] * 6 + [VMEM] * 2, [((2, rows, LANES),...  3 us
    pallas_call x1, Pallas kernels, on_device(): call(pack_kernel, 'pack', [SMEM] + [pltpu.HBM] * 4, [(store_shape, f32),...  2.98 us
    all_to_all x1, waiting for transfers between devices, on_device(): arrived = trade(payload)  2.28 us
    pallas_call x1, Pallas kernels, on_device(): call(local_kernel, 'local', [SMEM] * 3 + [VMEM] * 3, [(store_shape, f32),...  1.81 us
  transfers between devices with their start and end apart: 2, of which 2 were waited for; matrix products, arithmetic and copies ran while one was open for 0% of the time, Pallas kernels for 13%

profile of v2, /device:TPU:0, one launch (start us, length us, event | category | flops | bytes accessed | tf_op | source)
XLA Modules:
  0.0 38.3 jit_solution(4753817366565764058)
XLA Ops:
  0.0 0.0 copy-start.2
  0.0 1.1 %copy-done.2 = f32[8,18432]{1,0:T(8,128)S(1)} copy-done((f32[8,18432]{1,0:T(8,128)S(1)}, f32[8,18432]{1,0:T(8,128)}, u32[]{:S(2)}) %copy-start.2) | copy-done | bytes 589848
  1.1 0.0 copy-start.4
  1.1 0.7 %copy-done.4 = s32[8,4]{0,1:T(4,128)S(1)} copy-done((s32[8,4]{0,1:T(4,128)S(1)}, s32[8,4]{0,1:T(4,128)}, u32[]{:S(2)}) %copy-start.4) | copy-done | bytes 152
  1.7 0.0 copy-start.11
  1.7 0.7 %copy-done.11 = s32[1,48]{1,0:T(1,128)S(1)} copy-done((s32[1,48]{1,0:T(1,128)S(1)}, s32[1,48]{1,0:T(1,128)}, u32[]{:S(2)}) %copy-start.11) | copy-done | bytes 216
  2.4 0.0 copy-start.14
  2.4 0.7 %copy-done.14 = s32[1,48]{1,0:T(1,128)S(1)} copy-done((s32[1,48]{1,0:T(1,128)S(1)}, s32[1,48]{1,0:T(1,128)}, u32[]{:S(2)}) %copy-start.14) | copy-done | bytes 216
  3.1 3.0 %pack.1 = (f32[4,800,128]{2,1,0:T(8,128)S(1)}, f32[32,1,1280]{2,1,0:T(1,128)}) custom-call(s32[1]{0:T(128)} %bitcast.band_ref, s32[1,48]{1,0:T(1,128)S(1)} %copy-done.11, s32[4,8]{1,0:T(4,128)S(1)} %bitcast.19, s32[1,48]{1,0:T(1,128)S(1)} %copy-done.14, f32[1152,128]{1,0:T(8,128)S(1)} %bitcast.18), custom_call_target="tpu_custom_call" | custom-call | tf_op jit(solution)/shard_map/pack/pallas_call | solution.py:461
  6.0 7.3 %all-to-all-start = ((f32[32,1,1280]{2,1,0:T(1,128)}), f32[32,1,1280]{2,1,0:T(1,128)S(1)}, u32[]{:S(2)}, u32[]{:S(2)}) async-start(f32[32,1,1280]{2,1,0:T(1,128)} %get-tuple-element.13), calls=%async_computation | async-start | bytes 327680 | tf_op jit(solution)/shard_map/all_to_all | solution.py:475
  13.4 0.0 copy-start.3
  13.4 0.8 %copy-done.3 = f32[96,96]{1,0:T(8,128)S(1)} copy-done((f32[96,96]{1,0:T(8,128)S(1)}, f32[96,96]{1,0:T(8,128)}, u32[]{:S(2)}) %copy-start.3) | copy-done | bytes 36888
  14.2 0.0 copy-start.5
  14.2 0.7 %copy-done.5 = s32[8,4]{0,1:T(4,128)S(1)} copy-done((s32[8,4]{0,1:T(4,128)S(1)}, s32[8,4]{0,1:T(4,128)}, u32[]{:S(2)}) %copy-start.5) | copy-done | bytes 152
  14.9 0.0 copy-start.7
  14.9 0.7 %copy-done.7 = s32[96]{0:T(128)S(1)} copy-done((s32[96]{0:T(128)S(1)}, s32[96]{0:T(128)}, u32[]{:S(2)}) %copy-start.7) | copy-done | bytes 408
  15.5 0.0 copy-start.9
  15.5 0.7 %copy-done.9 = f32[96]{0:T(128)S(1)} copy-done((f32[96]{0:T(128)S(1)}, f32[96]{0:T(128)}, u32[]{:S(2)}) %copy-start.9) | copy-done | bytes 408
  16.2 0.0 copy-start.13
  16.2 0.7 %copy-done.13 = f32[96]{0:T(128)S(1)} copy-done((f32[96]{0:T(128)S(1)}, f32[96]{0:T(128)}, u32[]{:S(2)}) %copy-start.13) | copy-done | bytes 408
  16.8 0.0 copy-start.6
  16.8 0.0 copy-start.8
  16.8 0.0 copy-start.10
  16.8 0.0 copy-start.12
  16.8 0.0 copy-start.15
  16.9 1.8 %local.1 = (f32[4,800,128]{2,1,0:T(8,128)S(1)}, f32[3,800,128]{2,1,0:T(8,128)S(1)}) custom-call(s32[4,8]{1,0:T(4,128)S(1)} %bitcast.20, s32[1,96]{1,0:T(1,128)S(1)} %bitcast.22, f32[1,96]{1,0:T(1,128)S(1)} %bitcast.24, f32[4,800,128]{2,1,0:T(8,128)S(1)} %get-tuple-element.14.store_ref, f32[96,96]{1,0:T(8,128)S(1)} %copy-done.3, f32[1,96]{1,0:T(1,128)S(1)} %bitcast.26), custom_call_target="tpu_custom_call" | custom-call | tf_op jit(solution)/shard_map/local/pallas_call | solution.py:476
  18.7 0.0 copy-start
  18.7 1.0 %copy-done = f32[3,800,128]{2,1,0:T(8,128)} copy-done((f32[3,800,128]{2,1,0:T(8,128)}, f32[3,800,128]{2,1,0:T(8,128)S(1)}, u32[]{:S(2)}) %copy-start) | copy-done | bytes 1228824
  19.7 2.3 %all-to-all-done.arrived_ref = f32[32,1,1280]{2,1,0:T(1,128)S(1)} async-done(((f32[32,1,1280]{2,1,0:T(1,128)}), f32[32,1,1280]{2,1,0:T(1,128)S(1)}, u32[]{:S(2)}, u32[]{:S(2)}) %all-to-all-start) | async-done | bytes 163872 | tf_op jit(solution)/shard_map/all_to_all | solution.py:475
  22.0 0.0 copy-start.1
  22.0 1.3 %copy-done.1 = f32[3,800,128]{2,1,0:T(8,128)S(1)} copy-done((f32[3,800,128]{2,1,0:T(8,128)S(1)}, f32[3,800,128]{2,1,0:T(8,128)}, u32[]{:S(2)}) %copy-start.1) | copy-done | bytes 1228824
  23.3 1.5 %answer.1 = f32[32,1,1152]{2,1,0:T(1,128)} custom-call(s32[1]{0:T(128)} %bitcast.band_ref, f32[32,1,1280]{2,1,0:T(1,128)S(1)} %all-to-all-done.arrived_ref, f32[3,800,128]{2,1,0:T(8,128)S(1)} %copy-done.1), custom_call_target="tpu_custom_call" | custom-call | tf_op jit(solution)/shard_map/answer/pallas_call | solution.py:483
  24.8 3.6 %all-to-all-start.1 = ((f32[32,1,1152]{2,1,0:T(1,128)}), f32[32,1,1152]{2,1,0:T(1,128)S(1)}, u32[]{:S(2)}, u32[]{:S(2)}) async-start(f32[32,1,1152]{2,1,0:T(1,128)} %answer.1), calls=%async_computation.1 | async-start | bytes 294912 | tf_op jit(solution)/shard_map/all_to_all | solution.py:486
  28.4 0.0 copy-done.6
  28.4 0.0 copy-done.8
  28.4 0.0 copy-done.10
  28.4 0.0 copy-done.12
  28.4 0.0 copy-done.15
  28.4 3.0 %raise.1 = (f32[2,768,128]{2,1,0:T(8,128)S(1)}, bf16[128,1024]{1,0:T(8,128)(2,1)S(1)}, bf16[768,128]{1,0:T(8,128)(2,1)S(1)}, f32[2,48,128]{2,1,0:T(8,128)S(1)}) custom-call(s32[1]{0:T(128)} %bitcast.band_ref, s32[1,48]{1,0:T(1,128)S(1)} %copy-done.12, s32[4,8]{1,0:T(4,128)S(1)} %bitcast.21, s32[1,96]{1,0:T(1,128)S(1)} %bitcast.23, f32[1,96]{1,0:T(1,128)S(1)} %bitcast.25, ...), custom_call_target="tpu_custom_call" | custom-call | tf_op jit(solution)/shard_map/raise/pallas_call | solution.py:487
  31.5 5.4 %all-to-all-done.1 = f32[32,1,1152]{2,1,0:T(1,128)S(1)} async-done(((f32[32,1,1152]{2,1,0:T(1,128)}), f32[32,1,1152]{2,1,0:T(1,128)S(1)}, u32[]{:S(2)}, u32[]{:S(2)}) %all-to-all-start.1) | async-done | bytes 147488 | tf_op jit(solution)/shard_map/all_to_all | solution.py:486
  36.8 1.5 %lower.1 = f32[1152,128]{1,0:T(8,128)} custom-call(s32[1]{0:T(128)} %bitcast.band_ref, f32[288,128]{1,0:T(8,128)S(1)} %bitcast.17, f32[2,768,128]{2,1,0:T(8,128)S(1)} %get-tuple-element.17.sum_ref, bf16[128,1024]{1,0:T(8,128)(2,1)S(1)} %get-tuple-element.18.column_ref, bf16[768,128]{1,0:T(8,128)(2,1)S(1)} %get-tuple-element.19.place_ref, ...), custom_call_target="tpu_custom_call" | custom-call | tf_op jit(solution)/shard_map/lower/pallas_call | solution.py:500
Async XLA Ops:
  0.0 1.1 %copy-start.2 = (f32[8,18432]{1,0:T(8,128)S(1)}, f32[8,18432]{1,0:T(8,128)}, u32[]{:S(2)}) copy-start(f32[8,18432]{1,0:T(8,128)} %param.9) | copy-start | bytes 1769476
  1.1 0.7 %copy-start.4 = (s32[8,4]{0,1:T(4,128)S(1)}, s32[8,4]{0,1:T(4,128)}, u32[]{:S(2)}) copy-start(s32[8,4]{0,1:T(4,128)} %param.15) | copy-start | bytes 388
  1.7 0.7 %copy-start.11 = (s32[1,48]{1,0:T(1,128)S(1)}, s32[1,48]{1,0:T(1,128)}, u32[]{:S(2)}) copy-start(s32[1,48]{1,0:T(1,128)} %send_ref.1) | copy-start | bytes 580
  2.4 0.7 %copy-start.14 = (s32[1,48]{1,0:T(1,128)S(1)}, s32[1,48]{1,0:T(1,128)}, u32[]{:S(2)}) copy-start(s32[1,48]{1,0:T(1,128)} %slot_hbm.1) | copy-start | bytes 580
  6.0 16.0 %all-to-all-start = ((f32[32,1,1280]{2,1,0:T(1,128)}), f32[32,1,1280]{2,1,0:T(1,128)S(1)}, u32[]{:S(2)}, u32[]{:S(2)}) async-start(f32[32,1,1280]{2,1,0:T(1,128)} %get-tuple-element.13), calls=%async_computation | async-start | bytes 327680 | tf_op jit(solution)/shard_map/all_to_all | solution.py:475
  13.4 0.8 %copy-start.3 = (f32[96,96]{1,0:T(8,128)S(1)}, f32[96,96]{1,0:T(8,128)}, u32[]{:S(2)}) copy-start(f32[96,96]{1,0:T(8,128)} %coupling_ref.1) | copy-start | bytes 110596
  14.2 0.7 %copy-start.5 = (s32[8,4]{0,1:T(4,128)S(1)}, s32[8,4]{0,1:T(4,128)}, u32[]{:S(2)}) copy-start(s32[8,4]{0,1:T(4,128)} %param.15) | copy-start | bytes 388
  14.9 0.7 %copy-start.7 = (s32[96]{0:T(128)S(1)}, s32[96]{0:T(128)}, u32[]{:S(2)}) copy-start(s32[96]{0:T(128)} %param.14) | copy-start | bytes 1156
  15.5 0.7 %copy-start.9 = (f32[96]{0:T(128)S(1)}, f32[96]{0:T(128)}, u32[]{:S(2)}) copy-start(f32[96]{0:T(128)} %param.12) | copy-start | bytes 1156
  16.2 0.7 %copy-start.13 = (f32[96]{0:T(128)S(1)}, f32[96]{0:T(128)}, u32[]{:S(2)}) copy-start(f32[96]{0:T(128)} %param.11) | copy-start | bytes 1156
  16.8 11.6 %copy-start.6 = (s32[8,4]{0,1:T(4,128)S(1)}, s32[8,4]{0,1:T(4,128)}, u32[]{:S(2)}) copy-start(s32[8,4]{0,1:T(4,128)} %param.15) | copy-start | bytes 388
  16.8 11.6 %copy-start.8 = (s32[96]{0:T(128)S(1)}, s32[96]{0:T(128)}, u32[]{:S(2)}) copy-start(s32[96]{0:T(128)} %param.14) | copy-start | bytes 1156
  16.8 11.6 %copy-start.10 = (f32[96]{0:T(128)S(1)}, f32[96]{0:T(128)}, u32[]{:S(2)}) copy-start(f32[96]{0:T(128)} %param.12) | copy-start | bytes 1156
  16.8 11.6 %copy-start.12 = (s32[1,48]{1,0:T(1,128)S(1)}, s32[1,48]{1,0:T(1,128)}, u32[]{:S(2)}) copy-start(s32[1,48]{1,0:T(1,128)} %send_ref.1) | copy-start | bytes 580
  16.8 11.6 %copy-start.15 = (f32[96]{0:T(128)S(1)}, f32[96]{0:T(128)}, u32[]{:S(2)}) copy-start(f32[96]{0:T(128)} %param.13) | copy-start | bytes 1156
  18.7 1.1 %copy-start = (f32[3,800,128]{2,1,0:T(8,128)}, f32[3,800,128]{2,1,0:T(8,128)S(1)}, u32[]{:S(2)}) copy-start(f32[3,800,128]{2,1,0:T(8,128)S(1)} %get-tuple-element.15.store_ref) | copy-start | bytes 3686404
  22.0 1.3 %copy-start.1 = (f32[3,800,128]{2,1,0:T(8,128)S(1)}, f32[3,800,128]{2,1,0:T(8,128)}, u32[]{:S(2)}) copy-start(f32[3,800,128]{2,1,0:T(8,128)} %copy-done) | copy-start | bytes 3686404
  24.8 12.0 %all-to-all-start.1 = ((f32[32,1,1152]{2,1,0:T(1,128)}), f32[32,1,1152]{2,1,0:T(1,128)S(1)}, u32[]{:S(2)}, u32[]{:S(2)}) async-start(f32[32,1,1152]{2,1,0:T(1,128)} %answer.1), calls=%async_computation.1 | async-start | bytes 294912 | tf_op jit(solution)/shard_map/all_to_all | solution.py:486

commit v3 on v2

--- a/solution.py
+++ b/solution.py
@@ -21,6 +21,23 @@
 
 def lane_index(shape):
     return lax.broadcasted_iota(jnp.int32, shape, 1)
+
+
+def fetch(pairs, sems):
+    copies = [
+        pltpu.make_async_copy(source, target, sems.at[n]) for n, (source, target) in enumerate(pairs)
+    ]
+    for copy in copies:
+        copy.start()
+    return copies
+
+
+def send_blocks(work_ref, wire_hbm, sems, band, step, tiers, peers):
+    def block(g):
+        at = jnp.clip(band + g * step, 0, tiers - 1) * peers
+        return pltpu.make_async_copy(work_ref.at[g], wire_hbm.at[pl.ds(at, peers)], sems.at[g])
+
+    return block
 
 
 def merge(parts, lane, sites):
@@ -45,35 +62,31 @@
     slot_hbm,
     state_hbm,
     store_ref,
+    payload_hbm,
+    state_ref,
     payload_ref,
-    state_ref,
     send_ref,
     quanta_ref,
     slot_ref,
     sems,
     table_sems,
+    wire_sems,
 ):
     sites, aux, depth, peers, capacity, tiers = sizes
     tiles = 4 * sites // LANES
     pair_blocks = sites // (2 * SUB)
     chunk = aux * tiles * SUB
     rows = aux * sites
-    copies = [
-        pltpu.make_async_copy(
-            state_hbm.at[pl.ds(b * chunk, chunk), :],
-            state_ref.at[pl.ds(b * chunk, chunk), :],
-            sems.at[b],
-        )
-        for b in range(pair_blocks)
-    ]
-    tables = [
-        pltpu.make_async_copy(source, target, table_sems.at[t])
-        for t, (source, target) in enumerate(
-            ((send_hbm, send_ref), (quanta_hbm, quanta_ref), (slot_hbm, slot_ref))
-        )
-    ]
-    for copy in copies + tables:
-        copy.start()
+    copies = fetch(
+        [
+            (state_hbm.at[pl.ds(b * chunk, chunk), :], state_ref.at[pl.ds(b * chunk, chunk), :])
+            for b in range(pair_blocks)
+        ],
+        sems,
+    )
+    tables = fetch(
+        [(send_hbm, send_ref), (quanta_hbm, quanta_ref), (slot_hbm, slot_ref)], table_sems
+    )
     lane = lane_index((SUB, LANES))
     store_ref[:, pl.ds(rows, LANES - sites), :] = jnp.zeros((4, LANES - sites, LANES), jnp.float32)
     for block in range(pair_blocks):
@@ -99,11 +112,10 @@
         table.wait()
     band = band_ref[0]
     row_lane = lane_index((1, LANES))
+    block = send_blocks(payload_ref, payload_hbm, wire_sems, band, -1, tiers, peers)
     for g in (1, 0):
-        target = jnp.maximum(band - g, 0)
         inside = band - g >= 0
         for q in range(peers):
-            at_row = target * peers + q
             tags = jnp.zeros((1, LANES), jnp.int32)
             for j in range(capacity):
                 l = (g * peers + q) * capacity + j
@@ -120,10 +132,14 @@
                 tags = jnp.where(row_lane == 2 * j + 1, jnp.where(usable, site, 0), tags)
                 fields = merge([store_ref[f, row, :] for f in range(4)], row_lane, sites)
                 for f in range(FIELDS):
-                    payload_ref[at_row, :, pl.ds((j * FIELDS + f) * LANES, LANES)] = fields[f]
-            payload_ref[at_row, :, pl.ds(capacity * FIELDS * LANES, LANES)] = tags.astype(
-                jnp.float32
-            )
+                    payload_ref[g, q, :, pl.ds((j * FIELDS + f) * LANES, LANES)] = fields[f]
+            payload_ref[g, q, :, pl.ds(capacity * FIELDS * LANES, LANES)] = tags.astype(jnp.float32)
+        if g == 0:
+            block(g).start()
+        else:
+            pl.when(inside)(block(g).start)
+    block(0).wait()
+    pl.when(band >= 1)(block(1).wait)
 
 
 def read_tags(sizes, band, arrived_ref, tag_ref, sems):
@@ -150,21 +166,27 @@
     return tag_ref[at, 0, 2 * j].astype(jnp.int32) + tag_ref[at, 0, 2 * j + 1].astype(jnp.int32)
 
 
-def answer_kernel(sizes, band_ref, arrived_ref, store_ref, reply_ref, tag_ref, sems):
+def answer_kernel(
+    sizes, band_ref, arrived_ref, store_ref, reply_hbm, reply_ref, tag_ref, sems, wire_sems
+):
     sites, aux, depth, peers, capacity, tiers = sizes
     band = band_ref[0]
-    for copy in read_tags(sizes, band, arrived_ref, tag_ref, sems):
+    copies = read_tags(sizes, band, arrived_ref, tag_ref, sems)
+    block = send_blocks(reply_ref, reply_hbm, wire_sems, band, 1, tiers, peers)
+    for copy in copies:
         copy.wait()
     for g in (1, 0):
-        origin = jnp.minimum(band + g, tiers - 1)
         for p in range(peers):
-            at_row = origin * peers + p
             for j in range(capacity):
                 row = pl.ds(tag_row(tag_ref, g, p, j, peers), 1)
                 for f in range(FIELDS):
-                    reply_ref[at_row, :, pl.ds((j * FIELDS + f) * LANES, LANES)] = store_ref[
-                        f, row, :
-                    ]
+                    reply_ref[g, p, :, pl.ds((j * FIELDS + f) * LANES, LANES)] = store_ref[f, row, :]
+        if g == 0:
+            block(g).start()
+        else:
+            pl.when(band + g < tiers)(block(g).start)
+    block(0).wait()
+    pl.when(band + 1 < tiers)(block(1).wait)
 
 
 def split(value):
@@ -175,19 +197,39 @@
 
 def local_kernel(
     sizes,
+    quanta_hbm,
+    bath_hbm,
+    rate_hbm,
+    coupling_hbm,
+    energy_hbm,
+    store_ref,
+    acc_hbm,
+    merged_ref,
+    acc_ref,
+    matrix_ref,
+    coupling_ref,
+    energy_ref,
     quanta_ref,
     bath_ref,
     rate_ref,
-    store_ref,
-    coupling_ref,
-    energy_ref,
-    acc_ref,
-    merged_ref,
-    matrix_ref,
+    sems,
+    acc_sems,
 ):
     sites, aux, depth, peers, capacity, tiers = sizes
     row_ids = lax.broadcasted_iota(jnp.int32, (sites, sites), 0)
     col_ids = lax.broadcasted_iota(jnp.int32, (sites, sites), 1)
+    copies = fetch(
+        [
+            (coupling_hbm, coupling_ref),
+            (energy_hbm, energy_ref),
+            (quanta_hbm, quanta_ref),
+            (bath_hbm, bath_ref),
+            (rate_hbm, rate_ref),
+        ],
+        sems,
+    )
+    for copy in copies:
+        copy.wait()
     coupling = coupling_ref[...]
     hamilton = (coupling + coupling.T) * 0.5 + jnp.where(row_ids == col_ids, energy_ref[...], 0.0)
     matrix_ref[...] = jnp.zeros_like(matrix_ref)
@@ -195,6 +237,7 @@
     matrix_ref[pl.ds(LANES, sites), pl.ds(0, sites)] = -hamilton
     high, low = split(matrix_ref[...])
     dot = functools.partial(jnp.dot, preferred_element_type=jnp.float32)
+    saves = []
     for a in range(aux):
         damp = jnp.float32(0.0)
         for place in range(depth):
@@ -216,21 +259,26 @@
         fields = merge([store_ref[f, here, :] for f in range(4)], lane_index((sites, LANES)), sites)
         for f in range(FIELDS):
             merged_ref[f, here, :] = fields[f]
+        saves.append(
+            pltpu.make_async_copy(acc_ref.at[:, here, :], acc_hbm.at[:, here, :], acc_sems.at[a])
+        )
+        saves[-1].start()
     tail = pl.ds(aux * sites, LANES - sites)
-    acc_ref[:, tail, :] = jnp.zeros((4, LANES - sites, LANES), jnp.float32)
     merged_ref[:, tail, :] = jnp.zeros((FIELDS, LANES - sites, LANES), jnp.float32)
+    for save in saves:
+        save.wait()
 
 
 def raise_kernel(
     sizes,
     band_ref,
-    send_ref,
-    quanta_ref,
-    bath_ref,
-    rate_ref,
-    strength_ref,
+    send_hbm,
+    quanta_hbm,
+    bath_hbm,
+    rate_hbm,
+    strength_hbm,
     arrived_ref,
-    acc_ref,
+    acc_hbm,
     sum_ref,
     column_ref,
     place_ref,
@@ -238,6 +286,13 @@
     work_ref,
     column_work,
     place_work,
+    send_ref,
+    quanta_ref,
+    bath_ref,
+    rate_ref,
+    strength_ref,
+    table_sems,
+    acc_sems,
     tag_ref,
     sems,
 ):
@@ -245,11 +300,25 @@
     rows = aux * sites
     band = band_ref[0]
     copies = read_tags(sizes, band, arrived_ref, tag_ref, sems)
+    tables = fetch(
+        [
+            (send_hbm, send_ref),
+            (quanta_hbm, quanta_ref),
+            (bath_hbm, bath_ref),
+            (rate_hbm, rate_ref),
+            (strength_hbm, strength_ref),
+        ],
+        table_sems,
+    )
+    (load,) = fetch([(acc_hbm, work_ref.at[:, pl.ds(0, rows), :])], acc_sems)
+    tail = pl.ds(rows, LANES - sites)
+    work_ref[:, tail, :] = jnp.zeros((4, LANES - sites, LANES), jnp.float32)
     row_lane = lane_index((1, LANES))
-    work_ref[...] = acc_ref[...]
     column_work[...] = jnp.zeros_like(column_work)
     place_work[...] = jnp.zeros_like(place_work)
     half = column_work.shape[0] // 2
+    for table in tables:
+        table.wait()
     for g in range(2):
         inside = band - g >= 0
         for q in range(peers):
@@ -290,6 +359,7 @@
         column_ref[:, pl.ds(a * LANES, LANES)] = column_work[:, a, :].astype(jnp.bfloat16)
     for copy in copies:
         copy.wait()
+    load.wait()
     for g in range(2):
         origin = jnp.minimum(band + g, tiers - 1)
         inside = band + g < tiers
@@ -438,78 +508,144 @@
     strength_row = bath_strength.reshape(1, -1)
     pair_blocks = sites // (2 * SUB)
 
-    def call(kernel, name, in_spaces, outs, scratch, out_spaces=None):
+    def call(kernel, name, inputs, outs, scratch):
+        spaces = [space for space, _ in inputs]
+        values = [
+            value if space is SMEM else pltpu.with_memory_space_constraint(value, space)
+            for space, value in inputs
+        ]
         return pl.pallas_call(
             functools.partial(kernel, sizes),
-            out_shape=[jax.ShapeDtypeStruct(*out) for out in outs],
-            in_specs=[spec(space) for space in in_spaces],
-            out_specs=[spec(space) for space in out_spaces or [VMEM] * len(outs)],
+            out_shape=[space(shape, dtype) for space, shape, dtype in outs],
+            in_specs=[spec(space) for space in spaces],
+            out_specs=[spec(space) for space, _, _ in outs],
             scratch_shapes=scratch,
             name=name,
             compiler_params=pltpu.CompilerParams(vmem_limit_bytes=24 * 1024 * 1024),
-        )
-
+        )(*values)
+
+    HBM = pltpu.HBM
     dma = pltpu.SemaphoreType.DMA
     store_shape = (4, padded, LANES)
+    acc_shape = (4, rows, LANES)
     reply_shape = (tiers * peers, 1, slabs * LANES)
     payload_shape = (tiers * peers, 1, (slabs + 1) * LANES)
     tag_scratch = [SMEM((2 * peers, 1, LANES), f32), dma((2,))]
     flat_shape = (aux * chunks, LANES)
+    send_table = SMEM(send_list.shape, jnp.int32)
+    quanta_table = SMEM(turned_quanta.shape, jnp.int32)
+    bath_table = SMEM(bath_row.shape, jnp.int32)
+    site_table = SMEM(rate_row.shape, f32)
     trade = functools.partial(
         lax.all_to_all, axis_name=("tier", "aux"), split_axis=0, concat_axis=0, tiled=True
     )
     store, payload = call(
         pack_kernel,
         "pack",
-        [SMEM] + [pltpu.HBM] * 4,
-        [(store_shape, f32), (payload_shape, f32)],
+        [
+            (SMEM, band),
+            (HBM, send_list),
+            (HBM, turned_quanta),
+            (HBM, dest_slot),
+            (HBM, tiled),
+        ],
+        [(VMEM, store_shape, f32), (HBM, payload_shape, f32)],
         [
             VMEM(flat_shape, f32),
-            SMEM(send_list.shape, jnp.int32),
-            SMEM(turned_quanta.shape, jnp.int32),
-            SMEM(dest_slot.shape, jnp.int32),
+            VMEM((2, peers) + payload_shape[1:], f32),
+            send_table,
+            quanta_table,
+            send_table,
             dma((pair_blocks,)),
             dma((3,)),
-        ],
-    )(band, send_list, turned_quanta, dest_slot, tiled)
+            dma((2,)),
+        ],
+    )
     arrived = trade(payload)
     acc, merged = call(
         local_kernel,
         "local",
-        [SMEM] * 3 + [VMEM] * 3,
-        [(store_shape, f32), ((FIELDS, padded, LANES), f32)],
-        [VMEM((2 * LANES, 2 * LANES), f32)],
-    )(turned_quanta, bath_row, rate_row, store, coupling, site_energy.reshape(1, -1))
+        [
+            (HBM, turned_quanta),
+            (HBM, bath_row),
+            (HBM, rate_row),
+            (HBM, coupling),
+            (HBM, site_energy.reshape(1, -1)),
+            (VMEM, store),
+        ],
+        [(HBM, acc_shape, f32), (VMEM, (FIELDS, padded, LANES), f32)],
+        [
+            VMEM(acc_shape, f32),
+            VMEM((2 * LANES, 2 * LANES), f32),
+            VMEM(coupling.shape, f32),
+            VMEM(rate_row.shape, f32),
+            quanta_table,
+            bath_table,
+            site_table,
+            dma((5,)),
+            dma((aux,)),
+        ],
+    )
     (reply,) = call(
-        answer_kernel, "answer", [SMEM, VMEM, VMEM], [(reply_shape, f32)], tag_scratch
-    )(band, arrived, merged)
+        answer_kernel,
+        "answer",
+        [(SMEM, band), (VMEM, arrived), (VMEM, merged)],
+        [(HBM, reply_shape, f32)],
+        [VMEM((2, peers) + reply_shape[1:], f32)] + tag_scratch + [dma((2,))],
+    )
     returned = trade(reply)
     total, columns, places, coefs = call(
         raise_kernel,
         "raise",
-        [SMEM] * 6 + [VMEM] * 2,
-        [
-            ((2, rows, LANES), f32),
-            ((2 * half, aux * LANES), bf16),
-            ((rows, 2 * half), bf16),
-            ((2, lane_count, LANES), f32),
-        ],
-        [VMEM(store_shape, f32), VMEM((2 * half, 2 * SUB, LANES), f32), VMEM((2 * half // LANES, padded, LANES), f32)]
+        [
+            (SMEM, band),
+            (HBM, send_list),
+            (HBM, turned_quanta),
+            (HBM, bath_row),
+            (HBM, rate_row),
+            (HBM, strength_row),
+            (VMEM, arrived),
+            (HBM, acc),
+        ],
+        [
+            (VMEM, (2, rows, LANES), f32),
+            (VMEM, (2 * half, aux * LANES), bf16),
+            (VMEM, (rows, 2 * half), bf16),
+            (VMEM, (2, lane_count, LANES), f32),
+        ],
+        [
+            VMEM(store_shape, f32),
+            VMEM((2 * half, 2 * SUB, LANES), f32),
+            VMEM((2 * half // LANES, padded, LANES), f32),
+            send_table,
+            quanta_table,
+            bath_table,
+            site_table,
+            site_table,
+            dma((5,)),
+            dma((1,)),
+        ]
         + tag_scratch,
-    )(band, send_list, turned_quanta, bath_row, rate_row, strength_row, arrived, acc)
+    )
     (out,) = call(
         lower_kernel,
         "lower",
-        [SMEM] + [VMEM] * 5,
-        [(flat_shape, f32)],
+        [
+            (SMEM, band),
+            (VMEM, returned.reshape(-1, LANES)),
+            (VMEM, total),
+            (VMEM, columns),
+            (VMEM, places),
+            (VMEM, coefs),
+        ],
+        [(HBM, flat_shape, f32)],
         [
             VMEM((2, rows, LANES), f32),
             VMEM((4, 2 * half, LANES), f32),
             VMEM(flat_shape, f32),
             dma((pair_blocks,)),
         ],
-        [pltpu.HBM],
-    )(band, returned.reshape(-1, LANES), total, columns, places, coefs)
+    )
     return out.reshape(chunks, aux, LANES).transpose(1, 0, 2).reshape(aux, flat)
 
 

time: 38.7 us -> 33.4 us (0.86)
  local copies, waits for them, and re-layouts: 8.85 us -> 0 us
  waiting for transfers between devices: 7.64 us -> 10.8 us
  Pallas kernels: 10.8 us -> 12.3 us
  starting transfers between devices: 10.9 us -> 9.93 us
    unnamed x32 -> x0, local copies, waits for them, and re-layouts: 8.85 us -> none
    all_to_all x1, waiting for transfers between devices: 2.28 us -> 5.75 us  [on_device(): arrived = trade(payload)]
    pallas_call x5, Pallas kernels: 10.8 us -> 12.3 us  [call(): pl.pallas_call(functools.partial(kernel, sizes), out_shape=[space(shape,...]
    all_to_all x1, starting transfers between devices: 3.56 us -> 2.59 us  [on_device(): returned = trade(reply)]
  transfers between devices with their start and end apart: 2 -> 2, of which waited for: 2 -> 2; matrix products, arithmetic and copies ran while one was open for 0% -> 0% of each run, Pallas kernels for 13% -> 19%
where the time goes in v3:
time: 33.4 us; the launch traced here: 33.1 us
  Pallas kernels  12.3 us (37%)
  waiting for transfers between devices  10.8 us (32%)
  starting transfers between devices  9.93 us (30%)
    pallas_call x5, Pallas kernels, call(): pl.pallas_call(functools.partial(kernel, sizes), out_shape=[space(shape,...  12.3 us
    all_to_all x1, starting transfers between devices, on_device(): arrived = trade(payload)  7.33 us
    all_to_all x1, waiting for transfers between devices, on_device(): arrived = trade(payload)  5.75 us
    all_to_all x1, waiting for transfers between devices, on_device(): returned = trade(reply)  5.07 us
    all_to_all x1, starting transfers between devices, on_device(): returned = trade(reply)  2.59 us
  transfers between devices with their start and end apart: 2, of which 2 were waited for; matrix products, arithmetic and copies ran while one was open for 0% of the time, Pallas kernels for 19%

profile of v3, /device:TPU:0, one launch (start us, length us, event | category | flops | bytes accessed | tf_op | source)
XLA Modules:
  0.0 33.1 jit_solution(16491754988799749648)
XLA Ops:
  0.0 3.1 %pack.1 = (f32[4,800,128]{2,1,0:T(8,128)S(1)}, f32[32,1,1280]{2,1,0:T(1,128)}) custom-call(s32[1]{0:T(128)} %bitcast.band_ref, s32[1,48]{1,0:T(1,128)} %send_hbm.3, s32[4,8]{1,0:T(4,128)} %bitcast.19, s32[1,48]{1,0:T(1,128)} %slot_hbm.1, f32[1152,128]{1,0:T(8,128)} %bitcast.18), custom_call_target="tpu_custom_call" | custom-call | tf_op jit(solution)/shard_map/pack/pallas_call | solution.py:517
  3.1 7.3 %all-to-all-start = ((f32[32,1,1280]{2,1,0:T(1,128)}), f32[32,1,1280]{2,1,0:T(1,128)S(1)}, u32[]{:S(2)}, u32[]{:S(2)}) async-start(f32[32,1,1280]{2,1,0:T(1,128)} %get-tuple-element.13), calls=%async_computation | async-start | bytes 327680 | tf_op jit(solution)/shard_map/all_to_all | solution.py:564
  10.5 2.9 %local.1 = (f32[4,768,128]{2,1,0:T(8,128)}, f32[3,800,128]{2,1,0:T(8,128)S(1)}) custom-call(s32[4,8]{1,0:T(4,128)} %bitcast.20, s32[1,96]{1,0:T(1,128)} %bitcast.22, f32[1,96]{1,0:T(1,128)} %bitcast.24, f32[96,96]{1,0:T(8,128)} %coupling_hbm.1, f32[1,96]{1,0:T(1,128)} %bitcast.27, f32[4,800,128]{2,1,0:T(8,128)S(1)} %get-tuple-element.14.store_ref), custom_call_target="tpu_custom_call" | custom-call | tf_op jit(solution)/shard_map/local/pallas_call | solution.py:517
  13.3 5.8 %all-to-all-done.arrived_ref = f32[32,1,1280]{2,1,0:T(1,128)S(1)} async-done(((f32[32,1,1280]{2,1,0:T(1,128)}), f32[32,1,1280]{2,1,0:T(1,128)S(1)}, u32[]{:S(2)}, u32[]{:S(2)}) %all-to-all-start) | async-done | bytes 163872 | tf_op jit(solution)/shard_map/all_to_all | solution.py:564
  19.1 1.5 %answer.1 = f32[32,1,1152]{2,1,0:T(1,128)} custom-call(s32[1]{0:T(128)} %bitcast.band_ref, f32[32,1,1280]{2,1,0:T(1,128)S(1)} %all-to-all-done.arrived_ref, f32[3,800,128]{2,1,0:T(8,128)S(1)} %get-tuple-element.15.store_ref), custom_call_target="tpu_custom_call" | custom-call | tf_op jit(solution)/shard_map/answer/pallas_call | solution.py:517
  20.6 2.6 %all-to-all-start.1 = ((f32[32,1,1152]{2,1,0:T(1,128)}), f32[32,1,1152]{2,1,0:T(1,128)S(1)}, u32[]{:S(2)}, u32[]{:S(2)}) async-start(f32[32,1,1152]{2,1,0:T(1,128)} %answer.1), calls=%async_computation.1 | async-start | bytes 294912 | tf_op jit(solution)/shard_map/all_to_all | solution.py:596
  23.2 3.3 %raise.1 = (f32[2,768,128]{2,1,0:T(8,128)S(1)}, bf16[128,1024]{1,0:T(8,128)(2,1)S(1)}, bf16[768,128]{1,0:T(8,128)(2,1)S(1)}, f32[2,48,128]{2,1,0:T(8,128)S(1)}) custom-call(s32[1]{0:T(128)} %bitcast.band_ref, s32[1,48]{1,0:T(1,128)} %send_hbm.3, s32[4,8]{1,0:T(4,128)} %bitcast.21, s32[1,96]{1,0:T(1,128)} %bitcast.23, f32[1,96]{1,0:T(1,128)} %bitcast.25, ...), custom_call_target="tpu_custom_call" | custom-call | tf_op jit(solution)/shard_map/raise/pallas_call | solution.py:517
  26.5 5.1 %all-to-all-done.1 = f32[32,1,1152]{2,1,0:T(1,128)S(1)} async-done(((f32[32,1,1152]{2,1,0:T(1,128)}), f32[32,1,1152]{2,1,0:T(1,128)S(1)}, u32[]{:S(2)}, u32[]{:S(2)}) %all-to-all-start.1) | async-done | bytes 147488 | tf_op jit(solution)/shard_map/all_to_all | solution.py:596
  31.6 1.5 %lower.1 = f32[1152,128]{1,0:T(8,128)} custom-call(s32[1]{0:T(128)} %bitcast.band_ref, f32[288,128]{1,0:T(8,128)S(1)} %bitcast.17, f32[2,768,128]{2,1,0:T(8,128)S(1)} %get-tuple-element.17.sum_ref, bf16[128,1024]{1,0:T(8,128)(2,1)S(1)} %get-tuple-element.18.column_ref, bf16[768,128]{1,0:T(8,128)(2,1)S(1)} %get-tuple-element.19.place_ref, ...), custom_call_target="tpu_custom_call" | custom-call | tf_op jit(solution)/shard_map/lower/pallas_call | solution.py:517
Async XLA Ops:
  3.1 16.0 %all-to-all-start = ((f32[32,1,1280]{2,1,0:T(1,128)}), f32[32,1,1280]{2,1,0:T(1,128)S(1)}, u32[]{:S(2)}, u32[]{:S(2)}) async-start(f32[32,1,1280]{2,1,0:T(1,128)} %get-tuple-element.13), calls=%async_computation | async-start | bytes 327680 | tf_op jit(solution)/shard_map/all_to_all | solution.py:564
  20.6 11.0 %all-to-all-start.1 = ((f32[32,1,1152]{2,1,0:T(1,128)}), f32[32,1,1152]{2,1,0:T(1,128)S(1)}, u32[]{:S(2)}, u32[]{:S(2)}) async-start(f32[32,1,1152]{2,1,0:T(1,128)} %answer.1), calls=%async_computation.1 | async-start | bytes 294912 | tf_op jit(solution)/shard_map/all_to_all | solution.py:596

commit v4 on v3

--- a/solution.py
+++ b/solution.py
@@ -11,6 +11,7 @@
 LANES = 128
 SUB = 8
 FIELDS = 3
+TAG = 64
 VMEM = pltpu.VMEM
 SMEM = pltpu.SMEM
 
@@ -41,17 +42,28 @@
 
 
 def merge(parts, lane, sites):
+    rest = 2 * sites - LANES
+    first, second, col_real, col_imag = parts
+    return [
+        first,
+        jnp.where(lane < rest, second, pltpu.roll(col_imag, rest, 1)),
+        jnp.where(lane < sites, col_real, pltpu.roll(col_imag, sites + rest - LANES, 1)),
+    ]
+
+
+def imaginary(first, second, lane, sites):
     spare = LANES - sites
-    turned = [pltpu.roll(parts[FIELDS], sites - f * spare, 1) for f in range(FIELDS)]
-    return [jnp.where(lane < sites, parts[f], turned[f]) for f in range(FIELDS)]
+    return jnp.where(lane < spare, pltpu.roll(first, spare, 1), pltpu.roll(second, spare, 1))
 
 
 def unmerge(parts, lane, sites):
-    spare = LANES - sites
-    last = pltpu.roll(parts[FIELDS - 1], FIELDS * spare, 1)
-    for f in reversed(range(FIELDS - 1)):
-        last = jnp.where(lane < (f + 1) * spare, pltpu.roll(parts[f], (f + 1) * spare, 1), last)
-    return list(parts) + [last]
+    rest = 2 * sites - LANES
+    first, second, third = parts
+    kept = LANES - rest
+    col_imag = jnp.where(
+        lane < kept, pltpu.roll(second, kept, 1), pltpu.roll(third, 2 * LANES - sites - rest, 1)
+    )
+    return first, imaginary(first, second, lane, sites), third, col_imag
 
 
 def pack_kernel(
@@ -68,6 +80,7 @@
     send_ref,
     quanta_ref,
     slot_ref,
+    table_ref,
     sems,
     table_sems,
     wire_sems,
@@ -88,7 +101,9 @@
         [(send_hbm, send_ref), (quanta_hbm, quanta_ref), (slot_hbm, slot_ref)], table_sems
     )
     lane = lane_index((SUB, LANES))
-    store_ref[:, pl.ds(rows, LANES - sites), :] = jnp.zeros((4, LANES - sites, LANES), jnp.float32)
+    rest = 2 * sites - LANES
+    store_ref[pl.ds(2, 2)] = jnp.zeros((2,) + store_ref.shape[1:], jnp.float32)
+    table_ref[...] = jnp.zeros_like(table_ref)
     for block in range(pair_blocks):
         copies[block].wait()
         for a in range(aux):
@@ -96,48 +111,63 @@
                 state_ref[pl.ds(a + aux * (tiles * SUB * block + u), SUB, stride=aux * tiles), :]
                 for u in range(tiles)
             )
-            even_imag = jnp.where(lane < 32, pltpu.roll(first, 32, 1), pltpu.roll(middle, 32, 1))
-            odd_real = jnp.where(lane < 64, pltpu.roll(middle, 64, 1), pltpu.roll(last, 64, 1))
-            odd_imag = pltpu.roll(last, 96, 1)
+            middle_turned = pltpu.roll(middle, rest, 1)
+            last_turned = pltpu.roll(last, rest, 1)
             base = a * sites + 2 * SUB * block
             store_ref[0, pl.ds(base, SUB, stride=2), :] = first
-            store_ref[1, pl.ds(base, SUB, stride=2), :] = even_imag
-            store_ref[0, pl.ds(base + 1, SUB, stride=2), :] = odd_real
-            store_ref[1, pl.ds(base + 1, SUB, stride=2), :] = odd_imag
-    for a in range(aux):
-        for c in range(2):
-            block = store_ref[c, pl.ds(a * sites, LANES), :]
-            store_ref[2 + c, pl.ds(a * sites, sites), :] = block.T[:sites, :]
+            store_ref[1, pl.ds(base, SUB, stride=2), :] = middle
+            store_ref[0, pl.ds(base + 1, SUB, stride=2), :] = jnp.where(
+                lane < rest, middle_turned, last_turned
+            )
+            store_ref[1, pl.ds(base + 1, SUB, stride=2), :] = last_turned
     for table in tables:
         table.wait()
     band = band_ref[0]
     row_lane = lane_index((1, LANES))
+    entry = send_ref[...]
+    lane_count = entry.shape[1]
+    site = jnp.full(entry.shape, -1, jnp.int32)
+    base = jnp.zeros(entry.shape, jnp.int32)
+    for source in range(aux):
+        for place in range(depth):
+            here = entry == source * depth + place
+            site = jnp.where(here, quanta_ref[place, source], site)
+            base = jnp.where(here, source * sites, base)
+    group = (lane_index(entry.shape) >= peers * capacity).astype(jnp.int32)
+    usable = (entry >= 0) & (site >= 0) & (band - group >= 0)
+    site = jnp.maximum(site, 0)
+    table_ref[0, :, pl.ds(0, lane_count)] = base + site
+    table_ref[1, :, pl.ds(0, lane_count)] = jnp.where(usable, slot_ref[...] * sites, rows)
+    table_ref[2, :, pl.ds(0, lane_count)] = jnp.where(usable, site, 0)
+    slot_tags, site_tags = table_ref[1], table_ref[2]
+    for g in range(2):
+        for q in range(peers):
+            at = (g * peers + q) * capacity
+            tags = jnp.where(
+                row_lane < TAG,
+                pltpu.roll(slot_tags, (LANES - at) % LANES, 1),
+                pltpu.roll(site_tags, (LANES + TAG - at) % LANES, 1),
+            )
+            payload_ref[g, q, :, pl.ds(capacity * FIELDS * LANES, LANES)] = tags.astype(jnp.float32)
+    for a in range(aux):
+        here = pl.ds(a * sites, sites)
+        turned = store_ref[0, here, :].T
+        store_ref[2, here, pl.ds(0, sites)] = turned[:sites, :]
+        store_ref[3, pl.ds(a * sites, LANES - sites), pl.ds(0, sites)] = turned[sites:, :]
+        turned = store_ref[1, here, :].T
+        store_ref[3, pl.ds(a * sites + LANES - sites, rest), pl.ds(0, sites)] = turned[:rest, :]
     block = send_blocks(payload_ref, payload_hbm, wire_sems, band, -1, tiers, peers)
     for g in (1, 0):
-        inside = band - g >= 0
         for q in range(peers):
-            tags = jnp.zeros((1, LANES), jnp.int32)
             for j in range(capacity):
-                l = (g * peers + q) * capacity + j
-                entry = send_ref[0, l]
-                clipped = jnp.maximum(entry, 0)
-                source = clipped // depth
-                site = quanta_ref[clipped % depth, source]
-                usable = (entry >= 0) & (site >= 0) & inside
-                site = jnp.maximum(site, 0)
-                row = pl.ds(source * sites + site, 1)
-                tags = jnp.where(
-                    row_lane == 2 * j, jnp.where(usable, slot_ref[0, l] * sites, rows), tags
-                )
-                tags = jnp.where(row_lane == 2 * j + 1, jnp.where(usable, site, 0), tags)
+                row = pl.ds(table_ref[0, 0, (g * peers + q) * capacity + j], 1)
                 fields = merge([store_ref[f, row, :] for f in range(4)], row_lane, sites)
                 for f in range(FIELDS):
                     payload_ref[g, q, :, pl.ds((j * FIELDS + f) * LANES, LANES)] = fields[f]
-            payload_ref[g, q, :, pl.ds(capacity * FIELDS * LANES, LANES)] = tags.astype(jnp.float32)
         if g == 0:
             block(g).start()
         else:
-            pl.when(inside)(block(g).start)
+            pl.when(band >= g)(block(g).start)
     block(0).wait()
     pl.when(band >= 1)(block(1).wait)
 
@@ -163,22 +193,22 @@
 
 def tag_row(tag_ref, g, p, j, peers):
     at = g * peers + p
-    return tag_ref[at, 0, 2 * j].astype(jnp.int32) + tag_ref[at, 0, 2 * j + 1].astype(jnp.int32)
-
-
-def answer_kernel(
-    sizes, band_ref, arrived_ref, store_ref, reply_hbm, reply_ref, tag_ref, sems, wire_sems
-):
+    return tag_ref[at, 0, j].astype(jnp.int32) + tag_ref[at, 0, TAG + j].astype(jnp.int32)
+
+
+def answer_kernel(sizes, band_ref, arrived_ref, store_ref, reply_hbm, reply_ref, row_ref, wire_sems):
     sites, aux, depth, peers, capacity, tiers = sizes
     band = band_ref[0]
-    copies = read_tags(sizes, band, arrived_ref, tag_ref, sems)
     block = send_blocks(reply_ref, reply_hbm, wire_sems, band, 1, tiers, peers)
-    for copy in copies:
-        copy.wait()
+    for g in (1, 0):
+        origin = jnp.minimum(band + g, tiers - 1)
+        for p in range(peers):
+            tags = arrived_ref[origin * peers + p, :, pl.ds(capacity * FIELDS * LANES, LANES)]
+            row_ref[g * peers + p] = (tags + pltpu.roll(tags, TAG, 1)).astype(jnp.int32)
     for g in (1, 0):
         for p in range(peers):
             for j in range(capacity):
-                row = pl.ds(tag_row(tag_ref, g, p, j, peers), 1)
+                row = pl.ds(row_ref[g * peers + p, 0, j], 1)
                 for f in range(FIELDS):
                     reply_ref[g, p, :, pl.ds((j * FIELDS + f) * LANES, LANES)] = store_ref[f, row, :]
         if g == 0:
@@ -233,9 +263,12 @@
     coupling = coupling_ref[...]
     hamilton = (coupling + coupling.T) * 0.5 + jnp.where(row_ids == col_ids, energy_ref[...], 0.0)
     matrix_ref[...] = jnp.zeros_like(matrix_ref)
-    matrix_ref[pl.ds(0, sites), pl.ds(LANES, sites)] = hamilton
-    matrix_ref[pl.ds(LANES, sites), pl.ds(0, sites)] = -hamilton
-    high, low = split(matrix_ref[...])
+    splits = []
+    for half, start in enumerate((sites, LANES)):
+        matrix_ref[half, pl.ds(0, sites), pl.ds(LANES, sites)] = hamilton
+        matrix_ref[half, pl.ds(start, sites), pl.ds(0, sites)] = -hamilton
+        splits.append(split(matrix_ref[half]))
+    lane = lane_index((sites, LANES))
     dot = functools.partial(jnp.dot, preferred_element_type=jnp.float32)
     saves = []
     for a in range(aux):
@@ -246,17 +279,19 @@
             damp = damp + jnp.where(site >= 0, rate, 0.0)
         here = pl.ds(a * sites, sites)
         for half in range(2):
-            real, imag = store_ref[2 * half, here, :], store_ref[2 * half + 1, here, :]
-            both = jnp.concatenate([real, imag], axis=1)
+            high, low = splits[half]
+            first, second = store_ref[2 * half, here, :], store_ref[2 * half + 1, here, :]
+            both = jnp.concatenate([first, second], axis=1)
             both_high, both_low = split(both)
             product = dot(both_high, high) + (dot(both_low, high) + dot(both_high, low))
             if half == 0:
-                product = product - damp * both
+                imag = imaginary(first, second, lane, sites)
+                product = product - damp * jnp.concatenate([first, imag], axis=1)
             else:
                 product = -product
             acc_ref[2 * half, here, :] = product[:, :LANES]
             acc_ref[2 * half + 1, here, :] = product[:, LANES:]
-        fields = merge([store_ref[f, here, :] for f in range(4)], lane_index((sites, LANES)), sites)
+        fields = merge([store_ref[f, here, :] for f in range(4)], lane, sites)
         for f in range(FIELDS):
             merged_ref[f, here, :] = fields[f]
         saves.append(
@@ -549,13 +584,14 @@
             (HBM, dest_slot),
             (HBM, tiled),
         ],
-        [(VMEM, store_shape, f32), (HBM, payload_shape, f32)],
+        [(VMEM, acc_shape, f32), (HBM, payload_shape, f32)],
         [
             VMEM(flat_shape, f32),
             VMEM((2, peers) + payload_shape[1:], f32),
-            send_table,
+            VMEM(send_list.shape, jnp.int32),
             quanta_table,
-            send_table,
+            VMEM(dest_slot.shape, jnp.int32),
+            VMEM((3, 1, LANES), jnp.int32),
             dma((pair_blocks,)),
             dma((3,)),
             dma((2,)),
@@ -576,7 +612,7 @@
         [(HBM, acc_shape, f32), (VMEM, (FIELDS, padded, LANES), f32)],
         [
             VMEM(acc_shape, f32),
-            VMEM((2 * LANES, 2 * LANES), f32),
+            VMEM((2, 2 * LANES, 2 * LANES), f32),
             VMEM(coupling.shape, f32),
             VMEM(rate_row.shape, f32),
             quanta_table,
@@ -591,7 +627,11 @@
         "answer",
         [(SMEM, band), (VMEM, arrived), (VMEM, merged)],
         [(HBM, reply_shape, f32)],
-        [VMEM((2, peers) + reply_shape[1:], f32)] + tag_scratch + [dma((2,))],
+        [
+            VMEM((2, peers) + reply_shape[1:], f32),
+            VMEM((2 * peers, 1, LANES), jnp.int32),
+            dma((2,)),
+        ],
     )
     returned = trade(reply)
     total, columns, places, coefs = call(

time: 33.4 us -> 34.2 us (1.024)
  Pallas kernels: 12.3 us -> 13.1 us
    pallas_call x5, Pallas kernels: 12.3 us -> 13.1 us  [call(): pl.pallas_call(functools.partial(kernel, sizes), out_shape=[space(shape,...]
  transfers between devices with their start and end apart: 2 -> 2, of which waited for: 2 -> 2; matrix products, arithmetic and copies ran while one was open for 0% -> 0% of each run, Pallas kernels for 19% -> 18%
where the time goes in v4:
time: 34.2 us; the launch traced here: 33.9 us
  Pallas kernels  13.1 us (38%)
  waiting for transfers between devices  10.8 us (32%)
  starting transfers between devices  9.93 us (29%)
    pallas_call x5, Pallas kernels, call(): pl.pallas_call(functools.partial(kernel, sizes), out_shape=[space(shape,...  13.1 us
    all_to_all x1, starting transfers between devices, on_device(): arrived = trade(payload)  7.33 us
    all_to_all x1, waiting for transfers between devices, on_device(): arrived = trade(payload)  5.75 us
    all_to_all x1, waiting for transfers between devices, on_device(): returned = trade(reply)  5.06 us
    all_to_all x1, starting transfers between devices, on_device(): returned = trade(reply)  2.59 us
  transfers between devices with their start and end apart: 2, of which 2 were waited for; matrix products, arithmetic and copies ran while one was open for 0% of the time, Pallas kernels for 18%

profile of v4, /device:TPU:0, one launch (start us, length us, event | category | flops | bytes accessed | tf_op | source)
XLA Modules:
  0.0 33.9 jit_solution(3262026290897834256)
XLA Ops:
  0.0 4.5 %pack.1 = (f32[4,768,128]{2,1,0:T(8,128)S(1)}, f32[32,1,1280]{2,1,0:T(1,128)}) custom-call(s32[1]{0:T(128)} %bitcast.band_ref, s32[1,48]{1,0:T(1,128)} %send_hbm.3, s32[4,8]{1,0:T(4,128)} %bitcast.19, s32[1,48]{1,0:T(1,128)} %slot_hbm.1, f32[1152,128]{1,0:T(8,128)} %bitcast.18), custom_call_target="tpu_custom_call" | custom-call | tf_op jit(solution)/shard_map/pack/pallas_call | solution.py:552
  4.5 7.3 %all-to-all-start = ((f32[32,1,1280]{2,1,0:T(1,128)}), f32[32,1,1280]{2,1,0:T(1,128)S(1)}, u32[]{:S(2)}, u32[]{:S(2)}) async-start(f32[32,1,1280]{2,1,0:T(1,128)} %get-tuple-element.13), calls=%async_computation | async-start | bytes 327680 | tf_op jit(solution)/shard_map/all_to_all | solution.py:600
  11.8 2.9 %local.1 = (f32[4,768,128]{2,1,0:T(8,128)}, f32[3,800,128]{2,1,0:T(8,128)S(1)}) custom-call(s32[4,8]{1,0:T(4,128)} %bitcast.20, s32[1,96]{1,0:T(1,128)} %bitcast.22, f32[1,96]{1,0:T(1,128)} %bitcast.24, f32[96,96]{1,0:T(8,128)} %coupling_hbm.1, f32[1,96]{1,0:T(1,128)} %bitcast.27, f32[4,768,128]{2,1,0:T(8,128)S(1)} %get-tuple-element.14.store_ref), custom_call_target="tpu_custom_call" | custom-call | tf_op jit(solution)/shard_map/local/pallas_call | solution.py:552
  14.7 5.7 %all-to-all-done.arrived_ref = f32[32,1,1280]{2,1,0:T(1,128)S(1)} async-done(((f32[32,1,1280]{2,1,0:T(1,128)}), f32[32,1,1280]{2,1,0:T(1,128)S(1)}, u32[]{:S(2)}, u32[]{:S(2)}) %all-to-all-start) | async-done | bytes 163872 | tf_op jit(solution)/shard_map/all_to_all | solution.py:600
  20.4 0.9 %answer.1 = f32[32,1,1152]{2,1,0:T(1,128)} custom-call(s32[1]{0:T(128)} %bitcast.band_ref, f32[32,1,1280]{2,1,0:T(1,128)S(1)} %all-to-all-done.arrived_ref, f32[3,800,128]{2,1,0:T(8,128)S(1)} %get-tuple-element.15.store_ref), custom_call_target="tpu_custom_call" | custom-call | tf_op jit(solution)/shard_map/answer/pallas_call | solution.py:552
  21.4 2.6 %all-to-all-start.1 = ((f32[32,1,1152]{2,1,0:T(1,128)}), f32[32,1,1152]{2,1,0:T(1,128)S(1)}, u32[]{:S(2)}, u32[]{:S(2)}) async-start(f32[32,1,1152]{2,1,0:T(1,128)} %answer.1), calls=%async_computation.1 | async-start | bytes 294912 | tf_op jit(solution)/shard_map/all_to_all | solution.py:636
  24.0 3.3 %raise.1 = (f32[2,768,128]{2,1,0:T(8,128)S(1)}, bf16[128,1024]{1,0:T(8,128)(2,1)S(1)}, bf16[768,128]{1,0:T(8,128)(2,1)S(1)}, f32[2,48,128]{2,1,0:T(8,128)S(1)}) custom-call(s32[1]{0:T(128)} %bitcast.band_ref, s32[1,48]{1,0:T(1,128)} %send_hbm.3, s32[4,8]{1,0:T(4,128)} %bitcast.21, s32[1,96]{1,0:T(1,128)} %bitcast.23, f32[1,96]{1,0:T(1,128)} %bitcast.25, ...), custom_call_target="tpu_custom_call" | custom-call | tf_op jit(solution)/shard_map/raise/pallas_call | solution.py:552
  27.3 5.1 %all-to-all-done.1 = f32[32,1,1152]{2,1,0:T(1,128)S(1)} async-done(((f32[32,1,1152]{2,1,0:T(1,128)}), f32[32,1,1152]{2,1,0:T(1,128)S(1)}, u32[]{:S(2)}, u32[]{:S(2)}) %all-to-all-start.1) | async-done | bytes 147488 | tf_op jit(solution)/shard_map/all_to_all | solution.py:636
  32.4 1.5 %lower.1 = f32[1152,128]{1,0:T(8,128)} custom-call(s32[1]{0:T(128)} %bitcast.band_ref, f32[288,128]{1,0:T(8,128)S(1)} %bitcast.17, f32[2,768,128]{2,1,0:T(8,128)S(1)} %get-tuple-element.17.sum_ref, bf16[128,1024]{1,0:T(8,128)(2,1)S(1)} %get-tuple-element.18.column_ref, bf16[768,128]{1,0:T(8,128)(2,1)S(1)} %get-tuple-element.19.place_ref, ...), custom_call_target="tpu_custom_call" | custom-call | tf_op jit(solution)/shard_map/lower/pallas_call | solution.py:552
Async XLA Ops:
  4.5 16.0 %all-to-all-start = ((f32[32,1,1280]{2,1,0:T(1,128)}), f32[32,1,1280]{2,1,0:T(1,128)S(1)}, u32[]{:S(2)}, u32[]{:S(2)}) async-start(f32[32,1,1280]{2,1,0:T(1,128)} %get-tuple-element.13), calls=%async_computation | async-start | bytes 327680 | tf_op jit(solution)/shard_map/all_to_all | solution.py:600
  21.4 11.0 %all-to-all-start.1 = ((f32[32,1,1152]{2,1,0:T(1,128)}), f32[32,1,1152]{2,1,0:T(1,128)S(1)}, u32[]{:S(2)}, u32[]{:S(2)}) async-start(f32[32,1,1152]{2,1,0:T(1,128)} %answer.1), calls=%async_computation.1 | async-start | bytes 294912 | tf_op jit(solution)/shard_map/all_to_all | solution.py:636

commit v5 on v4

v5 whole, which is shorter than its diff:
```python
import functools

import jax
import jax.numpy as jnp
from jax import lax
from jax.experimental import pallas as pl
from jax.experimental.pallas import tpu as pltpu
from jax.sharding import PartitionSpec as P

thermal = 0.5
LANES = 128
SUB = 8
FIELDS = 3
TAG = 64
VMEM = pltpu.VMEM
SMEM = pltpu.SMEM


def spec(space):
    return pl.BlockSpec(memory_space=space)


def lane_index(shape):
    return lax.broadcasted_iota(jnp.int32, shape, 1)


def fetch(pairs, sems):
    copies = [
        pltpu.make_async_copy(source, target, sems.at[n]) for n, (source, target) in enumerate(pairs)
    ]
    for copy in copies:
        copy.start()
    return copies


def send_blocks(work_ref, wire_hbm, sems, band, step, tiers, peers):
    def block(g):
        at = jnp.clip(band + g * step, 0, tiers - 1) * peers
        return pltpu.make_async_copy(work_ref.at[g], wire_hbm.at[pl.ds(at, peers)], sems.at[g])

    return block


def imaginary(first, second, lane, sites):
    spare = LANES - sites
    return jnp.where(lane < spare, pltpu.roll(first, spare, 1), pltpu.roll(second, spare, 1))


def unmerge(parts, lane, sites):
    rest = 2 * sites - LANES
    first, second, third = parts
    kept = LANES - rest
    col_imag = jnp.where(
        lane < kept, pltpu.roll(second, kept, 1), pltpu.roll(third, 2 * LANES - sites - rest, 1)
    )
    return first, imaginary(first, second, lane, sites), third, col_imag


def pack_kernel(
    sizes,
    band_ref,
    send_hbm,
    quanta_hbm,
    slot_hbm,
    state_hbm,
    store_ref,
    payload_ref,
    state_ref,
    send_ref,
    quanta_ref,
    slot_ref,
    table_ref,
    row_ref,
    sems,
    table_sems,
):
    sites, aux, depth, peers, capacity, tiers = sizes
    tiles = 4 * sites // LANES
    pair_blocks = sites // (2 * SUB)
    chunk = aux * tiles * SUB
    rows = aux * sites
    tables = fetch(
        [(send_hbm, send_ref), (quanta_hbm, quanta_ref), (slot_hbm, slot_ref)], table_sems
    )
    copies = fetch(
        [
            (state_hbm.at[pl.ds(b * chunk, chunk), :], state_ref.at[pl.ds(b * chunk, chunk), :])
            for b in range(pair_blocks)
        ],
        sems,
    )
    lane = lane_index((SUB, LANES))
    rest = 2 * sites - LANES
    store_ref[:, pl.ds(rows, LANES - sites), :] = jnp.zeros(
        (FIELDS, LANES - sites, LANES), jnp.float32
    )
    table_ref[...] = jnp.zeros_like(table_ref)
    for table in tables:
        table.wait()
    band = band_ref[0]
    row_lane = lane_index((1, LANES))
    entry = send_ref[...]
    lane_count = entry.shape[1]
    site = jnp.full(entry.shape, -1, jnp.int32)
    base = jnp.zeros(entry.shape, jnp.int32)
    for source in range(aux):
        for place in range(depth):
            here = entry == source * depth + place
            site = jnp.where(here, quanta_ref[place, source], site)
            base = jnp.where(here, source * sites, base)
    group = (lane_index(entry.shape) >= peers * capacity).astype(jnp.int32)
    usable = (entry >= 0) & (site >= 0) & (band - group >= 0)
    site = jnp.maximum(site, 0)
    table_ref[0, :, pl.ds(0, lane_count)] = base + site
    table_ref[1, :, pl.ds(0, lane_count)] = jnp.where(usable, slot_ref[...] * sites, rows)
    table_ref[2, :, pl.ds(0, lane_count)] = jnp.where(usable, site, 0)
    slot_tags, site_tags = table_ref[1], table_ref[2]
    for g in (1, 0):
        for q in range(peers):
            at = (g * peers + q) * capacity
            tags = jnp.where(
                row_lane < TAG,
                pltpu.roll(slot_tags, (LANES - at) % LANES, 1),
                pltpu.roll(site_tags, (LANES + TAG - at) % LANES, 1),
            )
            at_row = jnp.maximum(band - g, 0) * peers + q
            payload_ref[at_row, :, pl.ds(capacity * FIELDS * LANES, LANES)] = tags.astype(
                jnp.float32
            )
    for l in range(lane_count):
        row_ref[l] = table_ref[0, 0, l]
    for block in range(pair_blocks):
        copies[block].wait()
        for a in range(aux):
            first, middle, last = (
                state_ref[pl.ds(a + aux * (tiles * SUB * block + u), SUB, stride=aux * tiles), :]
                for u in range(tiles)
            )
            middle_turned = pltpu.roll(middle, rest, 1)
            last_turned = pltpu.roll(last, rest, 1)
            base = a * sites + 2 * SUB * block
            store_ref[0, pl.ds(base, SUB, stride=2), :] = first
            store_ref[1, pl.ds(base, SUB, stride=2), :] = middle
            store_ref[0, pl.ds(base + 1, SUB, stride=2), :] = jnp.where(
                lane < rest, middle_turned, last_turned
            )
            store_ref[1, pl.ds(base + 1, SUB, stride=2), :] = last_turned
    for a in range(aux):
        here = pl.ds(a * sites, sites)
        first = store_ref[0, here, :].T
        second = store_ref[1, here, :].T
        col_imag = jnp.concatenate([first[sites:, :], second[:rest, :]], axis=0)
        store_ref[2, here, pl.ds(0, sites)] = first[:sites, :]
        store_ref[1, here, pl.ds(rest, LANES - rest)] = col_imag[:, : LANES - rest]
        store_ref[2, here, pl.ds(sites, LANES - sites)] = col_imag[:, LANES - rest :]
    for g in (1, 0):
        for q in range(peers):
            at_row = jnp.maximum(band - g, 0) * peers + q
            for j in range(capacity):
                row = pl.ds(row_ref[(g * peers + q) * capacity + j], 1)
                for f in range(FIELDS):
                    payload_ref[at_row, :, pl.ds((j * FIELDS + f) * LANES, LANES)] = store_ref[
                        f, row, :
                    ]


def read_rows(sizes, band, arrived_ref, row_ref):
    sites, aux, depth, peers, capacity, tiers = sizes
    slabs = capacity * FIELDS + 1
    for g in range(2):
        origin = jnp.minimum(band + g, tiers - 1) * peers
        for p in range(peers):
            tags = arrived_ref[pl.ds((origin + p) * slabs + slabs - 1, 1), :]
            total = (tags + pltpu.roll(tags, TAG, 1)).astype(jnp.int32)
            row_ref[g * peers + p] = jnp.where(band + g < tiers, total, aux * sites)


def answer_kernel(sizes, band_ref, arrived_ref, store_ref, reply_hbm, reply_ref, row_ref, wire_sems):
    sites, aux, depth, peers, capacity, tiers = sizes
    band = band_ref[0]
    block = send_blocks(reply_ref, reply_hbm, wire_sems, band, 1, tiers, peers)
    read_rows(sizes, band, arrived_ref, row_ref)
    for g in (1, 0):
        for p in range(peers):
            for j in range(capacity):
                row = pl.ds(row_ref[g * peers + p, 0, j], 1)
                for f in range(FIELDS):
                    reply_ref[g, p, :, pl.ds((j * FIELDS + f) * LANES, LANES)] = store_ref[f, row, :]
        if g == 0:
            block(g).start()
        else:
            pl.when(band + g < tiers)(block(g).start)
    block(0).wait()
    pl.when(band + 1 < tiers)(block(1).wait)


def split(value):
    high = value.astype(jnp.bfloat16)
    low = (value - high.astype(jnp.float32)).astype(jnp.bfloat16)
    return high, low


def spread(row):
    return jnp.broadcast_to(row, (row.shape[1], row.shape[1])).T


def middle_kernel(
    sizes,
    band_ref,
    send_hbm,
    quanta_hbm,
    bath_hbm,
    rate_hbm,
    strength_hbm,
    coupling_hbm,
    energy_hbm,
    arrived_ref,
    store_ref,
    sum_ref,
    column_ref,
    place_ref,
    coef_ref,
    work_ref,
    matrix_ref,
    edge_ref,
    row_ref,
    coupling_ref,
    vector_ref,
    send_ref,
    bath_row,
    quanta_ref,
    bath_ref,
    rate_ref,
    index_ref,
    sems,
):
    sites, aux, depth, peers, capacity, tiers = sizes
    rows = aux * sites
    rest = 2 * sites - LANES
    f32 = jnp.float32
    band = band_ref[0]
    copies = fetch(
        [
            (coupling_hbm, coupling_ref),
            (energy_hbm, vector_ref.at[0]),
            (rate_hbm, vector_ref.at[1]),
            (strength_hbm, vector_ref.at[2]),
            (send_hbm, send_ref),
            (bath_hbm, bath_row),
            (quanta_hbm, quanta_ref),
            (bath_hbm, bath_ref),
            (rate_hbm, rate_ref),
        ],
        sems,
    )
    read_rows(sizes, band, arrived_ref, row_ref)
    lane = lane_index((peers, LANES))
    for g in range(2):
        origin = jnp.minimum(band + g, tiers - 1) * peers
        for j in range(capacity):
            slabs = capacity * FIELDS + 1
            parts = [
                arrived_ref[pl.ds(origin * slabs + j * FIELDS + f, peers, stride=slabs), :]
                for f in range(FIELDS)
            ]
            row_real, row_imag, col_real, col_imag = unmerge(parts, lane, sites)
            for f, value in enumerate((row_imag, -row_real, -col_imag, col_real)):
                edge_ref[f, pl.ds(g * peers * capacity + j, peers, stride=capacity), :] = value
    matrix_ref[...] = jnp.zeros_like(matrix_ref)
    index_ref[...] = jnp.full(index_ref.shape, -1.0, f32)
    work_ref[:, pl.ds(rows, LANES - sites), :] = jnp.zeros((4, LANES - sites, LANES), f32)
    for copy in copies:
        copy.wait()
    row_ids = lax.broadcasted_iota(jnp.int32, (sites, sites), 0)
    col_ids = lane_index((sites, sites))
    coupling = coupling_ref[...]
    hamilton = (coupling + coupling.T) * 0.5 + jnp.where(row_ids == col_ids, vector_ref[0], 0.0)
    real, imag = pl.ds(0, sites), pl.ds(LANES, sites)
    matrix_ref[0, real, imag] = hamilton
    matrix_ref[0, pl.ds(sites, sites), real] = -hamilton
    matrix_ref[1, pl.ds(LANES, sites), imag] = -hamilton
    matrix_ref[1, pl.ds(rest, LANES - rest), real] = hamilton[: LANES - rest, :]
    matrix_ref[1, pl.ds(LANES + sites, LANES - sites), real] = hamilton[LANES - rest :, :]
    dot = functools.partial(jnp.dot, preferred_element_type=f32)
    splits = [split(matrix_ref[half]) for half in range(2)]
    lane = lane_index((sites, LANES))
    for a in range(aux):
        damp = f32(0.0)
        for place in range(depth):
            site = quanta_ref[place, a]
            rate = rate_ref[0, bath_ref[0, jnp.maximum(site, 0)]]
            damp = damp + jnp.where(site >= 0, rate, 0.0)
        here = pl.ds(a * sites, sites)
        for half in range(2):
            high, low = splits[half]
            first, second = store_ref[half, here, :], store_ref[half + 1, here, :]
            both_high, both_low = split(jnp.concatenate([first, second], axis=1))
            product = dot(both_high, high) + (dot(both_low, high) + dot(both_high, low))
            pair = [product[:, :LANES], product[:, LANES:]]
            if half == 0:
                pair[0] = pair[0] - damp * first
                pair[1] = pair[1] - damp * imaginary(first, second, lane, sites)
            for c in range(2):
                work_ref[2 * half + c, here, :] = pair[c]

    entry = send_ref[...]
    lane_count = entry.shape[1]
    half = index_ref.shape[2] // 2
    site = jnp.full(entry.shape, -1, jnp.int32)
    source = jnp.zeros(entry.shape, jnp.int32)
    for a in range(aux):
        for place in range(depth):
            hit = entry == a * depth + place
            site = jnp.where(hit, quanta_ref[place, a], site)
            source = jnp.where(hit, a, source)
    weight = jnp.zeros(entry.shape, f32)
    for a in range(aux):
        for place in range(depth):
            hit = (source == a) & (site == quanta_ref[place, a])
            weight = weight + jnp.where(hit, 1.0, 0.0)
    group = (lane_index(entry.shape) >= peers * capacity).astype(jnp.int32)
    usable = (entry >= 0) & (site >= 0) & (band - group >= 0)
    weight = jnp.where(usable, weight, 0.0)
    bath_of = spread(bath_row[...].astype(f32)) == col_ids.astype(f32)
    rate_of = jnp.sum(jnp.where(bath_of, vector_ref[1], 0.0), axis=1, keepdims=True)
    strength_of = jnp.sum(jnp.where(bath_of, vector_ref[2], 0.0), axis=1, keepdims=True)
    at_site = lax.broadcasted_iota(jnp.int32, (sites, lane_count), 0) == site
    rate = jnp.sum(jnp.where(at_site, rate_of, 0.0), axis=0, keepdims=True)
    strength = jnp.sum(jnp.where(at_site, strength_of, 0.0), axis=0, keepdims=True)
    lanes = pl.ds(0, lane_count)
    index_ref[2, :, lanes] = -weight * (strength * rate)
    index_ref[3, :, lanes] = weight * (2.0 * thermal * strength)
    for c in range(2):
        coef_ref[c] = spread(index_ref[2 + c, :, pl.ds(0, LANES)])[:lane_count, :]
    row_index = jnp.where(usable, source * sites + site, -1).astype(f32)
    column_index = jnp.where(usable, source * LANES + site, -1).astype(f32)
    for start in (0, half):
        index_ref[0, :, pl.ds(start, lane_count)] = row_index
        index_ref[1, :, pl.ds(start, lane_count)] = column_index
    for slab in range(2 * half // LANES):
        part = pl.ds(slab * LANES, LANES)
        turned = spread(index_ref[1, :, part])
        row_index = index_ref[0, :, part]
        for a in range(aux):
            at = (lane_index((LANES, LANES)) + a * LANES).astype(f32)
            column_ref[part, pl.ds(a * LANES, LANES)] = jnp.where(turned == at, 1.0, 0.0).astype(
                jnp.bfloat16
            )
            at = (lax.broadcasted_iota(jnp.int32, (sites, LANES), 0) + a * sites).astype(f32)
            place_ref[pl.ds(a * sites, sites), part] = jnp.where(row_index == at, 1.0, 0.0).astype(
                jnp.bfloat16
            )

    for g in range(2):
        for p in range(peers):
            for j in range(capacity):
                l = (g * peers + p) * capacity + j
                row = pl.ds(row_ref[g * peers + p, 0, j], 1)
                for c in range(4):
                    work_ref[c, row, :] = work_ref[c, row, :] + edge_ref[c, pl.ds(l, 1), :]
    for a in range(aux):
        here = pl.ds(a * sites, sites)
        for c in range(2):
            turned = work_ref[2 + c, pl.ds(a * sites, LANES), :].T[:sites, :]
            sum_ref[c, here, :] = work_ref[c, here, :] + turned


def lower_kernel(
    sizes,
    band_ref,
    returned_ref,
    sum_ref,
    column_ref,
    place_ref,
    coef_ref,
    out_hbm,
    work_ref,
    edge_ref,
    out_ref,
    sems,
):
    sites, aux, depth, peers, capacity, tiers = sizes
    tiles = 4 * sites // LANES
    pair_blocks = sites // (2 * SUB)
    chunk = aux * tiles * SUB
    slabs = capacity * FIELDS
    used = 2 * capacity * peers
    half = edge_ref.shape[1] // 2
    band = band_ref[0]
    lane = lane_index((peers, LANES))
    if used < half:
        for top in (used, half + used):
            edge_ref[:, pl.ds(top, half - used), :] = jnp.zeros(
                (4, half - used, LANES), jnp.float32
            )
    for g in range(2):
        target = jnp.maximum(band - g, 0)
        for j in range(capacity):
            start = target * (peers * slabs) + j * FIELDS
            parts = [
                returned_ref[pl.ds(start + f, peers, stride=slabs), :] for f in range(FIELDS)
            ]
            row_real, row_imag, col_real, col_imag = unmerge(parts, lane, sites)
            base = g * peers * capacity + j
            shared = coef_ref[0, pl.ds(base, peers, stride=capacity), :]
            turn = coef_ref[1, pl.ds(base, peers, stride=capacity), :]
            values = (
                shared * row_real + turn * row_imag,
                shared * row_imag - turn * row_real,
                shared * col_real - turn * col_imag,
                shared * col_imag + turn * col_real,
            )
            for f, value in enumerate(values):
                high = value.astype(jnp.bfloat16).astype(jnp.float32)
                edge_ref[f, pl.ds(base, peers, stride=capacity), :] = high
                edge_ref[f, pl.ds(half + base, peers, stride=capacity), :] = value - high
    dot = functools.partial(jnp.dot, preferred_element_type=jnp.float32)
    row_data = jnp.concatenate([edge_ref[0], edge_ref[1]], axis=1).astype(jnp.bfloat16)
    col_data = jnp.concatenate([edge_ref[2].T, edge_ref[3].T], axis=0).astype(jnp.bfloat16)
    for pair in range(aux // 2):
        columns = dot(col_data, column_ref[:, pl.ds(2 * pair * LANES, 2 * LANES)])
        for o in range(2):
            here = pl.ds((2 * pair + o) * sites, sites)
            placed = dot(place_ref[here, :], row_data)
            for c in range(2):
                work_ref[c, here, :] = (
                    sum_ref[c, here, :]
                    + placed[:, c * LANES : (c + 1) * LANES]
                    + columns[c * LANES : c * LANES + sites, o * LANES : (o + 1) * LANES]
                )
    lane = lane_index((SUB, LANES))
    copies = []
    for block in range(pair_blocks):
        for a in range(aux):
            base = a * sites + 2 * SUB * block
            even_real, even_imag, odd_real, odd_imag = (
                work_ref[c, pl.ds(base + o, SUB, stride=2), :] for o in (0, 1) for c in (0, 1)
            )
            turned_imag = pltpu.roll(even_imag, 96, 1)
            turned_real = pltpu.roll(odd_real, 64, 1)
            parts = (
                jnp.where(lane < 96, even_real, turned_imag),
                jnp.where(lane < 64, turned_imag, turned_real),
                jnp.where(lane < 32, turned_real, pltpu.roll(odd_imag, 32, 1)),
            )
            for u in range(tiles):
                start = a + aux * (tiles * SUB * block + u)
                out_ref[pl.ds(start, SUB, stride=aux * tiles), :] = parts[u]
        here = pl.ds(block * chunk, chunk)
        copies.append(pltpu.make_async_copy(out_ref.at[here, :], out_hbm.at[here, :], sems.at[block]))
        copies[-1].start()
    for copy in copies:
        copy.wait()


def on_device(
    section_state,
    coupling,
    site_energy,
    bath_rate,
    bath_strength,
    bath_of_site,
    quanta,
    send_list,
    dest_slot,
):
    sites = coupling.shape[0]
    aux, flat = section_state.shape
    depth = quanta.shape[1]
    lane_count = send_list.shape[1]
    peers = lax.axis_size("aux")
    tiers = lax.axis_size("tier")
    capacity = lane_count // (2 * peers)
    sizes = (sites, aux, depth, peers, capacity, tiers)
    rows = aux * sites
    padded = rows + LANES - sites
    slabs = capacity * FIELDS
    chunks = flat // LANES
    half = -(-lane_count // 64) * 64
    f32 = jnp.float32
    bf16 = jnp.bfloat16
    band = lax.axis_index("tier").reshape(1)
    tiled = section_state.reshape(aux, chunks, LANES).transpose(1, 0, 2).reshape(-1, LANES)
    turned_quanta = quanta.T
    bath_row = bath_of_site.reshape(1, -1)
    rate_row = bath_rate.reshape(1, -1)
    strength_row = bath_strength.reshape(1, -1)
    pair_blocks = sites // (2 * SUB)

    def call(kernel, name, inputs, outs, scratch):
        spaces = [space for space, _ in inputs]
        values = [
            value if space is SMEM else pltpu.with_memory_space_constraint(value, space)
            for space, value in inputs
        ]
        return pl.pallas_call(
            functools.partial(kernel, sizes),
            out_shape=[space(shape, dtype) for space, shape, dtype in outs],
            in_specs=[spec(space) for space in spaces],
            out_specs=[spec(space) for space, _, _ in outs],
            scratch_shapes=scratch,
            name=name,
            compiler_params=pltpu.CompilerParams(vmem_limit_bytes=24 * 1024 * 1024),
        )(*values)

    HBM = pltpu.HBM
    dma = pltpu.SemaphoreType.DMA
    i32 = jnp.int32
    store_shape = (FIELDS, padded, LANES)
    reply_shape = (tiers * peers, 1, slabs * LANES)
    payload_shape = (tiers * peers, 1, (slabs + 1) * LANES)
    flat_shape = (aux * chunks, LANES)
    row_scratch = VMEM((2 * peers, 1, LANES), i32)
    trade = functools.partial(
        lax.all_to_all, axis_name=("tier", "aux"), split_axis=0, concat_axis=0, tiled=True
    )
    store, payload = call(
        pack_kernel,
        "pack",
        [(SMEM, band), (HBM, send_list), (HBM, turned_quanta), (HBM, dest_slot), (HBM, tiled)],
        [(VMEM, store_shape, f32), (VMEM, payload_shape, f32)],
        [
            VMEM(flat_shape, f32),
            VMEM(send_list.shape, i32),
            SMEM(turned_quanta.shape, i32),
            VMEM(dest_slot.shape, i32),
            VMEM((3, 1, LANES), i32),
            SMEM((lane_count,), i32),
            dma((pair_blocks,)),
            dma((3,)),
        ],
    )
    arrived = trade(payload).reshape(-1, LANES)
    (reply,) = call(
        answer_kernel,
        "answer",
        [(SMEM, band), (VMEM, arrived), (VMEM, store)],
        [(HBM, reply_shape, f32)],
        [VMEM((2, peers) + reply_shape[1:], f32), row_scratch, dma((2,))],
    )
    returned = trade(reply)
    total, columns, places, coefs = call(
        middle_kernel,
        "middle",
        [
            (SMEM, band),
            (HBM, send_list),
            (HBM, turned_quanta),
            (HBM, bath_row),
            (HBM, rate_row),
            (HBM, strength_row),
            (HBM, coupling),
            (HBM, site_energy.reshape(1, -1)),
            (VMEM, arrived),
            (VMEM, store),
        ],
        [
            (VMEM, (2, rows, LANES), f32),
            (VMEM, (2 * half, aux * LANES), bf16),
            (VMEM, (rows, 2 * half), bf16),
            (VMEM, (2, lane_count, LANES), f32),
        ],
        [
            VMEM((4, padded, LANES), f32),
            VMEM((2, 2 * LANES, 2 * LANES), f32),
            VMEM((4, lane_count, LANES), f32),
            row_scratch,
            VMEM(coupling.shape, f32),
            VMEM((3, 1, sites), f32),
            VMEM(send_list.shape, i32),
            VMEM(bath_row.shape, i32),
            SMEM(turned_quanta.shape, i32),
            SMEM(bath_row.shape, i32),
            SMEM(rate_row.shape, f32),
            VMEM((4, 1, 2 * half), f32),
            dma((9,)),
        ],
    )
    (out,) = call(
        lower_kernel,
        "lower",
        [
            (SMEM, band),
            (VMEM, returned.reshape(-1, LANES)),
            (VMEM, total),
            (VMEM, columns),
            (VMEM, places),
            (VMEM, coefs),
        ],
        [(HBM, flat_shape, f32)],
        [
            VMEM((2, rows, LANES), f32),
            VMEM((4, 2 * half, LANES), f32),
            VMEM(flat_shape, f32),
            dma((pair_blocks,)),
        ],
    )
    return out.reshape(chunks, aux, LANES).transpose(1, 0, 2).reshape(aux, flat)


def solution(mesh):
    return jax.shard_map(
        on_device,
        mesh=mesh,
        in_specs=(
            P(("tier", "aux"), None),
            P(),
            P(),
            P(),
            P(),
            P(),
            P(("tier", "aux"), None),
            P(("tier", "aux"), None),
            P(("tier", "aux"), None),
        ),
        out_specs=P(("tier", "aux"), None),
        check_vma=False,
    )
```

time: 34.2 us -> 31.8 us (0.930)
  blocking collectives: 0 us -> 15.8 us
  starting transfers between devices: 9.93 us -> 2.59 us
  Pallas kernels: 13.1 us -> 7.5 us
  waiting for transfers between devices: 10.8 us -> 5.66 us
    all_to_all x0 -> x1, blocking collectives: none -> 15.8 us  [on_device(): arrived = trade(payload).reshape(-1, LANES)]
    all_to_all x1 -> x0, starting transfers between devices: 7.33 us -> none  [on_device(): arrived = trade(payload)]
    all_to_all x1 -> x0, waiting for transfers between devices: 5.75 us -> none  [on_device(): arrived = trade(payload)]
    pallas_call x5 -> x4, Pallas kernels: 13.1 us -> 7.5 us  [call(): pl.pallas_call(functools.partial(kernel, sizes), out_shape=[space(shape,...]
    all_to_all x1, waiting for transfers between devices: 5.06 us -> 5.66 us  [on_device(): returned = trade(reply)]
  transfers between devices with their start and end apart: 2 -> 1, of which waited for: 2 -> 1; matrix products, arithmetic and copies ran while one was open for 0% -> 0% of each run, Pallas kernels for 18% -> 9%
where the time goes in v5:
time: 31.8 us; the launch traced here: 31.5 us
  blocking collectives  15.8 us (50%)
  Pallas kernels  7.5 us (24%)
  waiting for transfers between devices  5.66 us (18%)
  starting transfers between devices  2.59 us (8%)
    all_to_all x1, blocking collectives, on_device(): arrived = trade(payload).reshape(-1, LANES)  15.8 us
    pallas_call x4, Pallas kernels, call(): pl.pallas_call(functools.partial(kernel, sizes), out_shape=[space(shape,...  7.5 us
    all_to_all x1, waiting for transfers between devices, on_device(): returned = trade(reply)  5.66 us
    all_to_all x1, starting transfers between devices, on_device(): returned = trade(reply)  2.59 us
  transfers between devices with their start and end apart: 1, of which 1 were waited for; matrix products, arithmetic and copies ran while one was open for 0% of the time, Pallas kernels for 9%

profile of v5, /device:TPU:0, one launch (start us, length us, event | category | flops | bytes accessed | tf_op | source)
XLA Modules:
  0.0 31.5 jit_solution(9451647827031525129)
XLA Ops:
  0.0 2.3 %pack.1 = (f32[3,800,128]{2,1,0:T(8,128)S(1)}, f32[32,1,1280]{2,1,0:T(1,128)S(1)}) custom-call(s32[1]{0:T(128)} %bitcast.band_ref, s32[1,48]{1,0:T(1,128)} %send_hbm.3, s32[4,8]{1,0:T(4,128)} %bitcast.22, s32[1,48]{1,0:T(1,128)} %slot_hbm.1, f32[1152,128]{1,0:T(8,128)} %bitcast.21), custom_call_target="tpu_custom_call" | custom-call | tf_op jit(solution)/shard_map/pack/pallas_call | solution.py:496
  2.3 15.8 %all_to_all.10 = f32[32,1,1280]{2,1,0:T(1,128)S(1)} all-to-all(f32[32,1,1280]{2,1,0:T(1,128)S(1)} %get-tuple-element.11), channel_id=1, replica_groups=mesh['tier'=4,'aux'=8] {'tier','aux'}, dimensions={0} | all-to-all | bytes 327680 | tf_op jit(solution)/shard_map/all_to_all | solution.py:533
  18.1 0.9 %answer.1 = f32[32,1,1152]{2,1,0:T(1,128)} custom-call(s32[1]{0:T(128)} %bitcast.band_ref, f32[320,128]{1,0:T(8,128)S(1)} %bitcast.18, f32[3,800,128]{2,1,0:T(8,128)S(1)} %get-tuple-element.12.store_ref), custom_call_target="tpu_custom_call" | custom-call | tf_op jit(solution)/shard_map/answer/pallas_call | solution.py:496
  19.0 2.6 %all-to-all-start.1 = ((f32[32,1,1152]{2,1,0:T(1,128)}), f32[32,1,1152]{2,1,0:T(1,128)S(1)}, u32[]{:S(2)}, u32[]{:S(2)}) async-start(f32[32,1,1152]{2,1,0:T(1,128)} %answer.1), calls=%async_computation.1 | async-start | bytes 294912 | tf_op jit(solution)/shard_map/all_to_all | solution.py:541
  21.6 2.7 %middle.1 = (f32[2,768,128]{2,1,0:T(8,128)S(1)}, bf16[128,1024]{1,0:T(8,128)(2,1)S(1)}, bf16[768,128]{1,0:T(8,128)(2,1)S(1)}, f32[2,48,128]{2,1,0:T(8,128)S(1)}) custom-call(s32[1]{0:T(128)} %bitcast.band_ref, s32[1,48]{1,0:T(1,128)} %send_hbm.3, s32[4,8]{1,0:T(4,128)} %bitcast.23, s32[1,96]{1,0:T(1,128)} %bitcast.24, f32[1,96]{1,0:T(1,128)} %bitcast.25, ...), custom_call_target="tpu_custom_call" | custom-call | tf_op jit(solution)/shard_map/middle/pallas_call | solution.py:496
  24.4 5.7 %all-to-all-done.1 = f32[32,1,1152]{2,1,0:T(1,128)S(1)} async-done(((f32[32,1,1152]{2,1,0:T(1,128)}), f32[32,1,1152]{2,1,0:T(1,128)S(1)}, u32[]{:S(2)}, u32[]{:S(2)}) %all-to-all-start.1) | async-done | bytes 147488 | tf_op jit(solution)/shard_map/all_to_all | solution.py:541
  30.0 1.5 %lower.1 = f32[1152,128]{1,0:T(8,128)} custom-call(s32[1]{0:T(128)} %bitcast.band_ref, f32[288,128]{1,0:T(8,128)S(1)} %bitcast.20, f32[2,768,128]{2,1,0:T(8,128)S(1)} %get-tuple-element.13.sum_ref, bf16[128,1024]{1,0:T(8,128)(2,1)S(1)} %get-tuple-element.14.column_ref, bf16[768,128]{1,0:T(8,128)(2,1)S(1)} %get-tuple-element.15.place_ref, ...), custom_call_target="tpu_custom_call" | custom-call | tf_op jit(solution)/shard_map/lower/pallas_call | solution.py:496
Async XLA Ops:
  19.0 11.0 %all-to-all-start.1 = ((f32[32,1,1152]{2,1,0:T(1,128)}), f32[32,1,1152]{2,1,0:T(1,128)S(1)}, u32[]{:S(2)}, u32[]{:S(2)}) async-start(f32[32,1,1152]{2,1,0:T(1,128)} %answer.1), calls=%async_computation.1 | async-start | bytes 294912 | tf_op jit(solution)/shard_map/all_to_all | solution.py:541

commit v6 on v5

--- a/solution.py
+++ b/solution.py
@@ -83,10 +83,7 @@
         [(send_hbm, send_ref), (quanta_hbm, quanta_ref), (slot_hbm, slot_ref)], table_sems
     )
     copies = fetch(
-        [
-            (state_hbm.at[pl.ds(b * chunk, chunk), :], state_ref.at[pl.ds(b * chunk, chunk), :])
-            for b in range(pair_blocks)
-        ],
+        [(state_hbm, state_ref)],
         sems,
     )
     lane = lane_index((SUB, LANES))
@@ -129,8 +126,9 @@
             )
     for l in range(lane_count):
         row_ref[l] = table_ref[0, 0, l]
+    for copy in copies:
+        copy.wait()
     for block in range(pair_blocks):
-        copies[block].wait()
         for a in range(aux):
             first, middle, last = (
                 state_ref[pl.ds(a + aux * (tiles * SUB * block + u), SUB, stride=aux * tiles), :]

time: 31.8 us -> 31.4 us (0.987)
  Pallas kernels: 7.5 us -> 7.08 us
    pallas_call x4, Pallas kernels: 7.5 us -> 7.08 us  [call(): pl.pallas_call(functools.partial(kernel, sizes), out_shape=[space(shape,...]
where the time goes in v6:
time: 31.4 us; the launch traced here: 31.1 us
  blocking collectives  15.8 us (50%)
  Pallas kernels  7.08 us (23%)
  waiting for transfers between devices  5.68 us (18%)
  starting transfers between devices  2.59 us (8%)
    all_to_all x1, blocking collectives, on_device(): arrived = trade(payload).reshape(-1, LANES)  15.8 us
    pallas_call x4, Pallas kernels, call(): pl.pallas_call(functools.partial(kernel, sizes), out_shape=[space(shape,...  7.08 us
    all_to_all x1, waiting for transfers between devices, on_device(): returned = trade(reply)  5.68 us
    all_to_all x1, starting transfers between devices, on_device(): returned = trade(reply)  2.59 us
  transfers between devices with their start and end apart: 1, of which 1 were waited for; matrix products, arithmetic and copies ran while one was open for 0% of the time, Pallas kernels for 9%

profile of v6, /device:TPU:0, one launch (start us, length us, event | category | flops | bytes accessed | tf_op | source)
XLA Modules:
  0.0 31.1 jit_solution(5859241303574172752)
XLA Ops:
  0.0 1.9 %pack.1 = (f32[3,800,128]{2,1,0:T(8,128)S(1)}, f32[32,1,1280]{2,1,0:T(1,128)S(1)}) custom-call(s32[1]{0:T(128)} %bitcast.band_ref, s32[1,48]{1,0:T(1,128)} %send_hbm.3, s32[4,8]{1,0:T(4,128)} %bitcast.22, s32[1,48]{1,0:T(1,128)} %slot_hbm.1, f32[1152,128]{1,0:T(8,128)} %bitcast.21), custom_call_target="tpu_custom_call" | custom-call | tf_op jit(solution)/shard_map/pack/pallas_call | solution.py:494
  1.9 15.8 %all_to_all.10 = f32[32,1,1280]{2,1,0:T(1,128)S(1)} all-to-all(f32[32,1,1280]{2,1,0:T(1,128)S(1)} %get-tuple-element.11), channel_id=1, replica_groups=mesh['tier'=4,'aux'=8] {'tier','aux'}, dimensions={0} | all-to-all | bytes 327680 | tf_op jit(solution)/shard_map/all_to_all | solution.py:531
  17.7 0.9 %answer.1 = f32[32,1,1152]{2,1,0:T(1,128)} custom-call(s32[1]{0:T(128)} %bitcast.band_ref, f32[320,128]{1,0:T(8,128)S(1)} %bitcast.18, f32[3,800,128]{2,1,0:T(8,128)S(1)} %get-tuple-element.12.store_ref), custom_call_target="tpu_custom_call" | custom-call | tf_op jit(solution)/shard_map/answer/pallas_call | solution.py:494
  18.6 2.6 %all-to-all-start.1 = ((f32[32,1,1152]{2,1,0:T(1,128)}), f32[32,1,1152]{2,1,0:T(1,128)S(1)}, u32[]{:S(2)}, u32[]{:S(2)}) async-start(f32[32,1,1152]{2,1,0:T(1,128)} %answer.1), calls=%async_computation.1 | async-start | bytes 294912 | tf_op jit(solution)/shard_map/all_to_all | solution.py:539
  21.2 2.7 %middle.1 = (f32[2,768,128]{2,1,0:T(8,128)S(1)}, bf16[128,1024]{1,0:T(8,128)(2,1)S(1)}, bf16[768,128]{1,0:T(8,128)(2,1)S(1)}, f32[2,48,128]{2,1,0:T(8,128)S(1)}) custom-call(s32[1]{0:T(128)} %bitcast.band_ref, s32[1,48]{1,0:T(1,128)} %send_hbm.3, s32[4,8]{1,0:T(4,128)} %bitcast.23, s32[1,96]{1,0:T(1,128)} %bitcast.24, f32[1,96]{1,0:T(1,128)} %bitcast.25, ...), custom_call_target="tpu_custom_call" | custom-call | tf_op jit(solution)/shard_map/middle/pallas_call | solution.py:494
  24.0 5.7 %all-to-all-done.1 = f32[32,1,1152]{2,1,0:T(1,128)S(1)} async-done(((f32[32,1,1152]{2,1,0:T(1,128)}), f32[32,1,1152]{2,1,0:T(1,128)S(1)}, u32[]{:S(2)}, u32[]{:S(2)}) %all-to-all-start.1) | async-done | bytes 147488 | tf_op jit(solution)/shard_map/all_to_all | solution.py:539
  29.6 1.5 %lower.1 = f32[1152,128]{1,0:T(8,128)} custom-call(s32[1]{0:T(128)} %bitcast.band_ref, f32[288,128]{1,0:T(8,128)S(1)} %bitcast.20, f32[2,768,128]{2,1,0:T(8,128)S(1)} %get-tuple-element.13.sum_ref, bf16[128,1024]{1,0:T(8,128)(2,1)S(1)} %get-tuple-element.14.column_ref, bf16[768,128]{1,0:T(8,128)(2,1)S(1)} %get-tuple-element.15.place_ref, ...), custom_call_target="tpu_custom_call" | custom-call | tf_op jit(solution)/shard_map/lower/pallas_call | solution.py:494
Async XLA Ops:
  18.6 11.0 %all-to-all-start.1 = ((f32[32,1,1152]{2,1,0:T(1,128)}), f32[32,1,1152]{2,1,0:T(1,128)S(1)}, u32[]{:S(2)}, u32[]{:S(2)}) async-start(f32[32,1,1152]{2,1,0:T(1,128)} %answer.1), calls=%async_computation.1 | async-start | bytes 294912 | tf_op jit(solution)/shard_map/all_to_all | solution.py:539

commit v7 on v6

--- a/solution.py
+++ b/solution.py
@@ -47,13 +47,10 @@
 
 
 def unmerge(parts, lane, sites):
-    rest = 2 * sites - LANES
     first, second, third = parts
-    kept = LANES - rest
-    col_imag = jnp.where(
-        lane < kept, pltpu.roll(second, kept, 1), pltpu.roll(third, 2 * LANES - sites - rest, 1)
-    )
-    return first, imaginary(first, second, lane, sites), third, col_imag
+    kept = 2 * (LANES - sites)
+    col_imag = jnp.where(lane < kept, pltpu.roll(second, kept, 1), pltpu.roll(third, kept, 1))
+    return first, imaginary(first, second, lane, sites), pltpu.roll(third, sites, 1), col_imag
 
 
 def pack_kernel(
@@ -138,19 +135,22 @@
             last_turned = pltpu.roll(last, rest, 1)
             base = a * sites + 2 * SUB * block
             store_ref[0, pl.ds(base, SUB, stride=2), :] = first
-            store_ref[1, pl.ds(base, SUB, stride=2), :] = middle
+            store_ref[1, pl.ds(base, SUB, stride=2), :] = jnp.where(lane < rest, middle, first)
             store_ref[0, pl.ds(base + 1, SUB, stride=2), :] = jnp.where(
                 lane < rest, middle_turned, last_turned
             )
             store_ref[1, pl.ds(base + 1, SUB, stride=2), :] = last_turned
+    kept = LANES - rest
+    tail = sites - kept
+    wide = lane_index((sites, LANES))
     for a in range(aux):
         here = pl.ds(a * sites, sites)
-        first = store_ref[0, here, :].T
-        second = store_ref[1, here, :].T
-        col_imag = jnp.concatenate([first[sites:, :], second[:rest, :]], axis=0)
-        store_ref[2, here, pl.ds(0, sites)] = first[:sites, :]
-        store_ref[1, here, pl.ds(rest, LANES - rest)] = col_imag[:, : LANES - rest]
-        store_ref[2, here, pl.ds(sites, LANES - sites)] = col_imag[:, LANES - rest :]
+        first, second = store_ref[0, here, :], store_ref[1, here, :]
+        columns = jnp.concatenate([first[kept:, :], first], axis=0).T[:sites, :]
+        turned = jnp.concatenate([second[kept:, :], second[kept:, :], second[:kept, :]], axis=0).T
+        turned = jnp.concatenate([turned[LANES - tail :, :], turned[:rest, :]], axis=0)
+        store_ref[1, here, :] = jnp.where(wide < rest, second, turned)
+        store_ref[2, here, :] = jnp.where(wide < tail, turned, columns)
     for g in (1, 0):
         for q in range(peers):
             at_row = jnp.maximum(band - g, 0) * peers + q
@@ -276,9 +276,8 @@
     real, imag = pl.ds(0, sites), pl.ds(LANES, sites)
     matrix_ref[0, real, imag] = hamilton
     matrix_ref[0, pl.ds(sites, sites), real] = -hamilton
-    matrix_ref[1, pl.ds(LANES, sites), imag] = -hamilton
-    matrix_ref[1, pl.ds(rest, LANES - rest), real] = hamilton[: LANES - rest, :]
-    matrix_ref[1, pl.ds(LANES + sites, LANES - sites), real] = hamilton[LANES - rest :, :]
+    matrix_ref[1, pl.ds(rest, sites), real] = hamilton
+    matrix_ref[1, pl.ds(2 * LANES - sites, sites), imag] = -hamilton
     dot = functools.partial(jnp.dot, preferred_element_type=f32)
     splits = [split(matrix_ref[half]) for half in range(2)]
     lane = lane_index((sites, LANES))
@@ -414,17 +413,22 @@
                 edge_ref[f, pl.ds(half + base, peers, stride=capacity), :] = value - high
     dot = functools.partial(jnp.dot, preferred_element_type=jnp.float32)
     row_data = jnp.concatenate([edge_ref[0], edge_ref[1]], axis=1).astype(jnp.bfloat16)
-    col_data = jnp.concatenate([edge_ref[2].T, edge_ref[3].T], axis=0).astype(jnp.bfloat16)
+    col_data = jnp.concatenate(
+        [edge_ref[2].T[:sites, :], edge_ref[3].T[:sites, :]], axis=0
+    ).astype(jnp.bfloat16)
+    for a in range(aux):
+        here = pl.ds(a * sites, sites)
+        placed = dot(place_ref[here, :], row_data)
+        for c in range(2):
+            work_ref[c, here, :] = sum_ref[c, here, :] + placed[:, c * LANES : (c + 1) * LANES]
     for pair in range(aux // 2):
         columns = dot(col_data, column_ref[:, pl.ds(2 * pair * LANES, 2 * LANES)])
         for o in range(2):
             here = pl.ds((2 * pair + o) * sites, sites)
-            placed = dot(place_ref[here, :], row_data)
             for c in range(2):
                 work_ref[c, here, :] = (
-                    sum_ref[c, here, :]
-                    + placed[:, c * LANES : (c + 1) * LANES]
-                    + columns[c * LANES : c * LANES + sites, o * LANES : (o + 1) * LANES]
+                    work_ref[c, here, :]
+                    + columns[c * sites : (c + 1) * sites, o * LANES : (o + 1) * LANES]
                 )
     lane = lane_index((SUB, LANES))
     copies = []

time: 31.4 us -> 31.1 us (level)
  no operation moved by 1% of the time
where the time goes in v7:
time: 31.1 us; the launch traced here: 30.9 us
  blocking collectives  15.8 us (51%)
  Pallas kernels  6.93 us (22%)
  waiting for transfers between devices  5.57 us (18%)
  starting transfers between devices  2.59 us (8%)
    all_to_all x1, blocking collectives, on_device(): arrived = trade(payload).reshape(-1, LANES)  15.8 us
    pallas_call x4, Pallas kernels, call(): pl.pallas_call(functools.partial(kernel, sizes), out_shape=[space(shape,...  6.93 us
    all_to_all x1, waiting for transfers between devices, on_device(): returned = trade(reply)  5.57 us
    all_to_all x1, starting transfers between devices, on_device(): returned = trade(reply)  2.59 us
  transfers between devices with their start and end apart: 1, of which 1 were waited for; matrix products, arithmetic and copies ran while one was open for 0% of the time, Pallas kernels for 9%

profile of v7, /device:TPU:0, one launch (start us, length us, event | category | flops | bytes accessed | tf_op | source)
XLA Modules:
  0.0 30.9 jit_solution(13444464891811059725)
XLA Ops:
  0.0 1.8 %pack.1 = (f32[3,800,128]{2,1,0:T(8,128)S(1)}, f32[32,1,1280]{2,1,0:T(1,128)S(1)}) custom-call(s32[1]{0:T(128)} %bitcast.band_ref, s32[1,48]{1,0:T(1,128)} %send_hbm.3, s32[4,8]{1,0:T(4,128)} %bitcast.22, s32[1,48]{1,0:T(1,128)} %slot_hbm.1, f32[1152,128]{1,0:T(8,128)} %bitcast.21), custom_call_target="tpu_custom_call" | custom-call | tf_op jit(solution)/shard_map/pack/pallas_call | solution.py:498
  1.8 15.8 %all_to_all.10 = f32[32,1,1280]{2,1,0:T(1,128)S(1)} all-to-all(f32[32,1,1280]{2,1,0:T(1,128)S(1)} %get-tuple-element.11), channel_id=1, replica_groups=mesh['tier'=4,'aux'=8] {'tier','aux'}, dimensions={0} | all-to-all | bytes 327680 | tf_op jit(solution)/shard_map/all_to_all | solution.py:535
  17.5 0.9 %answer.1 = f32[32,1,1152]{2,1,0:T(1,128)} custom-call(s32[1]{0:T(128)} %bitcast.band_ref, f32[320,128]{1,0:T(8,128)S(1)} %bitcast.18, f32[3,800,128]{2,1,0:T(8,128)S(1)} %get-tuple-element.12.store_ref), custom_call_target="tpu_custom_call" | custom-call | tf_op jit(solution)/shard_map/answer/pallas_call | solution.py:498
  18.5 2.6 %all-to-all-start.1 = ((f32[32,1,1152]{2,1,0:T(1,128)}), f32[32,1,1152]{2,1,0:T(1,128)S(1)}, u32[]{:S(2)}, u32[]{:S(2)}) async-start(f32[32,1,1152]{2,1,0:T(1,128)} %answer.1), calls=%async_computation.1 | async-start | bytes 294912 | tf_op jit(solution)/shard_map/all_to_all | solution.py:543
  21.1 2.8 %middle.1 = (f32[2,768,128]{2,1,0:T(8,128)S(1)}, bf16[128,1024]{1,0:T(8,128)(2,1)S(1)}, bf16[768,128]{1,0:T(8,128)(2,1)S(1)}, f32[2,48,128]{2,1,0:T(8,128)S(1)}) custom-call(s32[1]{0:T(128)} %bitcast.band_ref, s32[1,48]{1,0:T(1,128)} %send_hbm.3, s32[4,8]{1,0:T(4,128)} %bitcast.23, s32[1,96]{1,0:T(1,128)} %bitcast.24, f32[1,96]{1,0:T(1,128)} %bitcast.25, ...), custom_call_target="tpu_custom_call" | custom-call | tf_op jit(solution)/shard_map/middle/pallas_call | solution.py:498
  23.9 5.6 %all-to-all-done.1 = f32[32,1,1152]{2,1,0:T(1,128)S(1)} async-done(((f32[32,1,1152]{2,1,0:T(1,128)}), f32[32,1,1152]{2,1,0:T(1,128)S(1)}, u32[]{:S(2)}, u32[]{:S(2)}) %all-to-all-start.1) | async-done | bytes 147488 | tf_op jit(solution)/shard_map/all_to_all | solution.py:543
  29.5 1.4 %lower.1 = f32[1152,128]{1,0:T(8,128)} custom-call(s32[1]{0:T(128)} %bitcast.band_ref, f32[288,128]{1,0:T(8,128)S(1)} %bitcast.20, f32[2,768,128]{2,1,0:T(8,128)S(1)} %get-tuple-element.13.sum_ref, bf16[128,1024]{1,0:T(8,128)(2,1)S(1)} %get-tuple-element.14.column_ref, bf16[768,128]{1,0:T(8,128)(2,1)S(1)} %get-tuple-element.15.place_ref, ...), custom_call_target="tpu_custom_call" | custom-call | tf_op jit(solution)/shard_map/lower/pallas_call | solution.py:498
Async XLA Ops:
  18.5 11.0 %all-to-all-start.1 = ((f32[32,1,1152]{2,1,0:T(1,128)}), f32[32,1,1152]{2,1,0:T(1,128)S(1)}, u32[]{:S(2)}, u32[]{:S(2)}) async-start(f32[32,1,1152]{2,1,0:T(1,128)} %answer.1), calls=%async_computation.1 | async-start | bytes 294912 | tf_op jit(solution)/shard_map/all_to_all | solution.py:543

commit v8 on v7

--- a/solution.py
+++ b/solution.py
@@ -198,6 +198,15 @@
     return high, low
 
 
+def column_tiles(sites):
+    spots = []
+    for field in range(4):
+        start = field * sites
+        first, last = start // LANES, (start + sites - 1) // LANES
+        spots += [(start, tile) for tile in range(first, last + 1)]
+    return spots
+
+
 def spread(row):
     return jnp.broadcast_to(row, (row.shape[1], row.shape[1])).T
 
@@ -218,6 +227,7 @@
     column_ref,
     place_ref,
     coef_ref,
+    mask_ref,
     work_ref,
     matrix_ref,
     edge_ref,
@@ -325,28 +335,35 @@
     rate = jnp.sum(jnp.where(at_site, rate_of, 0.0), axis=0, keepdims=True)
     strength = jnp.sum(jnp.where(at_site, strength_of, 0.0), axis=0, keepdims=True)
     lanes = pl.ds(0, lane_count)
-    index_ref[2, :, lanes] = -weight * (strength * rate)
-    index_ref[3, :, lanes] = weight * (2.0 * thermal * strength)
+    index_ref[3, :, lanes] = -weight * (strength * rate)
+    index_ref[4, :, lanes] = weight * (2.0 * thermal * strength)
     for c in range(2):
-        coef_ref[c] = spread(index_ref[2 + c, :, pl.ds(0, LANES)])[:lane_count, :]
-    row_index = jnp.where(usable, source * sites + site, -1).astype(f32)
-    column_index = jnp.where(usable, source * LANES + site, -1).astype(f32)
+        coef_ref[c] = spread(index_ref[3 + c, :, pl.ds(0, LANES)])[:lane_count, :]
+    rows_of = (
+        jnp.where(usable, source * sites + site, -1),
+        jnp.where(usable, site, -2 * LANES),
+        jnp.where(usable, source, -1),
+    )
     for start in (0, half):
-        index_ref[0, :, pl.ds(start, lane_count)] = row_index
-        index_ref[1, :, pl.ds(start, lane_count)] = column_index
+        for c in range(3):
+            index_ref[c, :, pl.ds(start, lane_count)] = rows_of[c].astype(f32)
+    tiles = 4 * sites // LANES
+    pairs = sites // 2
     for slab in range(2 * half // LANES):
         part = pl.ds(slab * LANES, LANES)
         turned = spread(index_ref[1, :, part])
-        row_index = index_ref[0, :, part]
-        for a in range(aux):
-            at = (lane_index((LANES, LANES)) + a * LANES).astype(f32)
-            column_ref[part, pl.ds(a * LANES, LANES)] = jnp.where(turned == at, 1.0, 0.0).astype(
-                jnp.bfloat16
-            )
-            at = (lax.broadcasted_iota(jnp.int32, (sites, LANES), 0) + a * sites).astype(f32)
-            place_ref[pl.ds(a * sites, sites), part] = jnp.where(row_index == at, 1.0, 0.0).astype(
-                jnp.bfloat16
-            )
+        here = lane_index((LANES, LANES))
+        for n, (offset, tile) in enumerate(column_tiles(sites)):
+            hot = turned == (here + (tile * LANES - offset)).astype(f32)
+            column_ref[part, pl.ds(n * LANES, LANES)] = jnp.where(hot, 1.0, 0.0).astype(jnp.bfloat16)
+        at_aux = lax.broadcasted_iota(jnp.int32, (aux, LANES), 0).astype(f32)
+        mask_ref[:, part] = jnp.where(index_ref[2, :, part] == at_aux, 1.0, 0.0)
+        for o in range(2):
+            shape = (pairs, aux, LANES)
+            at = 2 * lax.broadcasted_iota(jnp.int32, shape, 0) + o
+            at = at + sites * lax.broadcasted_iota(jnp.int32, shape, 1)
+            hot = index_ref[0, :, part] == at.reshape(pairs * aux, LANES).astype(f32)
+            place_ref[o, :, part] = jnp.where(hot, 1.0, 0.0).astype(jnp.bfloat16)
 
     for g in range(2):
         for p in range(peers):
@@ -359,7 +376,25 @@
         here = pl.ds(a * sites, sites)
         for c in range(2):
             turned = work_ref[2 + c, pl.ds(a * sites, LANES), :].T[:sites, :]
-            sum_ref[c, here, :] = work_ref[c, here, :] + turned
+            work_ref[c, here, :] = work_ref[c, here, :] + turned
+    pair_blocks = sites // (2 * SUB)
+    lane = lane_index((SUB, LANES))
+    for block in range(pair_blocks):
+        for a in range(aux):
+            base = a * sites + 2 * SUB * block
+            even_real, even_imag, odd_real, odd_imag = (
+                work_ref[c, pl.ds(base + o, SUB, stride=2), :] for o in (0, 1) for c in (0, 1)
+            )
+            turned_imag = pltpu.roll(even_imag, 96, 1)
+            turned_real = pltpu.roll(odd_real, 64, 1)
+            parts = (
+                jnp.where(lane < 96, even_real, turned_imag),
+                jnp.where(lane < 64, turned_imag, turned_real),
+                jnp.where(lane < 32, turned_real, pltpu.roll(odd_imag, 32, 1)),
+            )
+            for u in range(tiles):
+                start = a + aux * (tiles * SUB * block + u)
+                sum_ref[pl.ds(start, SUB, stride=aux * tiles), :] = parts[u]
 
 
 def lower_kernel(
@@ -370,25 +405,28 @@
     column_ref,
     place_ref,
     coef_ref,
+    mask_ref,
     out_hbm,
-    work_ref,
     edge_ref,
+    turned_ref,
+    left_ref,
     out_ref,
     sems,
 ):
     sites, aux, depth, peers, capacity, tiers = sizes
     tiles = 4 * sites // LANES
-    pair_blocks = sites // (2 * SUB)
-    chunk = aux * tiles * SUB
+    pairs = sites // 2
     slabs = capacity * FIELDS
     used = 2 * capacity * peers
     half = edge_ref.shape[1] // 2
+    rest = 2 * sites - LANES
+    bf16 = jnp.bfloat16
     band = band_ref[0]
     lane = lane_index((peers, LANES))
     if used < half:
         for top in (used, half + used):
             edge_ref[:, pl.ds(top, half - used), :] = jnp.zeros(
-                (4, half - used, LANES), jnp.float32
+                (6, half - used, LANES), jnp.float32
             )
     for g in range(2):
         target = jnp.maximum(band - g, 0)
@@ -401,55 +439,56 @@
             base = g * peers * capacity + j
             shared = coef_ref[0, pl.ds(base, peers, stride=capacity), :]
             turn = coef_ref[1, pl.ds(base, peers, stride=capacity), :]
+            real = shared * row_real + turn * row_imag
+            imag = pltpu.roll(shared * row_imag - turn * row_real, sites, 1)
+            head = jnp.where(lane < sites, real, imag)
+            head_turned = pltpu.roll(head, rest, 1)
             values = (
-                shared * row_real + turn * row_imag,
-                shared * row_imag - turn * row_real,
+                head,
+                jnp.where(lane < rest, imag, 0.0),
+                jnp.where(lane < rest, 0.0, head_turned),
+                jnp.where(lane < rest, head_turned, pltpu.roll(imag, rest, 1)),
                 shared * col_real - turn * col_imag,
                 shared * col_imag + turn * col_real,
             )
             for f, value in enumerate(values):
-                high = value.astype(jnp.bfloat16).astype(jnp.float32)
+                high = value.astype(bf16).astype(jnp.float32)
                 edge_ref[f, pl.ds(base, peers, stride=capacity), :] = high
                 edge_ref[f, pl.ds(half + base, peers, stride=capacity), :] = value - high
+    for c in range(2):
+        turned_ref[c] = edge_ref[4 + c].T
+    mask = mask_ref[...]
+    for c in range(2):
+        for o in range(2):
+            for q in range(0, pairs, 2):
+                both = [turned_ref[c, pl.ds(2 * (q + d) + o, 1), :] * mask for d in range(2)]
+                left_ref[2 * o + c, pl.ds(q * aux, 2 * aux), :] = jnp.concatenate(both, 0).astype(bf16)
     dot = functools.partial(jnp.dot, preferred_element_type=jnp.float32)
-    row_data = jnp.concatenate([edge_ref[0], edge_ref[1]], axis=1).astype(jnp.bfloat16)
-    col_data = jnp.concatenate(
-        [edge_ref[2].T[:sites, :], edge_ref[3].T[:sites, :]], axis=0
-    ).astype(jnp.bfloat16)
-    for a in range(aux):
-        here = pl.ds(a * sites, sites)
-        placed = dot(place_ref[here, :], row_data)
-        for c in range(2):
-            work_ref[c, here, :] = sum_ref[c, here, :] + placed[:, c * LANES : (c + 1) * LANES]
-    for pair in range(aux // 2):
-        columns = dot(col_data, column_ref[:, pl.ds(2 * pair * LANES, 2 * LANES)])
-        for o in range(2):
-            here = pl.ds((2 * pair + o) * sites, sites)
-            for c in range(2):
-                work_ref[c, here, :] = (
-                    work_ref[c, here, :]
-                    + columns[c * sites : (c + 1) * sites, o * LANES : (o + 1) * LANES]
-                )
-    lane = lane_index((SUB, LANES))
+    spots = column_tiles(sites)
+    hots = [column_ref[:, n * LANES : (n + 1) * LANES] for n in range(len(spots))]
+    rights = [edge_ref[f].astype(bf16) for f in range(4)]
+    row_spots = ((0, 0, 0), (0, 1, 1), (1, 1, 2), (1, 2, 3))
+    terms = [[] for _ in range(tiles)]
+    for n, (start, tile) in enumerate(spots):
+        terms[tile].append((start // sites, hots[n]))
+    for o, tile, f in row_spots:
+        terms[tile].append((4 + o, rights[f]))
+    parts = 3
+    size = pairs // parts
     copies = []
-    for block in range(pair_blocks):
-        for a in range(aux):
-            base = a * sites + 2 * SUB * block
-            even_real, even_imag, odd_real, odd_imag = (
-                work_ref[c, pl.ds(base + o, SUB, stride=2), :] for o in (0, 1) for c in (0, 1)
-            )
-            turned_imag = pltpu.roll(even_imag, 96, 1)
-            turned_real = pltpu.roll(odd_real, 64, 1)
-            parts = (
-                jnp.where(lane < 96, even_real, turned_imag),
-                jnp.where(lane < 64, turned_imag, turned_real),
-                jnp.where(lane < 32, turned_real, pltpu.roll(odd_imag, 32, 1)),
-            )
-            for u in range(tiles):
-                start = a + aux * (tiles * SUB * block + u)
-                out_ref[pl.ds(start, SUB, stride=aux * tiles), :] = parts[u]
-        here = pl.ds(block * chunk, chunk)
-        copies.append(pltpu.make_async_copy(out_ref.at[here, :], out_hbm.at[here, :], sems.at[block]))
+    for part in range(parts):
+        here = pl.ds(part * size * aux, size * aux)
+        lefts = [left_ref[n, here, :] for n in range(4)]
+        lefts += [place_ref[o, here, :] for o in range(2)]
+        for tile in range(tiles):
+            left = jnp.concatenate([lefts[n] for n, _ in terms[tile]], axis=1)
+            right = jnp.concatenate([right for _, right in terms[tile]], axis=0)
+            placed = dot(left, right)
+            for q in range(size):
+                at = pl.ds(((part * size + q) * tiles + tile) * aux, aux)
+                out_ref[at, :] = sum_ref[at, :] + placed[q * aux : (q + 1) * aux, :]
+        here = pl.ds(part * size * tiles * aux, size * tiles * aux)
+        copies.append(pltpu.make_async_copy(out_ref.at[here, :], out_hbm.at[here, :], sems.at[part]))
         copies[-1].start()
     for copy in copies:
         copy.wait()
@@ -541,7 +580,7 @@
         [VMEM((2, peers) + reply_shape[1:], f32), row_scratch, dma((2,))],
     )
     returned = trade(reply)
-    total, columns, places, coefs = call(
+    total, columns, places, coefs, masks = call(
         middle_kernel,
         "middle",
         [
@@ -557,10 +596,11 @@
             (VMEM, store),
         ],
         [
-            (VMEM, (2, rows, LANES), f32),
-            (VMEM, (2 * half, aux * LANES), bf16),
-            (VMEM, (rows, 2 * half), bf16),
+            (VMEM, flat_shape, f32),
+            (VMEM, (2 * half, len(column_tiles(sites)) * LANES), bf16),
+            (VMEM, (2, rows // 2, 2 * half), bf16),
             (VMEM, (2, lane_count, LANES), f32),
+            (VMEM, (aux, 2 * half), f32),
         ],
         [
             VMEM((4, padded, LANES), f32),
@@ -574,7 +614,7 @@
             SMEM(turned_quanta.shape, i32),
             SMEM(bath_row.shape, i32),
             SMEM(rate_row.shape, f32),
-            VMEM((4, 1, 2 * half), f32),
+            VMEM((5, 1, 2 * half), f32),
             dma((9,)),
         ],
     )
@@ -588,11 +628,13 @@
             (VMEM, columns),
             (VMEM, places),
             (VMEM, coefs),
+            (VMEM, masks),
         ],
         [(HBM, flat_shape, f32)],
         [
-            VMEM((2, rows, LANES), f32),
-            VMEM((4, 2 * half, LANES), f32),
+            VMEM((6, 2 * half, LANES), f32),
+            VMEM((2, LANES, 2 * half), f32),
+            VMEM((4, rows // 2, 2 * half), bf16),
             VMEM(flat_shape, f32),
             dma((pair_blocks,)),
         ],

time: 31.1 us -> 31.1 us (level)
  transfers between devices with their start and end apart: 1 -> 1, of which waited for: 1 -> 1; matrix products, arithmetic and copies ran while one was open for 0% -> 0% of each run, Pallas kernels for 9% -> 10%
where the time goes in v8:
time: 31.1 us; the launch traced here: 30.8 us
  blocking collectives  15.8 us (51%)
  Pallas kernels  7 us (23%)
  waiting for transfers between devices  5.44 us (17%)
  starting transfers between devices  2.59 us (8%)
    all_to_all x1, blocking collectives, on_device(): arrived = trade(payload).reshape(-1, LANES)  15.8 us
    pallas_call x4, Pallas kernels, call(): pl.pallas_call(functools.partial(kernel, sizes), out_shape=[space(shape,...  7 us
    all_to_all x1, waiting for transfers between devices, on_device(): returned = trade(reply)  5.44 us
    all_to_all x1, starting transfers between devices, on_device(): returned = trade(reply)  2.59 us
  transfers between devices with their start and end apart: 1, of which 1 were waited for; matrix products, arithmetic and copies ran while one was open for 0% of the time, Pallas kernels for 10%

profile of v8, /device:TPU:0, one launch (start us, length us, event | category | flops | bytes accessed | tf_op | source)
XLA Modules:
  0.0 30.8 jit_solution(13080495168070939987)
XLA Ops:
  0.0 1.8 %pack.1 = (f32[3,800,128]{2,1,0:T(8,128)S(1)}, f32[32,1,1280]{2,1,0:T(1,128)S(1)}) custom-call(s32[1]{0:T(128)} %bitcast.band_ref, s32[1,48]{1,0:T(1,128)} %send_hbm.3, s32[4,8]{1,0:T(4,128)} %bitcast.22, s32[1,48]{1,0:T(1,128)} %slot_hbm.1, f32[1152,128]{1,0:T(8,128)} %bitcast.21), custom_call_target="tpu_custom_call" | custom-call | tf_op jit(solution)/shard_map/pack/pallas_call | solution.py:537
  1.8 15.8 %all_to_all.10 = f32[32,1,1280]{2,1,0:T(1,128)S(1)} all-to-all(f32[32,1,1280]{2,1,0:T(1,128)S(1)} %get-tuple-element.12), channel_id=1, replica_groups=mesh['tier'=4,'aux'=8] {'tier','aux'}, dimensions={0} | all-to-all | bytes 327680 | tf_op jit(solution)/shard_map/all_to_all | solution.py:574
  17.5 0.9 %answer.1 = f32[32,1,1152]{2,1,0:T(1,128)} custom-call(s32[1]{0:T(128)} %bitcast.band_ref, f32[320,128]{1,0:T(8,128)S(1)} %bitcast.18, f32[3,800,128]{2,1,0:T(8,128)S(1)} %get-tuple-element.13.store_ref), custom_call_target="tpu_custom_call" | custom-call | tf_op jit(solution)/shard_map/answer/pallas_call | solution.py:537
  18.5 2.6 %all-to-all-start.1 = ((f32[32,1,1152]{2,1,0:T(1,128)}), f32[32,1,1152]{2,1,0:T(1,128)S(1)}, u32[]{:S(2)}, u32[]{:S(2)}) async-start(f32[32,1,1152]{2,1,0:T(1,128)} %answer.1), calls=%async_computation.1 | async-start | bytes 294912 | tf_op jit(solution)/shard_map/all_to_all | solution.py:582
  21.1 3.0 %middle.1 = (f32[1152,128]{1,0:T(8,128)S(1)}, bf16[128,768]{1,0:T(8,128)(2,1)S(1)}, bf16[2,384,128]{2,1,0:T(8,128)(2,1)S(1)}, f32[2,48,128]{2,1,0:T(8,128)S(1)}, f32[8,128]{1,0:T(8,128)S(1)}) custom-call(s32[1]{0:T(128)} %bitcast.band_ref, s32[1,48]{1,0:T(1,128)} %send_hbm.3, s32[4,8]{1,0:T(4,128)} %bitcast.23, s32[1,96]{1,0:T(1,128)} %bitcast.24, ...), custom_call_target="tpu_custom_call" | custom-call | tf_op jit(solution)/shard_map/middle/pallas_call | solution.py:537
  24.0 5.4 %all-to-all-done.1 = f32[32,1,1152]{2,1,0:T(1,128)S(1)} async-done(((f32[32,1,1152]{2,1,0:T(1,128)}), f32[32,1,1152]{2,1,0:T(1,128)S(1)}, u32[]{:S(2)}, u32[]{:S(2)}) %all-to-all-start.1) | async-done | bytes 147488 | tf_op jit(solution)/shard_map/all_to_all | solution.py:582
  29.5 1.4 %lower.1 = f32[1152,128]{1,0:T(8,128)} custom-call(s32[1]{0:T(128)} %bitcast.band_ref, f32[288,128]{1,0:T(8,128)S(1)} %bitcast.20, f32[1152,128]{1,0:T(8,128)S(1)} %get-tuple-element.14.sum_ref, bf16[128,768]{1,0:T(8,128)(2,1)S(1)} %get-tuple-element.15.column_ref, bf16[2,384,128]{2,1,0:T(8,128)(2,1)S(1)} %get-tuple-element.16.place_ref, ...), custom_call_target="tpu_custom_call" | custom-call | tf_op jit(solution)/shard_map/lower/pallas_call | solution.py:537
Async XLA Ops:
  18.5 11.0 %all-to-all-start.1 = ((f32[32,1,1152]{2,1,0:T(1,128)}), f32[32,1,1152]{2,1,0:T(1,128)S(1)}, u32[]{:S(2)}, u32[]{:S(2)}) async-start(f32[32,1,1152]{2,1,0:T(1,128)} %answer.1), calls=%async_computation.1 | async-start | bytes 294912 | tf_op jit(solution)/shard_map/all_to_all | solution.py:582

commit v9 on v8

--- a/solution.py
+++ b/solution.py
@@ -167,10 +167,9 @@
     slabs = capacity * FIELDS + 1
     for g in range(2):
         origin = jnp.minimum(band + g, tiers - 1) * peers
-        for p in range(peers):
-            tags = arrived_ref[pl.ds((origin + p) * slabs + slabs - 1, 1), :]
-            total = (tags + pltpu.roll(tags, TAG, 1)).astype(jnp.int32)
-            row_ref[g * peers + p] = jnp.where(band + g < tiers, total, aux * sites)
+        tags = arrived_ref[pl.ds(origin * slabs + slabs - 1, peers, stride=slabs), :]
+        total = (tags + pltpu.roll(tags, TAG, 1)).astype(jnp.int32)
+        row_ref[pl.ds(g * peers, peers), :] = jnp.where(band + g < tiers, total, aux * sites)
 
 
 def answer_kernel(sizes, band_ref, arrived_ref, store_ref, reply_hbm, reply_ref, row_ref, wire_sems):
@@ -181,7 +180,7 @@
     for g in (1, 0):
         for p in range(peers):
             for j in range(capacity):
-                row = pl.ds(row_ref[g * peers + p, 0, j], 1)
+                row = pl.ds(row_ref[g * peers + p, j], 1)
                 for f in range(FIELDS):
                     reply_ref[g, p, :, pl.ds((j * FIELDS + f) * LANES, LANES)] = store_ref[f, row, :]
         if g == 0:
@@ -369,7 +368,7 @@
         for p in range(peers):
             for j in range(capacity):
                 l = (g * peers + p) * capacity + j
-                row = pl.ds(row_ref[g * peers + p, 0, j], 1)
+                row = pl.ds(row_ref[g * peers + p, j], 1)
                 for c in range(4):
                     work_ref[c, row, :] = work_ref[c, row, :] + edge_ref[c, pl.ds(l, 1), :]
     for a in range(aux):
@@ -551,7 +550,7 @@
     reply_shape = (tiers * peers, 1, slabs * LANES)
     payload_shape = (tiers * peers, 1, (slabs + 1) * LANES)
     flat_shape = (aux * chunks, LANES)
-    row_scratch = VMEM((2 * peers, 1, LANES), i32)
+    row_scratch = VMEM((2 * peers, LANES), i32)
     trade = functools.partial(
         lax.all_to_all, axis_name=("tier", "aux"), split_axis=0, concat_axis=0, tiled=True
     )

time: 31.1 us -> 31.1 us (level)
  no operation moved by 1% of the time
where the time goes in v9:
time: 31.1 us; the launch traced here: 30.8 us
  blocking collectives  15.8 us (51%)
  Pallas kernels  7.04 us (23%)
  waiting for transfers between devices  5.42 us (17%)
  starting transfers between devices  2.59 us (8%)
    all_to_all x1, blocking collectives, on_device(): arrived = trade(payload).reshape(-1, LANES)  15.8 us
    pallas_call x4, Pallas kernels, call(): pl.pallas_call(functools.partial(kernel, sizes), out_shape=[space(shape,...  7.04 us
    all_to_all x1, waiting for transfers between devices, on_device(): returned = trade(reply)  5.42 us
    all_to_all x1, starting transfers between devices, on_device(): returned = trade(reply)  2.59 us
  transfers between devices with their start and end apart: 1, of which 1 were waited for; matrix products, arithmetic and copies ran while one was open for 0% of the time, Pallas kernels for 10%

profile of v9, /device:TPU:0, one launch (start us, length us, event | category | flops | bytes accessed | tf_op | source)
XLA Modules:
  0.0 30.8 jit_solution(6202034468518784773)
XLA Ops:
  0.0 1.8 %pack.1 = (f32[3,800,128]{2,1,0:T(8,128)S(1)}, f32[32,1,1280]{2,1,0:T(1,128)S(1)}) custom-call(s32[1]{0:T(128)} %bitcast.band_ref, s32[1,48]{1,0:T(1,128)} %send_hbm.3, s32[4,8]{1,0:T(4,128)} %bitcast.22, s32[1,48]{1,0:T(1,128)} %slot_hbm.1, f32[1152,128]{1,0:T(8,128)} %bitcast.21), custom_call_target="tpu_custom_call" | custom-call | tf_op jit(solution)/shard_map/pack/pallas_call | solution.py:536
  1.8 15.8 %all_to_all.10 = f32[32,1,1280]{2,1,0:T(1,128)S(1)} all-to-all(f32[32,1,1280]{2,1,0:T(1,128)S(1)} %get-tuple-element.12), channel_id=1, replica_groups=mesh['tier'=4,'aux'=8] {'tier','aux'}, dimensions={0} | all-to-all | bytes 327680 | tf_op jit(solution)/shard_map/all_to_all | solution.py:573
  17.5 0.9 %answer.1 = f32[32,1,1152]{2,1,0:T(1,128)} custom-call(s32[1]{0:T(128)} %bitcast.band_ref, f32[320,128]{1,0:T(8,128)S(1)} %bitcast.18, f32[3,800,128]{2,1,0:T(8,128)S(1)} %get-tuple-element.13.store_ref), custom_call_target="tpu_custom_call" | custom-call | tf_op jit(solution)/shard_map/answer/pallas_call | solution.py:536
  18.5 2.6 %all-to-all-start.1 = ((f32[32,1,1152]{2,1,0:T(1,128)}), f32[32,1,1152]{2,1,0:T(1,128)S(1)}, u32[]{:S(2)}, u32[]{:S(2)}) async-start(f32[32,1,1152]{2,1,0:T(1,128)} %answer.1), calls=%async_computation.1 | async-start | bytes 294912 | tf_op jit(solution)/shard_map/all_to_all | solution.py:581
  21.1 3.0 %middle.1 = (f32[1152,128]{1,0:T(8,128)S(1)}, bf16[128,768]{1,0:T(8,128)(2,1)S(1)}, bf16[2,384,128]{2,1,0:T(8,128)(2,1)S(1)}, f32[2,48,128]{2,1,0:T(8,128)S(1)}, f32[8,128]{1,0:T(8,128)S(1)}) custom-call(s32[1]{0:T(128)} %bitcast.band_ref, s32[1,48]{1,0:T(1,128)} %send_hbm.3, s32[4,8]{1,0:T(4,128)} %bitcast.23, s32[1,96]{1,0:T(1,128)} %bitcast.24, ...), custom_call_target="tpu_custom_call" | custom-call | tf_op jit(solution)/shard_map/middle/pallas_call | solution.py:536
  24.1 5.4 %all-to-all-done.1 = f32[32,1,1152]{2,1,0:T(1,128)S(1)} async-done(((f32[32,1,1152]{2,1,0:T(1,128)}), f32[32,1,1152]{2,1,0:T(1,128)S(1)}, u32[]{:S(2)}, u32[]{:S(2)}) %all-to-all-start.1) | async-done | bytes 147488 | tf_op jit(solution)/shard_map/all_to_all | solution.py:581
  29.5 1.4 %lower.1 = f32[1152,128]{1,0:T(8,128)} custom-call(s32[1]{0:T(128)} %bitcast.band_ref, f32[288,128]{1,0:T(8,128)S(1)} %bitcast.20, f32[1152,128]{1,0:T(8,128)S(1)} %get-tuple-element.14.sum_ref, bf16[128,768]{1,0:T(8,128)(2,1)S(1)} %get-tuple-element.15.column_ref, bf16[2,384,128]{2,1,0:T(8,128)(2,1)S(1)} %get-tuple-element.16.place_ref, ...), custom_call_target="tpu_custom_call" | custom-call | tf_op jit(solution)/shard_map/lower/pallas_call | solution.py:536
Async XLA Ops:
  18.5 11.0 %all-to-all-start.1 = ((f32[32,1,1152]{2,1,0:T(1,128)}), f32[32,1,1152]{2,1,0:T(1,128)S(1)}, u32[]{:S(2)}, u32[]{:S(2)}) async-start(f32[32,1,1152]{2,1,0:T(1,128)} %answer.1), calls=%async_computation.1 | async-start | bytes 294912 | tf_op jit(solution)/shard_map/all_to_all | solution.py:581

commit v10 on v8

--- a/solution.py
+++ b/solution.py
@@ -473,11 +473,11 @@
         terms[tile].append((start // sites, hots[n]))
     for o, tile, f in row_spots:
         terms[tile].append((4 + o, rights[f]))
-    parts = 3
-    size = pairs // parts
+    cuts = [2 * (pairs * n // 16) for n in (0, 4, 7, 8)]
     copies = []
-    for part in range(parts):
-        here = pl.ds(part * size * aux, size * aux)
+    for part, (low, high) in enumerate(zip(cuts, cuts[1:])):
+        size = high - low
+        here = pl.ds(low * aux, size * aux)
         lefts = [left_ref[n, here, :] for n in range(4)]
         lefts += [place_ref[o, here, :] for o in range(2)]
         for tile in range(tiles):
@@ -485,9 +485,9 @@
             right = jnp.concatenate([right for _, right in terms[tile]], axis=0)
             placed = dot(left, right)
             for q in range(size):
-                at = pl.ds(((part * size + q) * tiles + tile) * aux, aux)
+                at = pl.ds(((low + q) * tiles + tile) * aux, aux)
                 out_ref[at, :] = sum_ref[at, :] + placed[q * aux : (q + 1) * aux, :]
-        here = pl.ds(part * size * tiles * aux, size * tiles * aux)
+        here = pl.ds(low * tiles * aux, size * tiles * aux)
         copies.append(pltpu.make_async_copy(out_ref.at[here, :], out_hbm.at[here, :], sems.at[part]))
         copies[-1].start()
     for copy in copies:

time: 31.1 us -> 31.1 us (level)
  no operation moved by 1% of the time
where the time goes in v10:
time: 31.1 us; the launch traced here: 30.8 us
  blocking collectives  15.8 us (51%)
  Pallas kernels  7.03 us (23%)
  waiting for transfers between devices  5.42 us (17%)
  starting transfers between devices  2.59 us (8%)
    all_to_all x1, blocking collectives, on_device(): arrived = trade(payload).reshape(-1, LANES)  15.8 us
    pallas_call x4, Pallas kernels, call(): pl.pallas_call(functools.partial(kernel, sizes), out_shape=[space(shape,...  7.03 us
    all_to_all x1, waiting for transfers between devices, on_device(): returned = trade(reply)  5.42 us
    all_to_all x1, starting transfers between devices, on_device(): returned = trade(reply)  2.59 us
  transfers between devices with their start and end apart: 1, of which 1 were waited for; matrix products, arithmetic and copies ran while one was open for 0% of the time, Pallas kernels for 10%

profile of v10, /device:TPU:0, one launch (start us, length us, event | category | flops | bytes accessed | tf_op | source)
XLA Modules:
  0.0 30.8 jit_solution(14527594123644095123)
XLA Ops:
  0.0 1.8 %pack.1 = (f32[3,800,128]{2,1,0:T(8,128)S(1)}, f32[32,1,1280]{2,1,0:T(1,128)S(1)}) custom-call(s32[1]{0:T(128)} %bitcast.band_ref, s32[1,48]{1,0:T(1,128)} %send_hbm.3, s32[4,8]{1,0:T(4,128)} %bitcast.22, s32[1,48]{1,0:T(1,128)} %slot_hbm.1, f32[1152,128]{1,0:T(8,128)} %bitcast.21), custom_call_target="tpu_custom_call" | custom-call | tf_op jit(solution)/shard_map/pack/pallas_call | solution.py:537
  1.8 15.8 %all_to_all.10 = f32[32,1,1280]{2,1,0:T(1,128)S(1)} all-to-all(f32[32,1,1280]{2,1,0:T(1,128)S(1)} %get-tuple-element.12), channel_id=1, replica_groups=mesh['tier'=4,'aux'=8] {'tier','aux'}, dimensions={0} | all-to-all | bytes 327680 | tf_op jit(solution)/shard_map/all_to_all | solution.py:574
  17.5 0.9 %answer.1 = f32[32,1,1152]{2,1,0:T(1,128)} custom-call(s32[1]{0:T(128)} %bitcast.band_ref, f32[320,128]{1,0:T(8,128)S(1)} %bitcast.18, f32[3,800,128]{2,1,0:T(8,128)S(1)} %get-tuple-element.13.store_ref), custom_call_target="tpu_custom_call" | custom-call | tf_op jit(solution)/shard_map/answer/pallas_call | solution.py:537
  18.5 2.6 %all-to-all-start.1 = ((f32[32,1,1152]{2,1,0:T(1,128)}), f32[32,1,1152]{2,1,0:T(1,128)S(1)}, u32[]{:S(2)}, u32[]{:S(2)}) async-start(f32[32,1,1152]{2,1,0:T(1,128)} %answer.1), calls=%async_computation.1 | async-start | bytes 294912 | tf_op jit(solution)/shard_map/all_to_all | solution.py:582
  21.1 3.0 %middle.1 = (f32[1152,128]{1,0:T(8,128)S(1)}, bf16[128,768]{1,0:T(8,128)(2,1)S(1)}, bf16[2,384,128]{2,1,0:T(8,128)(2,1)S(1)}, f32[2,48,128]{2,1,0:T(8,128)S(1)}, f32[8,128]{1,0:T(8,128)S(1)}) custom-call(s32[1]{0:T(128)} %bitcast.band_ref, s32[1,48]{1,0:T(1,128)} %send_hbm.3, s32[4,8]{1,0:T(4,128)} %bitcast.23, s32[1,96]{1,0:T(1,128)} %bitcast.24, ...), custom_call_target="tpu_custom_call" | custom-call | tf_op jit(solution)/shard_map/middle/pallas_call | solution.py:537
  24.1 5.4 %all-to-all-done.1 = f32[32,1,1152]{2,1,0:T(1,128)S(1)} async-done(((f32[32,1,1152]{2,1,0:T(1,128)}), f32[32,1,1152]{2,1,0:T(1,128)S(1)}, u32[]{:S(2)}, u32[]{:S(2)}) %all-to-all-start.1) | async-done | bytes 147488 | tf_op jit(solution)/shard_map/all_to_all | solution.py:582
  29.5 1.4 %lower.1 = f32[1152,128]{1,0:T(8,128)} custom-call(s32[1]{0:T(128)} %bitcast.band_ref, f32[288,128]{1,0:T(8,128)S(1)} %bitcast.20, f32[1152,128]{1,0:T(8,128)S(1)} %get-tuple-element.14.sum_ref, bf16[128,768]{1,0:T(8,128)(2,1)S(1)} %get-tuple-element.15.column_ref, bf16[2,384,128]{2,1,0:T(8,128)(2,1)S(1)} %get-tuple-element.16.place_ref, ...), custom_call_target="tpu_custom_call" | custom-call | tf_op jit(solution)/shard_map/lower/pallas_call | solution.py:537
Async XLA Ops:
  18.5 11.0 %all-to-all-start.1 = ((f32[32,1,1152]{2,1,0:T(1,128)}), f32[32,1,1152]{2,1,0:T(1,128)S(1)}, u32[]{:S(2)}, u32[]{:S(2)}) async-start(f32[32,1,1152]{2,1,0:T(1,128)} %answer.1), calls=%async_computation.1 | async-start | bytes 294912 | tf_op jit(solution)/shard_map/all_to_all | solution.py:582

commit v11 on v8

--- a/solution.py
+++ b/solution.py
@@ -131,14 +131,12 @@
                 state_ref[pl.ds(a + aux * (tiles * SUB * block + u), SUB, stride=aux * tiles), :]
                 for u in range(tiles)
             )
-            middle_turned = pltpu.roll(middle, rest, 1)
+            mixed_turned = pltpu.roll(jnp.where(lane < rest, last, middle), rest, 1)
             last_turned = pltpu.roll(last, rest, 1)
             base = a * sites + 2 * SUB * block
             store_ref[0, pl.ds(base, SUB, stride=2), :] = first
             store_ref[1, pl.ds(base, SUB, stride=2), :] = jnp.where(lane < rest, middle, first)
-            store_ref[0, pl.ds(base + 1, SUB, stride=2), :] = jnp.where(
-                lane < rest, middle_turned, last_turned
-            )
+            store_ref[0, pl.ds(base + 1, SUB, stride=2), :] = mixed_turned
             store_ref[1, pl.ds(base + 1, SUB, stride=2), :] = last_turned
     kept = LANES - rest
     tail = sites - kept

time: 31.1 us -> 31.1 us (level)
  no operation moved by 1% of the time
where the time goes in v11:
time: 31.1 us; the launch traced here: 30.8 us
  blocking collectives  15.8 us (51%)
  Pallas kernels  7.04 us (23%)
  waiting for transfers between devices  5.41 us (17%)
  starting transfers between devices  2.59 us (8%)
    all_to_all x1, blocking collectives, on_device(): arrived = trade(payload).reshape(-1, LANES)  15.8 us
    pallas_call x4, Pallas kernels, call(): pl.pallas_call(functools.partial(kernel, sizes), out_shape=[space(shape,...  7.04 us
    all_to_all x1, waiting for transfers between devices, on_device(): returned = trade(reply)  5.41 us
    all_to_all x1, starting transfers between devices, on_device(): returned = trade(reply)  2.59 us
  transfers between devices with their start and end apart: 1, of which 1 were waited for; matrix products, arithmetic and copies ran while one was open for 0% of the time, Pallas kernels for 10%

profile of v11, /device:TPU:0, one launch (start us, length us, event | category | flops | bytes accessed | tf_op | source)
XLA Modules:
  0.0 30.8 jit_solution(13253807495097282195)
XLA Ops:
  0.0 1.8 %pack.1 = (f32[3,800,128]{2,1,0:T(8,128)S(1)}, f32[32,1,1280]{2,1,0:T(1,128)S(1)}) custom-call(s32[1]{0:T(128)} %bitcast.band_ref, s32[1,48]{1,0:T(1,128)} %send_hbm.3, s32[4,8]{1,0:T(4,128)} %bitcast.22, s32[1,48]{1,0:T(1,128)} %slot_hbm.1, f32[1152,128]{1,0:T(8,128)} %bitcast.21), custom_call_target="tpu_custom_call" | custom-call | tf_op jit(solution)/shard_map/pack/pallas_call | solution.py:535
  1.8 15.8 %all_to_all.10 = f32[32,1,1280]{2,1,0:T(1,128)S(1)} all-to-all(f32[32,1,1280]{2,1,0:T(1,128)S(1)} %get-tuple-element.12), channel_id=1, replica_groups=mesh['tier'=4,'aux'=8] {'tier','aux'}, dimensions={0} | all-to-all | bytes 327680 | tf_op jit(solution)/shard_map/all_to_all | solution.py:572
  17.5 0.9 %answer.1 = f32[32,1,1152]{2,1,0:T(1,128)} custom-call(s32[1]{0:T(128)} %bitcast.band_ref, f32[320,128]{1,0:T(8,128)S(1)} %bitcast.18, f32[3,800,128]{2,1,0:T(8,128)S(1)} %get-tuple-element.13.store_ref), custom_call_target="tpu_custom_call" | custom-call | tf_op jit(solution)/shard_map/answer/pallas_call | solution.py:535
  18.5 2.6 %all-to-all-start.1 = ((f32[32,1,1152]{2,1,0:T(1,128)}), f32[32,1,1152]{2,1,0:T(1,128)S(1)}, u32[]{:S(2)}, u32[]{:S(2)}) async-start(f32[32,1,1152]{2,1,0:T(1,128)} %answer.1), calls=%async_computation.1 | async-start | bytes 294912 | tf_op jit(solution)/shard_map/all_to_all | solution.py:580
  21.1 3.0 %middle.1 = (f32[1152,128]{1,0:T(8,128)S(1)}, bf16[128,768]{1,0:T(8,128)(2,1)S(1)}, bf16[2,384,128]{2,1,0:T(8,128)(2,1)S(1)}, f32[2,48,128]{2,1,0:T(8,128)S(1)}, f32[8,128]{1,0:T(8,128)S(1)}) custom-call(s32[1]{0:T(128)} %bitcast.band_ref, s32[1,48]{1,0:T(1,128)} %send_hbm.3, s32[4,8]{1,0:T(4,128)} %bitcast.23, s32[1,96]{1,0:T(1,128)} %bitcast.24, ...), custom_call_target="tpu_custom_call" | custom-call | tf_op jit(solution)/shard_map/middle/pallas_call | solution.py:535
  24.1 5.4 %all-to-all-done.1 = f32[32,1,1152]{2,1,0:T(1,128)S(1)} async-done(((f32[32,1,1152]{2,1,0:T(1,128)}), f32[32,1,1152]{2,1,0:T(1,128)S(1)}, u32[]{:S(2)}, u32[]{:S(2)}) %all-to-all-start.1) | async-done | bytes 147488 | tf_op jit(solution)/shard_map/all_to_all | solution.py:580
  29.5 1.4 %lower.1 = f32[1152,128]{1,0:T(8,128)} custom-call(s32[1]{0:T(128)} %bitcast.band_ref, f32[288,128]{1,0:T(8,128)S(1)} %bitcast.20, f32[1152,128]{1,0:T(8,128)S(1)} %get-tuple-element.14.sum_ref, bf16[128,768]{1,0:T(8,128)(2,1)S(1)} %get-tuple-element.15.column_ref, bf16[2,384,128]{2,1,0:T(8,128)(2,1)S(1)} %get-tuple-element.16.place_ref, ...), custom_call_target="tpu_custom_call" | custom-call | tf_op jit(solution)/shard_map/lower/pallas_call | solution.py:535
Async XLA Ops:
  18.5 11.0 %all-to-all-start.1 = ((f32[32,1,1152]{2,1,0:T(1,128)}), f32[32,1,1152]{2,1,0:T(1,128)S(1)}, u32[]{:S(2)}, u32[]{:S(2)}) async-start(f32[32,1,1152]{2,1,0:T(1,128)} %answer.1), calls=%async_computation.1 | async-start | bytes 294912 | tf_op jit(solution)/shard_map/all_to_all | solution.py:580
